TPU v7x, 32 devices: a whole 2x2x4 slice. The times are simulated.
32 devices in a mesh: ctx: 16 (over z, y, core), head: 2 (over x).
Axes of the slice: x: 2, y: 2, z: 4, core: 2. Of those that a mesh axis runs over, the one named last changes fastest.
Arguments:
- queries: bfloat16 [4096, 2048], P(('ctx', 'head')), may hold values from -24 to 24
- keys: bfloat16 [4096, 256], P(('ctx', 'head')), may hold values from -24 to 24
- values: bfloat16 [4096, 256], P(('ctx', 'head')), may hold values from -6 to 6
- d_out: bfloat16 [4096, 2048], P(('ctx', 'head')), may hold values from -6 to 6
- doc_lengths: int32 [32], replicated, may hold values from 1 to 768, 4096 in all
Outputs:
- attn_out: bfloat16 [4096, 2048], P('ctx', 'head')
- grad_queries: bfloat16 [4096, 2048], P('ctx', 'head')
- grad_keys: bfloat16 [4096, 256], P('ctx', 'head')
- grad_values: bfloat16 [4096, 256], P('ctx', 'head')
Inputs may be any that keep to these rules, and one draw needn't show every extreme that they name: `doc_lengths`: the lengths sum to 4096; some document holds exactly 768 tokens.
All inputs are finite; a program needn't handle non-finite values.
Results may differ from a plain program's by a relative error of at most 0.02.
Values may be sent and summed in bfloat16 or wider, within the bound.
No kernel may reach another device: no remote copies, remote signals or barrier semaphores. Data moves between devices by JAX's collectives and lax.ppermute only.
A program may use at most 64 MiB of HBM per device.

v0:
```python
import jax
import jax.numpy as jnp
from jax import lax
from jax.sharding import PartitionSpec as P

WIN = 4


def passed_along(value, axis, steps):
    count = lax.axis_size(axis)
    first, last = (max(0, -steps), min(count, count - steps))
    return lax.ppermute(value, axis, [(source, source + steps) for source in range(first, last)])


def token_docs(starts, positions):
    return jnp.sum((starts[None, :] <= positions[:, None]).astype(jnp.int32), axis=1)


def body(queries, keys, values, d_out, doc_lengths):
    query_local, key_local, value_local, grad_local = (
        lax.all_to_all(queries, "head", split_axis=1, concat_axis=0, tiled=True),
        lax.all_to_all(keys, "head", split_axis=1, concat_axis=0, tiled=True),
        lax.all_to_all(values, "head", split_axis=1, concat_axis=0, tiled=True),
        lax.all_to_all(d_out, "head", split_axis=1, concat_axis=0, tiled=True),
    )
    tok_rows = query_local.shape[0]
    head_size = key_local.shape[1]
    scaling = head_size ** (-0.5)
    lead_rows = (WIN - 1) * tok_rows
    key_value = jnp.concatenate([key_local, value_local], axis=1)
    window = key_value
    stride = 1
    while stride < WIN:
        window = jnp.concatenate([passed_along(window, "ctx", stride), window], axis=0)
        stride = stride * 2
    first_row = lax.axis_index("ctx") * tok_rows
    starts = jnp.cumsum(doc_lengths) - doc_lengths
    query_pos = first_row + jnp.arange(tok_rows, dtype=jnp.int32)
    key_pos = first_row - lead_rows + jnp.arange(WIN * tok_rows, dtype=jnp.int32)
    same_doc = token_docs(starts, query_pos)[:, None] == token_docs(starts, key_pos)[None, :]
    allowed = same_doc & (key_pos[None, :] <= query_pos[:, None])
    heads_local = query_local.shape[1] // head_size
    heads_block = max(1, min(heads_local, 512 // tok_rows))
    while heads_local % heads_block:
        heads_block = heads_block - 1
    block_count = heads_local // heads_block
    query_blocks = (
        query_local.reshape(tok_rows, heads_local, head_size)
        .transpose(1, 0, 2)
        .reshape(block_count, heads_block, tok_rows, head_size)
    )
    grad_blocks = (
        grad_local.reshape(tok_rows, heads_local, head_size)
        .transpose(1, 0, 2)
        .reshape(block_count, heads_block, tok_rows, head_size)
    )
    offset = (WIN - WIN) * tok_rows
    key_window = window[offset:, :head_size]
    value_window = window[offset:, head_size:]

    def block_step(running, inputs_pair):
        query_block, grad_block = inputs_pair
        scores = (
            jnp.einsum("htd,kd->htk", query_block, key_window, preferred_element_type=jnp.float32)
            * scaling
        )
        scores = jnp.where(allowed[None], scores, -jnp.inf)
        maximum = jnp.max(scores, axis=2, keepdims=True)
        totals = jnp.sum(jnp.exp(scores - maximum), axis=2, keepdims=True)
        log_total = maximum + jnp.log(totals)
        weights = jnp.exp(scores - log_total)
        rounded = weights.astype(jnp.bfloat16)
        outputs = jnp.einsum(
            "htk,kd->htd", rounded, value_window, preferred_element_type=jnp.float32
        ).astype(jnp.bfloat16)
        deltas = jnp.sum(
            grad_block.astype(jnp.float32) * outputs.astype(jnp.float32), axis=2, keepdims=True
        )
        grad_weights = jnp.einsum(
            "htd,kd->htk", grad_block, value_window, preferred_element_type=jnp.float32
        )
        grad_scores = (weights * (grad_weights - deltas)).astype(jnp.bfloat16)
        grad_query = (
            jnp.einsum("htk,kd->htd", grad_scores, key_window, preferred_element_type=jnp.float32)
            * scaling
        ).astype(jnp.bfloat16)
        grad_key = (
            jnp.einsum("htk,htd->kd", grad_scores, query_block, preferred_element_type=jnp.float32)
            * scaling
        )
        grad_value = jnp.einsum(
            "htk,htd->kd", rounded, grad_block, preferred_element_type=jnp.float32
        )
        return (running + jnp.concatenate([grad_key, grad_value], axis=1), (outputs, grad_query))

    start_sum = jnp.zeros((WIN * tok_rows, 2 * head_size), jnp.float32)
    summed, (outputs, grad_query) = lax.scan(block_step, start_sum, (query_blocks, grad_blocks))
    partials = jnp.concatenate([jnp.zeros((offset, 2 * head_size), jnp.float32), summed], axis=0)
    outputs, grad_query, partials = (outputs, grad_query, partials)
    attn_out = (
        outputs.reshape(heads_local, tok_rows, head_size)
        .transpose(1, 0, 2)
        .reshape(tok_rows, heads_local * head_size)
    )
    grad_queries = (
        grad_query.reshape(heads_local, tok_rows, head_size)
        .transpose(1, 0, 2)
        .reshape(tok_rows, heads_local * head_size)
    )
    own_rows = partials
    stride = WIN // 2
    while stride >= 1:
        half_rows = stride * tok_rows
        own_rows = own_rows[half_rows:] + passed_along(own_rows[:half_rows], "ctx", -stride)
        stride = stride // 2
    grad_keys = own_rows[:, :head_size].astype(jnp.bfloat16)
    grad_values = own_rows[:, head_size:].astype(jnp.bfloat16)
    return (attn_out, grad_queries, grad_keys, grad_values)


def solution(mesh):
    in_specs = (
        P(("ctx", "head"), None),
        P(("ctx", "head"), None),
        P(("ctx", "head"), None),
        P(("ctx", "head"), None),
        P(),
    )
    out_specs = (P("ctx", "head"), P("ctx", "head"), P("ctx", "head"), P("ctx", "head"))
    return jax.shard_map(body, mesh=mesh, in_specs=in_specs, out_specs=out_specs, check_vma=False)
```

profile of v0, /device:TPU:1, one launch (start us, length us, event | category | flops | bytes accessed | tf_op | source)
XLA Modules:
  0.0 88.5 jit_solution(8610057316855036472)
XLA Ops:
  0.6 1.6 %copy.76 = bf16[128,256]{0,1:T(8,128)(2,1)} copy(bf16[128,256]{1,0:T(8,128)(2,1)} %param.8) | data formatting | bytes 131072 | tf_op args[1]
  2.3 3.3 %all-to-all-start.1 = ((bf16[128,2,128]{0,2,1:T(8,128)(2,1)}), bf16[128,2,128]{0,2,1:T(8,128)(2,1)S(1)}, u32[]{:S(2)}, u32[]{:S(2)}) async-start(bf16[128,2,128]{0,2,1:T(8,128)(2,1)} %bitcast.3), calls=%async_computation.1 | async-start | bytes 131072 | tf_op jit(solution)/shard_map/all_to_all | solution.py:22
  5.6 1.6 %copy.78 = bf16[128,256]{0,1:T(8,128)(2,1)} copy(bf16[128,256]{1,0:T(8,128)(2,1)} %param.9) | data formatting | bytes 131072 | tf_op args[2]
  7.2 2.0 %all-to-all-done.1 = bf16[128,2,128]{0,2,1:T(8,128)(2,1)S(1)} async-done(((bf16[128,2,128]{0,2,1:T(8,128)(2,1)}), bf16[128,2,128]{0,2,1:T(8,128)(2,1)S(1)}, u32[]{:S(2)}, u32[]{:S(2)}) %all-to-all-start.1) | async-done | bytes 65568 | tf_op jit(solution)/shard_map/all_to_all | solution.py:22
  9.1 3.3 %all-to-all-start.2 = ((bf16[128,2,128]{0,2,1:T(8,128)(2,1)}), bf16[128,2,128]{0,2,1:T(8,128)(2,1)S(1)}, u32[]{:S(2)}, u32[]{:S(2)}) async-start(bf16[128,2,128]{0,2,1:T(8,128)(2,1)} %bitcast.6), calls=%async_computation.2 | async-start | bytes 131072 | tf_op jit(solution)/shard_map/all_to_all | solution.py:23
  12.4 1.9 %copy.117 = bf16[16,2,8,1024]{3,2,0,1:T(8,128)(2,1)} copy(bf16[16,2,8,1024]{3,2,1,0:T(8,128)(2,1)} %bitcast.126) | data formatting | bytes 1048576 | tf_op jit(solution)/shard_map/all_to_all | solution.py:21
  14.4 1.0 %all-to-all-done.2 = bf16[128,2,128]{0,2,1:T(8,128)(2,1)S(1)} async-done(((bf16[128,2,128]{0,2,1:T(8,128)(2,1)}), bf16[128,2,128]{0,2,1:T(8,128)(2,1)S(1)}, u32[]{:S(2)}, u32[]{:S(2)}) %all-to-all-start.2) | async-done | bytes 65568 | tf_op jit(solution)/shard_map/all_to_all | solution.py:23
  15.4 3.5 %all-to-all-start = ((bf16[128,2,1024]{2,0,1:T(8,128)(2,1)}), bf16[128,2,1024]{2,0,1:T(8,128)(2,1)S(1)}, u32[]{:S(2)}, u32[]{:S(2)}) async-start(bf16[128,2,1024]{2,0,1:T(8,128)(2,1)} %bitcast.83), calls=%async_computation | async-start | bytes 1048576 | tf_op jit(solution)/shard_map/all_to_all | solution.py:21
  19.0 6.3 %collective-permute-start = (bf16[256,256]{1,0:T(8,128)(2,1)S(1)}, bf16[256,256]{1,0:T(8,128)(2,1)S(1)}, u32[]{:S(2)}, u32[]{:S(2)}) collective-permute-start(bf16[256,256]{1,0:T(8,128)(2,1)S(1)} %pad_maximum_fusion), channel_id=1, source_target_pairs={{0,2},{2,4},{4,6},{6,8},{8,10},{10,12},{12,14},{14,16},{16,18},{18... | collective-permute-start | bytes 393224 | tf_op jit(solution)/shard_map/ppermute | solution.py:12
  25.3 0.8 copy.116
  26.1 1.1 %collective-permute-done = bf16[256,256]{1,0:T(8,128)(2,1)S(1)} collective-permute-done((bf16[256,256]{1,0:T(8,128)(2,1)S(1)}, bf16[256,256]{1,0:T(8,128)(2,1)S(1)}, u32[]{:S(2)}, u32[]{:S(2)}) %collective-permute-start) | collective-permute-done | bytes 131104 | tf_op jit(solution)/shard_map/ppermute | solution.py:12
  27.2 0.7 maximum_maximum_fusion.1
  27.9 3.8 %collective-permute-start.1 = (bf16[512,256]{1,0:T(8,128)(2,1)}, bf16[512,256]{1,0:T(8,128)(2,1)}, u32[]{:S(2)}, u32[]{:S(2)}) collective-permute-start(bf16[512,256]{1,0:T(8,128)(2,1)} %maximum_maximum_fusion.1), channel_id=1, source_target_pairs={{0,4},{2,6},{4,8},{6,10},{8,12},{10,14},{12,16},{14,18},{16,20},{1... | collective-permute-start | bytes 786440 | tf_op jit(solution)/shard_map/ppermute | solution.py:12
  31.8 3.5 %all-to-all-start.3 = ((bf16[128,2,1024]{2,0,1:T(8,128)(2,1)}), bf16[128,2,1024]{2,0,1:T(8,128)(2,1)S(1)}, u32[]{:S(2)}, u32[]{:S(2)}) async-start(bf16[128,2,1024]{2,0,1:T(8,128)(2,1)} %bitcast.82), calls=%async_computation.3 | async-start | bytes 1048576 | tf_op jit(solution)/shard_map/all_to_all | solution.py:24
  35.9 6.4 %all-to-all-done.3 = bf16[128,2,1024]{2,0,1:T(8,128)(2,1)S(1)} async-done(((bf16[128,2,1024]{2,0,1:T(8,128)(2,1)}), bf16[128,2,1024]{2,0,1:T(8,128)(2,1)S(1)}, u32[]{:S(2)}, u32[]{:S(2)}) %all-to-all-start.3) | async-done | bytes 524320 | tf_op jit(solution)/shard_map/all_to_all | solution.py:24
  42.3 1.0 %maximum_maximum_fusion = bf16[1024,256]{1,0:T(8,128)(2,1)S(1)} fusion(bf16[256,128]{1,0:T(8,128)(2,1)S(1)} %bitcast.125, bf16[256,128]{1,0:T(8,128)(2,1)S(1)} %bitcast.122, bf16[256,256]{1,0:T(8,128)(2,1)S(1)} %collective-permute-done, bf16[512,256]{1,0:T(8,128)(2,1)} %collective-permute-done.1), kind=kLoop, calls=%fused_computation.32 | loop fusion | flops 2097152 | bytes 1048576 | tf_op jit(solution)/shard_map/concatenate | solution.py:34
  43.5 21.1 %while.15 = (s32[]{:T(128)}, f32[1024,256]{0,1:T(8,128)S(1)}, bf16[4,2,256,128]{3,2,1,0:T(8,128)(2,1)}, bf16[4,2,256,128]{3,2,1,0:T(8,128)(2,1)S(1)}, bf16[4,2,2...) while((s32[]{:T(128)}, f32[1024,256]{0,1:T(8,128)S(1)}, ...), condition=%wide.region_7.8_spmd.clone, body=%wide.region_3.7_spmd.clone.sunk | while | flops 814283776 | bytes 21135524 | solution.py:97
  44.0 0.6 fusion.32
  44.7 0.5 exponential_reduce_fusion.2
  45.2 0.6 multiply_reduce_fusion.2
  45.8 0.7 bitcast_dynamic-update-slice_fusion.2
  46.5 0.6 convolution_bitcast_fusion.3
  47.0 0.6 multiply_convert_fusion.2
  47.9 0.5 fusion.34
  49.3 0.6 fusion.32
  50.0 0.5 exponential_reduce_fusion.2
  50.5 0.6 multiply_reduce_fusion.2
  51.1 0.7 bitcast_dynamic-update-slice_fusion.2
  51.7 0.6 convolution_bitcast_fusion.3
  52.3 0.6 multiply_convert_fusion.2
  54.6 0.6 fusion.32
  55.2 0.5 exponential_reduce_fusion.2
  55.8 0.6 multiply_reduce_fusion.2
  56.3 0.7 bitcast_dynamic-update-slice_fusion.2
  57.0 0.6 convolution_bitcast_fusion.3
  57.6 0.6 multiply_convert_fusion.2
  59.9 0.6 fusion.32
  60.5 0.5 exponential_reduce_fusion.2
  61.0 0.6 multiply_reduce_fusion.2
  61.6 0.7 bitcast_dynamic-update-slice_fusion.2
  62.3 0.6 convolution_bitcast_fusion.3
  62.9 0.6 multiply_convert_fusion.2
  65.1 1.3 %collective-permute-start.2 = (f32[512,256]{1,0:T(8,128)S(1)}, f32[512,256]{1,0:T(8,128)S(1)}, u32[]{:S(2)}, u32[]{:S(2)}) collective-permute-start(f32[512,256]{1,0:T(8,128)S(1)} %slice.37), channel_id=1, source_target_pairs={{4,0},{6,2},{8,4},{10,6},{12,8},{14,10},{16,12},{18,14},{20,16},{2... | collective-permute-start | bytes 1572872 | tf_op jit(solution)/shard_map/ppermute | solution.py:12
  67.1 11.2 %collective-permute-done.2 = f32[512,256]{1,0:T(8,128)S(1)} collective-permute-done((f32[512,256]{1,0:T(8,128)S(1)}, f32[512,256]{1,0:T(8,128)S(1)}, u32[]{:S(2)}, u32[]{:S(2)}) %collective-permute-start.2) | collective-permute-done | bytes 524320 | tf_op jit(solution)/shard_map/ppermute | solution.py:12
  78.3 5.0 %collective-permute-start.3 = (f32[256,256]{1,0:T(8,128)S(1)}, f32[256,256]{1,0:T(8,128)S(1)}, u32[]{:S(2)}, u32[]{:S(2)}) collective-permute-start(f32[256,256]{1,0:T(8,128)S(1)} %slice.39), channel_id=1, source_target_pairs={{2,0},{4,2},{6,4},{8,6},{10,8},{12,10},{14,12},{16,14},{18,16},{20... | collective-permute-start | bytes 786440 | tf_op jit(solution)/shard_map/ppermute | solution.py:12
  83.3 1.2 %copy_bitcast_fusion.6 = (bf16[256,1024]{1,0:T(8,128)(2,1)}, bf16[256,1024]{1,0:T(8,128)(2,1)}) fusion(bf16[32,8,8,128]{3,2,1,0:T(8,128)(2,1)S(1)} %bitcast.118, bf16[32,8,8,128]{3,2,1,0:T(8,128)(2,1)S(1)} %bitcast.119), kind=kLoop, calls=%fused_computation.27 | loop fusion | bytes 2097152 | tf_op jit(solution)/shard_map/reshape | solution.py:108
  84.5 3.3 %collective-permute-done.3 = f32[256,256]{1,0:T(8,128)S(1)} collective-permute-done((f32[256,256]{1,0:T(8,128)S(1)}, f32[256,256]{1,0:T(8,128)S(1)}, u32[]{:S(2)}, u32[]{:S(2)}) %collective-permute-start.3) | collective-permute-done | bytes 262176 | tf_op jit(solution)/shard_map/ppermute | solution.py:12
  87.8 0.7 fusion.16
  (56 shorter events, 8.6 us)
Async XLA Ops:
  0.6 24.7 %copy-start = (bf16[128,2048]{1,0:T(8,128)(2,1)S(1)}, bf16[128,2048]{1,0:T(8,128)(2,1)}, u32[]{:S(2)}) copy-start(bf16[128,2048]{1,0:T(8,128)(2,1)} %param.10) | copy-start | bytes 1572868
  2.3 6.8 %all-to-all-start.1 = ((bf16[128,2,128]{0,2,1:T(8,128)(2,1)}), bf16[128,2,128]{0,2,1:T(8,128)(2,1)S(1)}, u32[]{:S(2)}, u32[]{:S(2)}) async-start(bf16[128,2,128]{0,2,1:T(8,128)(2,1)} %bitcast.3), calls=%async_computation.1 | async-start | bytes 131072 | tf_op jit(solution)/shard_map/all_to_all | solution.py:22
  9.1 6.3 %all-to-all-start.2 = ((bf16[128,2,128]{0,2,1:T(8,128)(2,1)}), bf16[128,2,128]{0,2,1:T(8,128)(2,1)S(1)}, u32[]{:S(2)}, u32[]{:S(2)}) async-start(bf16[128,2,128]{0,2,1:T(8,128)(2,1)} %bitcast.6), calls=%async_computation.2 | async-start | bytes 131072 | tf_op jit(solution)/shard_map/all_to_all | solution.py:23
  14.3 21.0 %copy-start.2 = (s32[32]{0:T(128)S(1)}, s32[32]{0:T(128)}, u32[]{:S(2)}) copy-start(s32[32]{0:T(128)} %param.11) | copy-start | bytes 388
  15.4 16.4 %all-to-all-start = ((bf16[128,2,1024]{2,0,1:T(8,128)(2,1)}), bf16[128,2,1024]{2,0,1:T(8,128)(2,1)S(1)}, u32[]{:S(2)}, u32[]{:S(2)}) async-start(bf16[128,2,1024]{2,0,1:T(8,128)(2,1)} %bitcast.83), calls=%async_computation | async-start | bytes 1048576 | tf_op jit(solution)/shard_map/all_to_all | solution.py:21
  19.0 8.2 %collective-permute-start = (bf16[256,256]{1,0:T(8,128)(2,1)S(1)}, bf16[256,256]{1,0:T(8,128)(2,1)S(1)}, u32[]{:S(2)}, u32[]{:S(2)}) collective-permute-start(bf16[256,256]{1,0:T(8,128)(2,1)S(1)} %pad_maximum_fusion), channel_id=1, source_target_pairs={{0,2},{2,4},{4,6},{6,8},{8,10},{10,12},{12,14},{14,16},{16,18},{18... | collective-permute-start | bytes 393224 | tf_op jit(solution)/shard_map/ppermute | solution.py:12
  27.9 14.4 %collective-permute-start.1 = (bf16[512,256]{1,0:T(8,128)(2,1)}, bf16[512,256]{1,0:T(8,128)(2,1)}, u32[]{:S(2)}, u32[]{:S(2)}) collective-permute-start(bf16[512,256]{1,0:T(8,128)(2,1)} %maximum_maximum_fusion.1), channel_id=1, source_target_pairs={{0,4},{2,6},{4,8},{6,10},{8,12},{10,14},{12,16},{14,18},{16,20},{1... | collective-permute-start | bytes 786440 | tf_op jit(solution)/shard_map/ppermute | solution.py:12
  31.8 10.5 %all-to-all-start.3 = ((bf16[128,2,1024]{2,0,1:T(8,128)(2,1)}), bf16[128,2,1024]{2,0,1:T(8,128)(2,1)S(1)}, u32[]{:S(2)}, u32[]{:S(2)}) async-start(bf16[128,2,1024]{2,0,1:T(8,128)(2,1)} %bitcast.82), calls=%async_computation.3 | async-start | bytes 1048576 | tf_op jit(solution)/shard_map/all_to_all | solution.py:24
  64.7 2.0 %copy-start.1 = (bf16[4,2,256,128]{3,2,1,0:T(8,128)(2,1)S(1)}, bf16[4,2,256,128]{3,2,1,0:T(8,128)(2,1)}, u32[]{:S(2)}) copy-start(bf16[4,2,256,128]{3,2,1,0:T(8,128)(2,1)} %get-tuple-element.53) | copy-start | bytes 1572868
  65.1 13.2 %collective-permute-start.2 = (f32[512,256]{1,0:T(8,128)S(1)}, f32[512,256]{1,0:T(8,128)S(1)}, u32[]{:S(2)}, u32[]{:S(2)}) collective-permute-start(f32[512,256]{1,0:T(8,128)S(1)} %slice.37), channel_id=1, source_target_pairs={{4,0},{6,2},{8,4},{10,6},{12,8},{14,10},{16,12},{18,14},{20,16},{2... | collective-permute-start | bytes 1572872 | tf_op jit(solution)/shard_map/ppermute | solution.py:12
  78.3 9.5 %collective-permute-start.3 = (f32[256,256]{1,0:T(8,128)S(1)}, f32[256,256]{1,0:T(8,128)S(1)}, u32[]{:S(2)}, u32[]{:S(2)}) collective-permute-start(f32[256,256]{1,0:T(8,128)S(1)} %slice.39), channel_id=1, source_target_pairs={{2,0},{4,2},{6,4},{8,6},{10,8},{12,10},{14,12},{16,14},{18,16},{20... | collective-permute-start | bytes 786440 | tf_op jit(solution)/shard_map/ppermute | solution.py:12
where the time goes:
time: 89.2 us; the launch traced here: 88.5 us
  starting transfers between devices  29.9 us (34%)
  waiting for transfers between devices  24.8 us (28%)
  local copies, waits for them, and re-layouts  13 us (15%)
  matrix products  12.7 us (14%)
  other arithmetic  6.85 us (8%)
    ppermute x4, starting transfers between devices, passed_along(): lax.ppermute(value, axis, [(source, source + steps) for source in range(f...  16.3 us
    ppermute x4, waiting for transfers between devices, passed_along(): lax.ppermute(value, axis, [(source, source + steps) for source in range(f...  15.6 us
    all_to_all x1, waiting for transfers between devices, body(): lax.all_to_all(d_out, 'head', split_axis=1, concat_axis=0, tiled=True)  6.37 us
    unnamed x11, local copies, waits for them, and re-layouts  3.55 us
    all_to_all x1, starting transfers between devices, body(): lax.all_to_all(d_out, 'head', split_axis=1, concat_axis=0, tiled=True)  3.49 us
    all_to_all x1, starting transfers between devices, body(): lax.all_to_all(queries, 'head', split_axis=1, concat_axis=0, tiled=True)  3.49 us
    all_to_all x1, starting transfers between devices, body(): lax.all_to_all(values, 'head', split_axis=1, concat_axis=0, tiled=True)  3.3 us
    all_to_all x1, starting transfers between devices, body(): lax.all_to_all(keys, 'head', split_axis=1, concat_axis=0, tiled=True)  3.3 us
  transfers between devices with their start and end apart: 8, of which 6 were waited for; matrix products, arithmetic and copies ran while one was open for 9% of the time, Pallas kernels for 0%

commit v1 on v0

v1 whole, which is shorter than its diff:
```python
import functools
import math

import jax
import jax.numpy as jnp
from jax import lax
from jax.experimental import pallas as pl
from jax.experimental.pallas import tpu as pltpu
from jax.sharding import PartitionSpec as P

WIN = 4
KEYS = 128
HEADS = 2
MASKED = -1e30
NT = (((1,), (1,)), ((), ()))
NN = (((1,), (0,)), ((), ()))


def dot(a, b, dims):
    return lax.dot_general(a, b, dims, preferred_element_type=jnp.float32)


def fold(x, op):
    return op(x.reshape(x.shape[0] // 8, 8, x.shape[1]), axis=0)


def attend_kernel(tiles, tile_of, flip_of, last, *refs):
    info, q_ref, do_ref = refs[:3]
    shard_refs = refs[3 : 3 + WIN]
    rest = refs[3 + WIN :]
    if last and tiles > 1:
        acc_in, _, _ = rest[:3]
        rest = rest[3:]
    else:
        acc_in = None
    out_ref, dq_ref = rest[:2]
    if last:
        own_ref = rest[2]
        far_refs = rest[3 : 2 + WIN]
        rest = rest[2 + WIN :]
    else:
        acc_out = rest[2]
        rest = rest[3:]
    k_ref, v_ref, kt_ref, vt_ref, bias_ref, s_ref, p_ref, ds_ref, acc_ref = rest

    shard = shard_refs[0].shape[0]
    hd = shard_refs[0].shape[1] // 2
    rows = q_ref.shape[0]
    lead = (WIN - 1) * shard
    blocks = bias_ref.shape[0] // KEYS
    step = pl.program_id(0)
    tile = tile_of(info)
    base = pl.multiple_of(tile * rows, KEYS)
    log2e = math.log2(math.e) / math.sqrt(hd)

    @pl.when(step == 0)
    def _():
        part = shard // tiles
        for s in range(WIN):
            for j in range(tiles):
                at = pl.multiple_of((WIN - 1 - s) * shard + (j ^ flip_of(info)) * part, 8 if part % KEYS else KEYS)
                k_ref[pl.ds(at, part), :] = shard_refs[s][j * part : (j + 1) * part, :hd]
                v_ref[pl.ds(at, part), :] = shard_refs[s][j * part : (j + 1) * part, hd:]
        for b in range(blocks):
            at = pl.ds(pl.multiple_of(base + b * KEYS, KEYS), KEYS)
            cols = slice(b * KEYS, (b + 1) * KEYS)
            kt_ref[:, cols] = k_ref[at, :].T
            vt_ref[:, cols] = v_ref[at, :].T
        first = info[0] * shard + tile * rows
        query = first + lax.broadcasted_iota(jnp.int32, (1, rows), 1)
        low = jnp.zeros((1, rows), jnp.int32)
        start = jnp.int32(0)
        for d in range(info.shape[0] - 2):
            low = jnp.where(query >= start, start, low)
            start = start + info[2 + d]
        for b in range(blocks):
            key = first - lead + b * KEYS + lax.broadcasted_iota(jnp.int32, (KEYS, rows), 0)
            ok = (key >= low) & (key <= query)
            bias_ref[b * KEYS : (b + 1) * KEYS, :] = jnp.where(ok, 0.0, MASKED)
        if acc_in is not None:
            acc_ref[...] = acc_in[...]
        else:
            acc_ref[...] = jnp.zeros_like(acc_ref)

    def block(b):
        return pl.ds(pl.multiple_of(base + b * KEYS, KEYS), KEYS)

    q = jnp.concatenate([q_ref[:, i * hd : (i + 1) * hd] for i in range(HEADS)], axis=0)
    do = jnp.concatenate([do_ref[:, i * hd : (i + 1) * hd] for i in range(HEADS)], axis=0)
    top = None
    for b in range(blocks):
        bias = bias_ref[b * KEYS : (b + 1) * KEYS, :]
        s = dot(k_ref[block(b), :], q, NT) + jnp.concatenate([bias] * HEADS, axis=1)
        s_ref[b * KEYS : (b + 1) * KEYS, :] = s
        m = fold(s, jnp.max)
        top = m if top is None else jnp.maximum(top, m)
    top = jnp.max(top, axis=0, keepdims=True)
    total = None
    for b in range(blocks):
        at = slice(b * KEYS, (b + 1) * KEYS)
        e = jnp.exp2((s_ref[at, :] - top) * log2e)
        s_ref[at, :] = e
        m = fold(e, jnp.sum)
        total = m if total is None else total + m
    inverse = 1.0 / jnp.sum(total, axis=0, keepdims=True)
    for b in range(blocks):
        at = slice(b * KEYS, (b + 1) * KEYS)
        p = s_ref[at, :] * inverse
        s_ref[at, :] = p
        p_ref[at, :] = p.astype(jnp.bfloat16)
    out = dot(vt_ref[...], p_ref[...], NN).astype(jnp.bfloat16)
    delta = jnp.sum(do.T.astype(jnp.float32) * out.astype(jnp.float32), axis=0, keepdims=True)
    for i in range(HEADS):
        out_ref[:, i * hd : (i + 1) * hd] = out[:, i * rows : (i + 1) * rows].T
    for b in range(blocks):
        at = slice(b * KEYS, (b + 1) * KEYS)
        dp = dot(v_ref[block(b), :], do, NT)
        ds = (s_ref[at, :] * (dp - delta)).astype(jnp.bfloat16)
        ds_ref[at, :] = ds
        acc_ref[block(b), :hd] += dot(ds, q, NN)
        acc_ref[block(b), hd:] += dot(p_ref[at, :], do, NN)
    dq = (dot(kt_ref[...], ds_ref[...], NN) / math.sqrt(hd)).astype(jnp.bfloat16)
    for i in range(HEADS):
        dq_ref[:, i * hd : (i + 1) * hd] = dq[:, i * rows : (i + 1) * rows].T

    @pl.when(step == pl.num_programs(0) - 1)
    def _():
        if last:
            own_ref[:, :hd] = acc_ref[lead:, :hd] / math.sqrt(hd)
            own_ref[:, hd:] = acc_ref[lead:, hd:]
            for s in range(1, WIN):
                at = slice((WIN - 1 - s) * shard, (WIN - s) * shard)
                far_refs[s - 1][:, :hd] = (acc_ref[at, :hd] / math.sqrt(hd)).astype(jnp.bfloat16)
                far_refs[s - 1][:, hd:] = acc_ref[at, hd:].astype(jnp.bfloat16)
        else:
            acc_out[...] = acc_ref[...]


def attend(info, q, do, shards, before, tiles, tile_of, flip_of, q_column):
    shard, width = shards[0].shape
    hd = width // 2
    rows = shard // tiles
    columns = HEADS * hd
    heads_columns = q_column[1]
    last = before is not None or tiles == 1
    keys = (WIN - 1) * shard + rows
    whole = pl.BlockSpec(memory_space=pltpu.VMEM)
    q_spec = pl.BlockSpec((rows, columns), lambda p, n: (0, q_column[0](n) + p))
    o_spec = pl.BlockSpec((rows, columns), lambda p, n: (tile_of(n), p))
    o_shape = jax.ShapeDtypeStruct((shard, heads_columns), jnp.bfloat16)
    acc_shape = jax.ShapeDtypeStruct((WIN * shard, width), jnp.float32)
    in_specs = [q_spec, q_spec] + [whole] * WIN
    args = [q, do, *shards]
    aliases = {}
    if before is not None:
        acc, out, dq = before
        in_specs += [whole, pl.BlockSpec(memory_space=pl.ANY), pl.BlockSpec(memory_space=pl.ANY)]
        aliases = {len(args) + 2: 0, len(args) + 3: 1}
        args += [acc, out, dq]
    if last:
        out_specs = [o_spec, o_spec] + [whole] * WIN
        out_shape = [o_shape, o_shape, jax.ShapeDtypeStruct((shard, width), jnp.float32)]
        out_shape += [jax.ShapeDtypeStruct((shard, width), jnp.bfloat16)] * (WIN - 1)
    else:
        out_specs = [o_spec, o_spec, whole]
        out_shape = [o_shape, o_shape, acc_shape]
    n = HEADS * rows
    return pl.pallas_call(
        functools.partial(attend_kernel, tiles, tile_of, flip_of, last),
        out_shape=out_shape,
        grid_spec=pltpu.PrefetchScalarGridSpec(
            num_scalar_prefetch=1,
            grid=(heads_columns // columns,),
            in_specs=in_specs,
            out_specs=out_specs,
            scratch_shapes=[
                pltpu.VMEM((WIN * shard, hd), jnp.bfloat16),
                pltpu.VMEM((WIN * shard, hd), jnp.bfloat16),
                pltpu.VMEM((hd, keys), jnp.bfloat16),
                pltpu.VMEM((hd, keys), jnp.bfloat16),
                pltpu.VMEM((keys, rows), jnp.float32),
                pltpu.VMEM((keys, n), jnp.float32),
                pltpu.VMEM((keys, n), jnp.bfloat16),
                pltpu.VMEM((keys, n), jnp.bfloat16),
                pltpu.VMEM((WIN * shard, width), jnp.float32),
            ],
        ),
        input_output_aliases=aliases,
        cost_estimate=pl.CostEstimate(
            flops=12 * keys * rows * heads_columns, transcendentals=keys * rows * heads_columns // hd, bytes_accessed=1 << 21
        ),
        name="attend_last" if last else "attend_first",
    )(info, *args)


def gather_kernel(own_ref, *refs):
    total = own_ref[...]
    for r in refs[:-2]:
        total = total + r[...].astype(jnp.float32)
    hd = refs[-1].shape[1]
    refs[-2][...] = total[:, :hd].astype(jnp.bfloat16)
    refs[-1][...] = total[:, hd:].astype(jnp.bfloat16)


def ring(value, axis, steps):
    count = lax.axis_size(axis)
    return lax.ppermute(value, axis, [(i, (i + steps) % count) for i in range(count)])


def body(queries, keys, values, d_out, doc_lengths):
    count = lax.axis_size("head")
    head = lax.axis_index("head")
    part = queries.shape[0]
    shard = count * part
    hd = keys.shape[1] // count
    group_columns = queries.shape[1] // count
    info = jnp.concatenate([jnp.stack([lax.axis_index("ctx"), head]).astype(jnp.int32), doc_lengths])
    if count == 2:
        other = 1 - head

        def columns(x, index, width):
            return lax.dynamic_slice_in_dim(x, index * width, width, 1)

        def key_value(index):
            return jnp.concatenate([columns(keys, index, hd), columns(values, index, hd)], axis=1)

        def swap(x):
            return lax.ppermute(x, "head", [(0, 1), (1, 0)])

        own = jnp.concatenate([key_value(head), swap(key_value(other))], axis=0)
        q_other = swap(columns(queries, other, group_columns))
        do_other = swap(columns(d_out, other, group_columns))
        shards = [own] + [ring(own, "ctx", s) for s in range(1, WIN)]
        blocks = group_columns // (HEADS * hd)
        flip_of = lambda n: n[1]
        first = attend(
            info, queries, d_out, shards, None, 2, lambda n: n[1], flip_of, (lambda n: n[1] * blocks, group_columns)
        )
        out, dq, total, *far = attend(
            info, q_other, do_other, shards, (first[2], first[0], first[1]), 2, lambda n: 1 - n[1], flip_of,
            (lambda n: 0, group_columns),
        )
    else:
        swap = lambda x: lax.all_to_all(x, "head", split_axis=1, concat_axis=0, tiled=True)
        own = jnp.concatenate([swap(keys), swap(values)], axis=1)
        shards = [own] + [ring(own, "ctx", s) for s in range(1, WIN)]
        zero = lambda n: 0
        out, dq, total, *far = attend(
            info, swap(queries), swap(d_out), shards, None, 1, zero, zero, (zero, group_columns)
        )
    near = [ring(x, "ctx", -s) for s, x in zip(range(1, WIN), far)]
    grad_keys, grad_values = pl.pallas_call(
        gather_kernel, out_shape=[jax.ShapeDtypeStruct((shard, hd), jnp.bfloat16)] * 2, name="gather"
    )(total, *near)
    return out, dq, grad_keys, grad_values


def solution(mesh):
    rows = P(("ctx", "head"), None)
    return jax.shard_map(
        body,
        mesh=mesh,
        in_specs=(rows, rows, rows, rows, P()),
        out_specs=(P("ctx", "head"),) * 4,
        check_vma=False,
    )
```

time: 89.2 us -> 56.8 us (0.64)
  the two profiles are of different devices: /device:TPU:1 before, /device:TPU:0 now
where the time goes in v1:
time: 56.8 us; the launch traced here: 56.5 us
  Pallas kernels  25.9 us (46%)
  waiting for transfers between devices  15.1 us (27%)
  starting transfers between devices  9.55 us (17%)
  local copies, waits for them, and re-layouts  4.55 us (8%)
  between operations  0.75 us (1%)
  other arithmetic  0.58 us (1%)
    pallas_call x2, Pallas kernels, attend(): pl.pallas_call(functools.partial(attend_kernel, tiles, tile_of, flip_of,...  24.1 us
    ppermute x6, waiting for transfers between devices, ring(): lax.ppermute(value, axis, [(i, (i + steps) % count) for i in range(count)])  13.7 us
    ppermute x3, starting transfers between devices, swap(): return lax.ppermute(x, 'head', [(0, 1), (1, 0)])  5.26 us
    ppermute x6, starting transfers between devices, ring(): lax.ppermute(value, axis, [(i, (i + steps) % count) for i in range(count)])  4.29 us
    unnamed x22, local copies, waits for them, and re-layouts  2.74 us
    dynamic_slice x3, local copies, waits for them, and re-layouts, columns(): return lax.dynamic_slice_in_dim(x, index * width, width, 1)  1.81 us
    pallas_call x1, Pallas kernels, body(): pl.pallas_call(gather_kernel, out_shape=[jax.ShapeDtypeStruct((shard, hd)...  1.81 us
    ppermute x3, waiting for transfers between devices, swap(): return lax.ppermute(x, 'head', [(0, 1), (1, 0)])  1.39 us
  transfers between devices with their start and end apart: 9, of which 6 were waited for; matrix products, arithmetic and copies ran while one was open for 3% of the time, Pallas kernels for 21%

profile of v1, /device:TPU:0, one launch (start us, length us, event | category | flops | bytes accessed | tf_op | source)
XLA Modules:
  0.0 56.5 jit_solution(17386457773225777435)
XLA Ops:
  0.6 0.8 %constant_dynamic-slice_fusion.2 = (bf16[128,128]{1,0:T(8,128)(2,1)S(1)}, bf16[128,128]{1,0:T(8,128)(2,1)S(1)}, bf16[128,128]{1,0:T(8,128)(2,1)S(1)}, bf16[128,128]{1,0:T(8,128)(2,1)S(1)}) fusion(bf16[128,256]{1,0:T(8,128)(2,1)} %param.7, s32[]{:T(128)S(6)} %select_n.13, s32[]{:T(128)S(6)} %select_n.14, bf16[128,256]{1,0:T(8,128)(2,1)} %param.6), kind=kLoop, calls=%fused_computation.4 | loop fusion | bytes 262152 | tf_op jit(solution)/shard_map/dynamic_slice | solution.py:222
  1.5 0.0 copy-start.3
  1.5 3.0 %collective-permute-start.2 = (bf16[128,256]{1,0:T(8,128)(2,1)S(1)}, bf16[128,256]{1,0:T(8,128)(2,1)S(1)}, u32[]{:S(2)}, u32[]{:S(2)}) collective-permute-start(bf16[128,256]{1,0:T(8,128)(2,1)S(1)} %pad_maximum_fusion.1), channel_id=1, source_target_pairs={{0,1},{1,0},{2,3},{3,2},{4,5},{5,4},{6,7},{7,6},{8,9},{9,8},{10,11... | collective-permute-start | bytes 196616 | tf_op jit(solution)/shard_map/ppermute | solution.py:228
  4.5 1.0 %constant_dynamic-slice_fusion.4 = bf16[128,1024]{1,0:T(8,128)(2,1)S(1)} fusion(bf16[128,2048]{1,0:T(8,128)(2,1)} %refs_2_.1, s32[]{:T(128)S(6)} %select_n.12), kind=kLoop, calls=%fused_computation.6 | loop fusion | bytes 524292 | tf_op jit(solution)/shard_map/dynamic_slice | solution.py:222
  5.5 0.1 collective-permute-start.1
  5.6 1.4 %collective-permute-done.2 = bf16[128,256]{1,0:T(8,128)(2,1)S(1)} collective-permute-done((bf16[128,256]{1,0:T(8,128)(2,1)S(1)}, bf16[128,256]{1,0:T(8,128)(2,1)S(1)}, u32[]{:S(2)}, u32[]{:S(2)}) %collective-permute-start.2) | collective-permute-done | bytes 65568 | tf_op jit(solution)/shard_map/ppermute | solution.py:228
  7.0 0.0 copy-start.4
  7.0 0.2 collective-permute-start.5
  7.2 1.8 %collective-permute-start.4 = (bf16[256,256]{1,0:T(8,128)(2,1)S(1)}, bf16[256,256]{1,0:T(8,128)(2,1)S(1)}, u32[]{:S(2)}, u32[]{:S(2)}) collective-permute-start(bf16[256,256]{1,0:T(8,128)(2,1)S(1)} %pad_maximum_fusion.refs_3_), channel_id=1, source_target_pairs={{0,4},{2,6},{4,8},{6,10},{8,12},{10,14},{12,16},{14,18},{16,20},{1... | collective-permute-start | bytes 393224 | tf_op jit(solution)/shard_map/ppermute | solution.py:207
  9.0 1.3 %collective-permute-start.3 = (bf16[256,256]{1,0:T(8,128)(2,1)S(1)}, bf16[256,256]{1,0:T(8,128)(2,1)S(1)}, u32[]{:S(2)}, u32[]{:S(2)}) collective-permute-start(bf16[256,256]{1,0:T(8,128)(2,1)S(1)} %pad_maximum_fusion.refs_3_), channel_id=1, source_target_pairs={{0,2},{2,4},{4,6},{6,8},{8,10},{10,12},{12,14},{14,16},{16,18},{18... | collective-permute-start | bytes 393224 | tf_op jit(solution)/shard_map/ppermute | solution.py:207
  10.3 0.0 copy-done.3
  10.3 0.0 copy-done.4
  10.4 2.1 %collective-permute-start = (bf16[128,1024]{1,0:T(8,128)(2,1)S(1)}, bf16[128,1024]{1,0:T(8,128)(2,1)S(1)}, u32[]{:S(2)}, u32[]{:S(2)}) collective-permute-start(bf16[128,1024]{1,0:T(8,128)(2,1)S(1)} %constant_dynamic-slice_fusion.5), channel_id=1, source_target_pairs={{0,1},{1,0},{2,3},{3,2},{4,5},{5,4},{6,7},{7,6},{8,9},{9,8},{10,11... | collective-permute-start | bytes 786440 | tf_op jit(solution)/shard_map/ppermute | solution.py:228
  12.5 0.0 copy-start.5
  12.5 0.7 %copy-done.5 = s32[32]{0:T(128)S(1)} copy-done((s32[32]{0:T(128)S(1)}, s32[32]{0:T(128)}, u32[]{:S(2)}) %copy-start.5) | copy-done | bytes 152
  13.1 0.6 pad_add_fusion.refs_0_
  13.7 0.0 collective-permute-done.5.refs_6_
  13.7 0.0 copy-start.8
  13.7 5.4 %collective-permute-done.4.refs_5_ = bf16[256,256]{1,0:T(8,128)(2,1)S(1)} collective-permute-done((bf16[256,256]{1,0:T(8,128)(2,1)S(1)}, bf16[256,256]{1,0:T(8,128)(2,1)S(1)}, u32[]{:S(2)}, u32[]{:S(2)}) %collective-permute-start.4) | collective-permute-done | bytes 131104 | tf_op jit(solution)/shard_map/ppermute | solution.py:207
  19.1 0.0 copy-start.9
  19.1 1.0 %collective-permute-done.3.refs_4_ = bf16[256,256]{1,0:T(8,128)(2,1)S(1)} collective-permute-done((bf16[256,256]{1,0:T(8,128)(2,1)S(1)}, bf16[256,256]{1,0:T(8,128)(2,1)S(1)}, u32[]{:S(2)}, u32[]{:S(2)}) %collective-permute-start.3) | collective-permute-done | bytes 131104 | tf_op jit(solution)/shard_map/ppermute | solution.py:207
  20.1 0.0 copy-done.8
  20.2 0.0 copy-done.9
  20.2 0.0 copy-start.10
  20.2 0.6 %copy-done.10 = bf16[256,256]{1,0:T(8,128)(2,1)} copy-done((bf16[256,256]{1,0:T(8,128)(2,1)}, bf16[256,256]{1,0:T(8,128)(2,1)S(1)}, u32[]{:S(2)}) %copy-start.10) | copy-done | bytes 131096
  20.8 11.9 %attend_first.1 = (bf16[256,1024]{1,0:T(8,128)(2,1)}, bf16[256,1024]{1,0:T(8,128)(2,1)}, f32[1024,256]{1,0:T(8,128)}) custom-call(s32[34]{0:T(128)} %pad_add_fusion.refs_0_, bf16[128,2048]{1,0:T(8,128)(2,1)} %refs_1_.1, bf16[128,2048]{1,0:T(8,128)(2,1)} %refs_2_.1, bf16[256,256]{1,0:T(8,128)(2,1)} %copy-done.4, bf16[256,256]{1,0:T(8,128)(2,1)} %copy-done.10, ...), custom_call_target="tpu_custom_call" | custom-call | flops 1409286144 | bytes 2097152 | tf_op jit(solution)/shard_map/attend_first/pallas_call | solution.py:168
  32.7 0.0 collective-permute-done.1.refs_2_
  32.7 0.0 copy-start.6
  32.8 0.0 collective-permute-done.refs_1_
  32.8 0.0 copy-start.7
  32.8 0.7 %copy-done.6 = bf16[128,1024]{1,0:T(8,128)(2,1)} copy-done((bf16[128,1024]{1,0:T(8,128)(2,1)}, bf16[128,1024]{1,0:T(8,128)(2,1)S(1)}, u32[]{:S(2)}) %copy-start.6) | copy-done | bytes 262168
  33.4 0.1 copy-done.7
  33.5 12.2 %attend_last.1 = (bf16[256,1024]{1,0:T(8,128)(2,1)}, bf16[256,1024]{1,0:T(8,128)(2,1)}, f32[256,256]{1,0:T(8,128)}, bf16[256,256]{1,0:T(8,128)(2,1)}, bf16[256,2...) custom-call(s32[34]{0:T(128)} %pad_add_fusion.refs_0_, ...), custom_call_target="tpu_custom_call", output_to_operand_aliasing={{0}: (8, {}), {1}: (9, {})} | custom-call | flops 1409286144 | bytes 2097152 | tf_op jit(solution)/shard_map/attend_last/pallas_call | solution.py:168
  45.7 0.1 collective-permute-start.6
  45.8 1.0 %collective-permute-start.7 = (bf16[256,256]{1,0:T(8,128)(2,1)}, bf16[256,256]{1,0:T(8,128)(2,1)S(1)}, u32[]{:S(2)}, u32[]{:S(2)}) collective-permute-start(bf16[256,256]{1,0:T(8,128)(2,1)} %get-tuple-element.22), channel_id=1, source_target_pairs={{0,28},{2,30},{4,0},{6,2},{8,4},{10,6},{12,8},{14,10},{16,12},{18,... | collective-permute-start | bytes 393224 | tf_op jit(solution)/shard_map/ppermute | solution.py:207
  46.7 0.0 collective-permute-start.8
  46.7 3.2 %collective-permute-done.6.refs_0_ = bf16[256,256]{1,0:T(8,128)(2,1)S(1)} collective-permute-done((bf16[256,256]{1,0:T(8,128)(2,1)}, bf16[256,256]{1,0:T(8,128)(2,1)S(1)}, u32[]{:S(2)}, u32[]{:S(2)}) %collective-permute-start.6) | collective-permute-done | bytes 131104 | tf_op jit(solution)/shard_map/ppermute | solution.py:207
  50.0 0.0 copy-start
  50.0 2.9 %collective-permute-done.7.refs_1_ = bf16[256,256]{1,0:T(8,128)(2,1)S(1)} collective-permute-done((bf16[256,256]{1,0:T(8,128)(2,1)}, bf16[256,256]{1,0:T(8,128)(2,1)S(1)}, u32[]{:S(2)}, u32[]{:S(2)}) %collective-permute-start.7) | collective-permute-done | bytes 131104 | tf_op jit(solution)/shard_map/ppermute | solution.py:207
  52.9 0.0 copy-start.1
  52.9 1.1 %collective-permute-done.8.refs_2_ = bf16[256,256]{1,0:T(8,128)(2,1)S(1)} collective-permute-done((bf16[256,256]{1,0:T(8,128)(2,1)}, bf16[256,256]{1,0:T(8,128)(2,1)S(1)}, u32[]{:S(2)}, u32[]{:S(2)}) %collective-permute-start.8) | collective-permute-done | bytes 131104 | tf_op jit(solution)/shard_map/ppermute | solution.py:207
  54.0 0.0 copy-start.2
  54.0 0.0 copy-done
  54.0 0.0 copy-done.1
  54.0 0.6 %copy-done.2 = bf16[256,256]{1,0:T(8,128)(2,1)} copy-done((bf16[256,256]{1,0:T(8,128)(2,1)}, bf16[256,256]{1,0:T(8,128)(2,1)S(1)}, u32[]{:S(2)}) %copy-start.2) | copy-done | bytes 131096
  54.7 1.8 %gather.1 = (bf16[256,128]{1,0:T(8,128)(2,1)}, bf16[256,128]{1,0:T(8,128)(2,1)}) custom-call(f32[256,256]{1,0:T(8,128)} %get-tuple-element.20.own_ref, bf16[256,256]{1,0:T(8,128)(2,1)} %copy-done, bf16[256,256]{1,0:T(8,128)(2,1)} %copy-done.1, bf16[256,256]{1,0:T(8,128)(2,1)} %copy-done.2), custom_call_target="tpu_custom_call" | custom-call | tf_op jit(solution)/shard_map/gather/pallas_call | solution.py:252
  (3 shorter events, 0.0 us)
Async XLA Ops:
  1.5 8.9 %copy-start.3 = (bf16[128,2048]{1,0:T(8,128)(2,1)S(1)}, bf16[128,2048]{1,0:T(8,128)(2,1)}, u32[]{:S(2)}) copy-start(bf16[128,2048]{1,0:T(8,128)(2,1)} %refs_1_.1) | copy-start | bytes 1572868
  1.5 5.5 %collective-permute-start.2 = (bf16[128,256]{1,0:T(8,128)(2,1)S(1)}, bf16[128,256]{1,0:T(8,128)(2,1)S(1)}, u32[]{:S(2)}, u32[]{:S(2)}) collective-permute-start(bf16[128,256]{1,0:T(8,128)(2,1)S(1)} %pad_maximum_fusion.1), channel_id=1, source_target_pairs={{0,1},{1,0},{2,3},{3,2},{4,5},{5,4},{6,7},{7,6},{8,9},{9,8},{10,11... | collective-permute-start | bytes 196616 | tf_op jit(solution)/shard_map/ppermute | solution.py:228
  5.5 27.2 %collective-permute-start.1 = (bf16[128,1024]{1,0:T(8,128)(2,1)S(1)}, bf16[128,1024]{1,0:T(8,128)(2,1)S(1)}, u32[]{:S(2)}, u32[]{:S(2)}) collective-permute-start(bf16[128,1024]{1,0:T(8,128)(2,1)S(1)} %constant_dynamic-slice_fusion.4), channel_id=1, source_target_pairs={{0,1},{1,0},{2,3},{3,2},{4,5},{5,4},{6,7},{7,6},{8,9},{9,8},{10,11... | collective-permute-start | bytes 786440 | tf_op jit(solution)/shard_map/ppermute | solution.py:228
  7.0 3.3 %copy-start.4 = (bf16[256,256]{1,0:T(8,128)(2,1)}, bf16[256,256]{1,0:T(8,128)(2,1)S(1)}, u32[]{:S(2)}) copy-start(bf16[256,256]{1,0:T(8,128)(2,1)S(1)} %pad_maximum_fusion.refs_3_) | copy-start | bytes 393220
  7.0 6.6 %collective-permute-start.5 = (bf16[256,256]{1,0:T(8,128)(2,1)S(1)}, bf16[256,256]{1,0:T(8,128)(2,1)S(1)}, u32[]{:S(2)}, u32[]{:S(2)}) collective-permute-start(bf16[256,256]{1,0:T(8,128)(2,1)S(1)} %pad_maximum_fusion.refs_3_), channel_id=1, source_target_pairs={{0,6},{2,8},{4,10},{6,12},{8,14},{10,16},{12,18},{14,20},{16,22},{... | collective-permute-start | bytes 393224 | tf_op jit(solution)/shard_map/ppermute | solution.py:207
  7.2 11.9 %collective-permute-start.4 = (bf16[256,256]{1,0:T(8,128)(2,1)S(1)}, bf16[256,256]{1,0:T(8,128)(2,1)S(1)}, u32[]{:S(2)}, u32[]{:S(2)}) collective-permute-start(bf16[256,256]{1,0:T(8,128)(2,1)S(1)} %pad_maximum_fusion.refs_3_), channel_id=1, source_target_pairs={{0,4},{2,6},{4,8},{6,10},{8,12},{10,14},{12,16},{14,18},{16,20},{1... | collective-permute-start | bytes 393224 | tf_op jit(solution)/shard_map/ppermute | solution.py:207
  9.0 11.2 %collective-permute-start.3 = (bf16[256,256]{1,0:T(8,128)(2,1)S(1)}, bf16[256,256]{1,0:T(8,128)(2,1)S(1)}, u32[]{:S(2)}, u32[]{:S(2)}) collective-permute-start(bf16[256,256]{1,0:T(8,128)(2,1)S(1)} %pad_maximum_fusion.refs_3_), channel_id=1, source_target_pairs={{0,2},{2,4},{4,6},{6,8},{8,10},{10,12},{12,14},{14,16},{16,18},{18... | collective-permute-start | bytes 393224 | tf_op jit(solution)/shard_map/ppermute | solution.py:207
  10.4 22.4 %collective-permute-start = (bf16[128,1024]{1,0:T(8,128)(2,1)S(1)}, bf16[128,1024]{1,0:T(8,128)(2,1)S(1)}, u32[]{:S(2)}, u32[]{:S(2)}) collective-permute-start(bf16[128,1024]{1,0:T(8,128)(2,1)S(1)} %constant_dynamic-slice_fusion.5), channel_id=1, source_target_pairs={{0,1},{1,0},{2,3},{3,2},{4,5},{5,4},{6,7},{7,6},{8,9},{9,8},{10,11... | collective-permute-start | bytes 786440 | tf_op jit(solution)/shard_map/ppermute | solution.py:228
  12.5 0.7 %copy-start.5 = (s32[32]{0:T(128)S(1)}, s32[32]{0:T(128)}, u32[]{:S(2)}) copy-start(s32[32]{0:T(128)} %param.9) | copy-start | bytes 388
  13.7 6.5 %copy-start.8 = (bf16[256,256]{1,0:T(8,128)(2,1)}, bf16[256,256]{1,0:T(8,128)(2,1)S(1)}, u32[]{:S(2)}) copy-start(bf16[256,256]{1,0:T(8,128)(2,1)S(1)} %collective-permute-done.5.refs_6_) | copy-start | bytes 393220
  19.1 1.1 %copy-start.9 = (bf16[256,256]{1,0:T(8,128)(2,1)}, bf16[256,256]{1,0:T(8,128)(2,1)S(1)}, u32[]{:S(2)}) copy-start(bf16[256,256]{1,0:T(8,128)(2,1)S(1)} %collective-permute-done.4.refs_5_) | copy-start | bytes 393220
  20.2 0.6 %copy-start.10 = (bf16[256,256]{1,0:T(8,128)(2,1)}, bf16[256,256]{1,0:T(8,128)(2,1)S(1)}, u32[]{:S(2)}) copy-start(bf16[256,256]{1,0:T(8,128)(2,1)S(1)} %collective-permute-done.3.refs_4_) | copy-start | bytes 393220
  32.7 0.7 %copy-start.6 = (bf16[128,1024]{1,0:T(8,128)(2,1)}, bf16[128,1024]{1,0:T(8,128)(2,1)S(1)}, u32[]{:S(2)}) copy-start(bf16[128,1024]{1,0:T(8,128)(2,1)S(1)} %collective-permute-done.1.refs_2_) | copy-start | bytes 786436
  32.8 0.8 %copy-start.7 = (bf16[128,1024]{1,0:T(8,128)(2,1)}, bf16[128,1024]{1,0:T(8,128)(2,1)S(1)}, u32[]{:S(2)}) copy-start(bf16[128,1024]{1,0:T(8,128)(2,1)S(1)} %collective-permute-done.refs_1_) | copy-start | bytes 786436
  45.7 4.3 %collective-permute-start.6 = (bf16[256,256]{1,0:T(8,128)(2,1)}, bf16[256,256]{1,0:T(8,128)(2,1)S(1)}, u32[]{:S(2)}, u32[]{:S(2)}) collective-permute-start(bf16[256,256]{1,0:T(8,128)(2,1)} %get-tuple-element.21), channel_id=1, source_target_pairs={{0,30},{2,0},{4,2},{6,4},{8,6},{10,8},{12,10},{14,12},{16,14},{18,... | collective-permute-start | bytes 393224 | tf_op jit(solution)/shard_map/ppermute | solution.py:207
  45.8 7.1 %collective-permute-start.7 = (bf16[256,256]{1,0:T(8,128)(2,1)}, bf16[256,256]{1,0:T(8,128)(2,1)S(1)}, u32[]{:S(2)}, u32[]{:S(2)}) collective-permute-start(bf16[256,256]{1,0:T(8,128)(2,1)} %get-tuple-element.22), channel_id=1, source_target_pairs={{0,28},{2,30},{4,0},{6,2},{8,4},{10,6},{12,8},{14,10},{16,12},{18,... | collective-permute-start | bytes 393224 | tf_op jit(solution)/shard_map/ppermute | solution.py:207
  46.7 7.3 %collective-permute-start.8 = (bf16[256,256]{1,0:T(8,128)(2,1)}, bf16[256,256]{1,0:T(8,128)(2,1)S(1)}, u32[]{:S(2)}, u32[]{:S(2)}) collective-permute-start(bf16[256,256]{1,0:T(8,128)(2,1)} %get-tuple-element.23), channel_id=1, source_target_pairs={{0,26},{2,28},{4,30},{6,0},{8,2},{10,4},{12,6},{14,8},{16,10},{18,... | collective-permute-start | bytes 393224 | tf_op jit(solution)/shard_map/ppermute | solution.py:207
  50.0 4.0 %copy-start = (bf16[256,256]{1,0:T(8,128)(2,1)}, bf16[256,256]{1,0:T(8,128)(2,1)S(1)}, u32[]{:S(2)}) copy-start(bf16[256,256]{1,0:T(8,128)(2,1)S(1)} %collective-permute-done.6.refs_0_) | copy-start | bytes 393220
  52.9 1.1 %copy-start.1 = (bf16[256,256]{1,0:T(8,128)(2,1)}, bf16[256,256]{1,0:T(8,128)(2,1)S(1)}, u32[]{:S(2)}) copy-start(bf16[256,256]{1,0:T(8,128)(2,1)S(1)} %collective-permute-done.7.refs_1_) | copy-start | bytes 393220
  54.0 0.7 %copy-start.2 = (bf16[256,256]{1,0:T(8,128)(2,1)}, bf16[256,256]{1,0:T(8,128)(2,1)S(1)}, u32[]{:S(2)}) copy-start(bf16[256,256]{1,0:T(8,128)(2,1)S(1)} %collective-permute-done.8.refs_2_) | copy-start | bytes 393220

commit v2 on v1

v2 whole, which is shorter than its diff:
```python
import functools
import math

import jax
import jax.numpy as jnp
from jax import lax
from jax.experimental import pallas as pl
from jax.experimental.pallas import tpu as pltpu
from jax.sharding import PartitionSpec as P

WIN = 4
KEYS = 128
HEADS = 2
MASKED = -1e30
NT = (((1,), (1,)), ((), ()))
NN = (((1,), (0,)), ((), ()))
WHOLE = pl.BlockSpec(memory_space=pltpu.VMEM)
ANY = pl.BlockSpec(memory_space=pl.ANY)
SCALARS = pl.BlockSpec(memory_space=pltpu.SMEM)


def in_vmem(*arrays):
    return [pltpu.with_memory_space_constraint(x, pltpu.VMEM) for x in arrays]


def dot(a, b, dims):
    return lax.dot_general(a, b, dims, preferred_element_type=jnp.float32)


def fold(x, op):
    return op(x.reshape(x.shape[0] // 8, 8, x.shape[1]), axis=0)


def mask_kernel(lead, info, *bias_refs):
    keys, rows = bias_refs[0].shape
    shard = len(bias_refs) * rows
    for i, bias_ref in enumerate(bias_refs):
        tile = i ^ info[1] if len(bias_refs) > 1 else i
        first = info[0] * shard + tile * rows
        query = first + lax.broadcasted_iota(jnp.int32, (1, rows), 1)
        low = jnp.zeros((1, rows), jnp.int32)
        start = jnp.int32(0)
        for d in range(info.shape[0] - 2):
            low = jnp.where(query >= start, start, low)
            start = start + info[2 + d]
        for b in range(keys // KEYS):
            key = first - lead + b * KEYS + lax.broadcasted_iota(jnp.int32, (KEYS, rows), 0)
            ok = (key >= low) & (key <= query)
            bias_ref[b * KEYS : (b + 1) * KEYS, :] = jnp.where(ok, 0.0, MASKED)


def attend_kernel(tiles, index, info, q_hbm, do_hbm, bias_ref, *refs):
    shard_refs = refs[:WIN]
    refs = refs[WIN:]
    last = index == tiles - 1
    acc_in = None
    if index:
        acc_in = refs[0]
        refs = refs[3:]
    out_hbm, dq_hbm = refs[:2]
    if last:
        own_ref = refs[2]
        far_refs = refs[3 : 2 + WIN]
        refs = refs[2 + WIN :]
    else:
        acc_out = refs[2]
        refs = refs[3:]
    k_ref, v_ref, kt_ref, vt_ref, q_ref, do_ref, q_rows, do_rows, p_ref, ds_ref, out_ref, dq_ref, acc_ref, sem = refs

    shard, width = shard_refs[0].shape
    hd = width // 2
    keys, rows = bias_ref.shape
    lead = (WIN - 1) * shard
    blocks = keys // KEYS
    columns = out_hbm.shape[1]
    heads = columns // hd
    pairs = heads // HEADS
    flip = info[1] if tiles > 1 else 0
    tile = index ^ flip
    base = pl.multiple_of(tile * rows, KEYS)
    log2e = math.log2(math.e) / math.sqrt(hd)
    scaling = 1 / math.sqrt(hd)

    loads = []
    if q_hbm.shape[1] == columns:
        q_ref, do_ref = q_hbm, do_hbm
    else:
        mine = pl.ds(pl.multiple_of(info[1] * columns, 128), columns)
        loads = [
            pltpu.make_async_copy(q_hbm.at[:, mine], q_ref, sem.at[0]),
            pltpu.make_async_copy(do_hbm.at[:, mine], do_ref, sem.at[1]),
        ]
    for copy in loads:
        copy.start()
    part = shard // tiles
    for s in range(WIN):
        for j in range(tiles):
            at = pl.ds(pl.multiple_of((WIN - 1 - s) * shard + (j ^ flip) * part, KEYS), part)
            k_ref[at, :] = shard_refs[s][j * part : (j + 1) * part, :hd]
            v_ref[at, :] = shard_refs[s][j * part : (j + 1) * part, hd:]
    window = pl.ds(base, keys)
    for copy in loads:
        copy.wait()
    for h in range(heads):
        q_rows[h * rows : (h + 1) * rows, :] = q_ref[:, h * hd : (h + 1) * hd]
        do_rows[h * rows : (h + 1) * rows, :] = do_ref[:, h * hd : (h + 1) * hd]
    kt_ref[...] = k_ref[window, :].T
    vt_ref[...] = v_ref[window, :].T
    n = HEADS * rows

    def at(p):
        return slice(p * n, (p + 1) * n)

    def weights(p):
        s = dot(k_ref[window, :], q_rows[at(p), :], NT)
        s = s + jnp.concatenate([bias_ref[...]] * HEADS, axis=1)
        top = jnp.max(fold(s, jnp.max), axis=0, keepdims=True)
        e = jnp.exp2((s - top) * log2e)
        total = jnp.sum(fold(e, jnp.sum), axis=0, keepdims=True)
        p_f32 = e * (1.0 / total)
        p_ref[:, at(p)] = p_f32.astype(jnp.bfloat16)
        return p_f32

    def backward(p, p_f32):
        out = dot(vt_ref[...], p_ref[:, at(p)], NN).astype(jnp.bfloat16)
        do_t = do_rows[at(p), :].T.astype(jnp.float32)
        delta = jnp.sum(do_t * out.astype(jnp.float32), axis=0, keepdims=True)
        dp = dot(v_ref[window, :], do_rows[at(p), :], NT)
        ds_ref[:, at(p)] = (p_f32 * (dp - delta)).astype(jnp.bfloat16)
        dq = (dot(kt_ref[...], ds_ref[:, at(p)], NN) * scaling).astype(jnp.bfloat16)
        for i in range(HEADS):
            h = p * HEADS + i
            out_ref[:, h * hd : (h + 1) * hd] = out[:, i * rows : (i + 1) * rows].T
            dq_ref[:, h * hd : (h + 1) * hd] = dq[:, i * rows : (i + 1) * rows].T
        place = pl.ds(pl.multiple_of(tile * rows, rows), rows), pl.ds(p * HEADS * hd, HEADS * hd)
        here = slice(None), slice(p * HEADS * hd, (p + 1) * HEADS * hd)
        stores = [
            pltpu.make_async_copy(out_ref.at[here], out_hbm.at[place], sem.at[2 + 2 * p]),
            pltpu.make_async_copy(dq_ref.at[here], dq_hbm.at[place], sem.at[3 + 2 * p]),
        ]
        for copy in stores:
            copy.start()
        return stores

    stores = []
    ahead = weights(0)
    for p in range(pairs):
        now = ahead
        if p + 1 < pairs:
            ahead = weights(p + 1)
        stores += backward(p, now)
    dv = dot(p_ref[...], do_rows[...], NN)
    dk = dot(ds_ref[...], q_rows[...], NN)
    if not last:
        acc_out[...] = jnp.zeros_like(acc_out)
        acc_out[window, :hd] = dk
        acc_out[window, hd:] = dv
    else:
        if acc_in is None:
            acc_ref[:, :hd] = dk
            acc_ref[:, hd:] = dv
        else:
            acc_ref[...] = acc_in[...]
            acc_ref[window, :hd] += dk
            acc_ref[window, hd:] += dv
        own_ref[:, :hd] = acc_ref[lead:, :hd] * scaling
        own_ref[:, hd:] = acc_ref[lead:, hd:]
        for s in range(1, WIN):
            rows_of = slice((WIN - 1 - s) * shard, (WIN - s) * shard)
            far_refs[s - 1][:, :hd] = (acc_ref[rows_of, :hd] * scaling).astype(jnp.bfloat16)
            far_refs[s - 1][:, hd:] = acc_ref[rows_of, hd:].astype(jnp.bfloat16)
    for copy in stores:
        copy.wait()


def masks(info, shard, tiles):
    rows = shard // tiles
    lead = (WIN - 1) * shard
    return pl.pallas_call(
        functools.partial(mask_kernel, lead),
        out_shape=[pltpu.VMEM((lead + rows, rows), jnp.float32)] * tiles,
        in_specs=[SCALARS],
        out_specs=[WHOLE] * tiles,
        name="masks",
    )(info)


def attend(info, q, do, bias, shards, before, tiles, columns):
    shard, width = shards[0].shape
    hd = width // 2
    rows = shard // tiles
    index = 0 if before is None else 1
    last = index == tiles - 1
    keys = (WIN - 1) * shard + rows
    heads = columns // hd
    bf16, f32 = jnp.bfloat16, jnp.float32
    inner = q.shape[1] == columns
    args = [info, *(in_vmem(q, do) if inner else (q, do)), *in_vmem(bias, *shards)]
    in_specs = [SCALARS] + [WHOLE if inner else ANY] * 2 + [WHOLE] * (1 + WIN)
    aliases = {}
    if before is not None:
        aliases = {len(args) + 1: 0, len(args) + 2: 1}
        args += in_vmem(before[0]) + list(before[1:])
        in_specs += [WHOLE, ANY, ANY]
    out_shape = [jax.ShapeDtypeStruct((shard, columns), bf16)] * 2
    out_specs = [ANY, ANY]
    if last:
        out_shape += [pltpu.VMEM((shard, width), f32)] + [pltpu.VMEM((shard, width), bf16)] * (WIN - 1)
        out_specs += [WHOLE] * WIN
    else:
        out_shape += [pltpu.VMEM((WIN * shard, width), f32)]
        out_specs += [WHOLE]
    return pl.pallas_call(
        functools.partial(attend_kernel, tiles, index),
        out_shape=out_shape,
        in_specs=in_specs,
        out_specs=out_specs,
        scratch_shapes=[
            pltpu.VMEM((WIN * shard, hd), bf16),
            pltpu.VMEM((WIN * shard, hd), bf16),
            pltpu.VMEM((hd, keys), bf16),
            pltpu.VMEM((hd, keys), bf16),
            pltpu.VMEM((rows, columns) if not inner else (16, 128), bf16),
            pltpu.VMEM((rows, columns) if not inner else (16, 128), bf16),
            pltpu.VMEM((heads * rows, hd), bf16),
            pltpu.VMEM((heads * rows, hd), bf16),
            pltpu.VMEM((keys, heads * rows), bf16),
            pltpu.VMEM((keys, heads * rows), bf16),
            pltpu.VMEM((rows, columns), bf16),
            pltpu.VMEM((rows, columns), bf16),
            pltpu.VMEM((WIN * shard, width) if last else (8, 128), f32),
            pltpu.SemaphoreType.DMA((2 + 2 * (heads // HEADS),)),
        ],
        input_output_aliases=aliases,
        cost_estimate=pl.CostEstimate(
            flops=12 * keys * rows * columns, transcendentals=keys * rows * heads, bytes_accessed=1 << 21
        ),
        name="attend_last" if last else "attend_first",
    )(*args)


def gather_kernel(own_ref, *refs):
    total = own_ref[...]
    for r in refs[:-2]:
        total = total + r[...].astype(jnp.float32)
    hd = refs[-1].shape[1]
    refs[-2][...] = total[:, :hd].astype(jnp.bfloat16)
    refs[-1][...] = total[:, hd:].astype(jnp.bfloat16)


def ring(value, axis, steps):
    count = lax.axis_size(axis)
    return lax.ppermute(value, axis, [(i, (i + steps) % count) for i in range(count)])


def body(queries, keys, values, d_out, doc_lengths):
    count = lax.axis_size("head")
    head = lax.axis_index("head")
    part = queries.shape[0]
    shard = count * part
    hd = keys.shape[1] // count
    columns = queries.shape[1] // count
    info = jnp.concatenate([jnp.stack([lax.axis_index("ctx"), head]).astype(jnp.int32), doc_lengths])
    tiles = 2 if count == 2 else 1
    bias = masks(info, shard, tiles)
    if tiles == 2:
        other = 1 - head

        def half(x, index):
            width = x.shape[1] // 2
            return lax.dynamic_slice_in_dim(x, index * width, width, 1)

        def key_value(index):
            return jnp.concatenate([half(keys, index), half(values, index)], axis=1)

        def swap(x):
            return lax.ppermute(x, "head", [(0, 1), (1, 0)])

        own = jnp.concatenate([key_value(head), swap(key_value(other))], axis=0)
        q_other = swap(half(queries, other))
        do_other = swap(half(d_out, other))
        shards = [own] + [ring(own, "ctx", s) for s in range(1, WIN)]
        out, dq, acc = attend(info, queries, d_out, bias[0], shards, None, 2, columns)
        out, dq, total, *far = attend(info, q_other, do_other, bias[1], shards, (acc, out, dq), 2, columns)
    else:
        swap = lambda x: lax.all_to_all(x, "head", split_axis=1, concat_axis=0, tiled=True)
        own = jnp.concatenate([swap(keys), swap(values)], axis=1)
        shards = [own] + [ring(own, "ctx", s) for s in range(1, WIN)]
        out, dq, total, *far = attend(info, swap(queries), swap(d_out), bias[0], shards, None, 1, columns)
    near = [ring(x, "ctx", -s) for s, x in zip(range(1, WIN), far)]
    grad_keys, grad_values = pl.pallas_call(
        gather_kernel,
        out_shape=[jax.ShapeDtypeStruct((shard, hd), jnp.bfloat16)] * 2,
        in_specs=[WHOLE] * WIN,
        out_specs=[WHOLE] * 2,
        name="gather",
    )(*in_vmem(total, *near))
    return out, dq, grad_keys, grad_values


def solution(mesh):
    rows = P(("ctx", "head"), None)
    return jax.shard_map(
        body,
        mesh=mesh,
        in_specs=(rows, rows, rows, rows, P()),
        out_specs=(P("ctx", "head"),) * 4,
        check_vma=False,
    )
```

time: 56.8 us -> 47.8 us (0.84)
  Pallas kernels: 25.9 us -> 13.9 us
  local copies, waits for them, and re-layouts: 4.55 us -> 9.3 us
  waiting for transfers between devices: 15.1 us -> 13.3 us
    pallas_call x2 -> x3, Pallas kernels: 24.1 us -> 13.2 us  [the longest x2 12.3 us: attend(): pl.pallas_call(functools.partial(attend_kernel, tiles, index), out_shape=...]
    unnamed x22 -> x24, local copies, waits for them, and re-layouts: 2.74 us -> 6.78 us
    ppermute x6, waiting for transfers between devices: 13.7 us -> 11.9 us  [ring(): lax.ppermute(value, axis, [(i, (i + steps) % count) for i in range(count)])]
    pallas_call x1, Pallas kernels: 1.81 us -> 0.69 us  [body(): pl.pallas_call(gather_kernel, out_shape=[jax.ShapeDtypeStruct((shard, hd)...]
    dynamic_slice x3, local copies, waits for them, and re-layouts: 1.81 us -> 2.52 us  [half(): return lax.dynamic_slice_in_dim(x, index * width, width, 1)]
  transfers between devices with their start and end apart: 9 -> 9, of which waited for: 6 -> 6; matrix products, arithmetic and copies ran while one was open for 3% -> 5% of each run, Pallas kernels for 21% -> 16%
where the time goes in v2:
time: 47.8 us; the launch traced here: 47.3 us
  Pallas kernels  13.9 us (29%)
  waiting for transfers between devices  13.3 us (28%)
  starting transfers between devices  9.45 us (20%)
  local copies, waits for them, and re-layouts  9.3 us (19%)
  between operations  0.77 us (2%)
  other arithmetic  0.63 us (1%)
    pallas_call x2, Pallas kernels, attend(): pl.pallas_call(functools.partial(attend_kernel, tiles, index), out_shape=...  12.3 us
    ppermute x6, waiting for transfers between devices, ring(): lax.ppermute(value, axis, [(i, (i + steps) % count) for i in range(count)])  11.9 us
    unnamed x24, local copies, waits for them, and re-layouts  6.78 us
    ppermute x3, starting transfers between devices, swap(): return lax.ppermute(x, 'head', [(0, 1), (1, 0)])  5.2 us
    ppermute x6, starting transfers between devices, ring(): lax.ppermute(value, axis, [(i, (i + steps) % count) for i in range(count)])  4.25 us
    dynamic_slice x3, local copies, waits for them, and re-layouts, half(): return lax.dynamic_slice_in_dim(x, index * width, width, 1)  2.52 us
    ppermute x3, waiting for transfers between devices, swap(): return lax.ppermute(x, 'head', [(0, 1), (1, 0)])  1.39 us
  transfers between devices with their start and end apart: 9, of which 6 were waited for; matrix products, arithmetic and copies ran while one was open for 5% of the time, Pallas kernels for 16%

profile of v2, /device:TPU:0, one launch (start us, length us, event | category | flops | bytes accessed | tf_op | source)
XLA Modules:
  0.0 47.3 jit_solution(15436015568437531138)
XLA Ops:
  0.6 0.8 %constant_dynamic-slice_fusion.2 = (bf16[128,128]{1,0:T(8,128)(2,1)S(1)}, bf16[128,128]{1,0:T(8,128)(2,1)S(1)}, bf16[128,128]{1,0:T(8,128)(2,1)S(1)}, bf16[128,128]{1,0:T(8,128)(2,1)S(1)}) fusion(bf16[128,256]{1,0:T(8,128)(2,1)} %param.7, s32[]{:T(128)S(6)} %select_n.13, s32[]{:T(128)S(6)} %select_n.14, bf16[128,256]{1,0:T(8,128)(2,1)} %param.6), kind=kLoop, calls=%fused_computation.4 | loop fusion | bytes 262152 | tf_op jit(solution)/shard_map/dynamic_slice | solution.py:271
  1.5 0.0 copy-start.10
  1.5 3.0 %collective-permute-start.2 = (bf16[128,256]{1,0:T(8,128)(2,1)S(1)}, bf16[128,256]{1,0:T(8,128)(2,1)S(1)}, u32[]{:S(2)}, u32[]{:S(2)}) collective-permute-start(bf16[128,256]{1,0:T(8,128)(2,1)S(1)} %pad_maximum_fusion.1), channel_id=1, source_target_pairs={{0,1},{1,0},{2,3},{3,2},{4,5},{5,4},{6,7},{7,6},{8,9},{9,8},{10,11... | collective-permute-start | bytes 196616 | tf_op jit(solution)/shard_map/ppermute | solution.py:277
  4.5 1.0 %constant_dynamic-slice_fusion.4 = bf16[128,1024]{1,0:T(8,128)(2,1)S(1)} fusion(bf16[128,2048]{1,0:T(8,128)(2,1)} %do_hbm.1, s32[]{:T(128)S(6)} %select_n.12), kind=kLoop, calls=%fused_computation.6 | loop fusion | bytes 524292 | tf_op jit(solution)/shard_map/dynamic_slice | solution.py:271
  5.5 0.1 collective-permute-start.1
  5.6 1.4 %collective-permute-done.2 = bf16[128,256]{1,0:T(8,128)(2,1)S(1)} collective-permute-done((bf16[128,256]{1,0:T(8,128)(2,1)S(1)}, bf16[128,256]{1,0:T(8,128)(2,1)S(1)}, u32[]{:S(2)}, u32[]{:S(2)}) %collective-permute-start.2) | collective-permute-done | bytes 65568 | tf_op jit(solution)/shard_map/ppermute | solution.py:277
  7.0 0.2 collective-permute-start.5
  7.2 1.8 %collective-permute-start.4 = (bf16[256,256]{1,0:T(8,128)(2,1)S(1)}, bf16[256,256]{1,0:T(8,128)(2,1)S(1)}, u32[]{:S(2)}, u32[]{:S(2)}) collective-permute-start(bf16[256,256]{1,0:T(8,128)(2,1)S(1)} %pad_maximum_fusion.refs_0_), channel_id=1, source_target_pairs={{0,4},{2,6},{4,8},{6,10},{8,12},{10,14},{12,16},{14,18},{16,20},{1... | collective-permute-start | bytes 393224 | tf_op jit(solution)/shard_map/ppermute | solution.py:253
  9.0 1.3 %collective-permute-start.3 = (bf16[256,256]{1,0:T(8,128)(2,1)S(1)}, bf16[256,256]{1,0:T(8,128)(2,1)S(1)}, u32[]{:S(2)}, u32[]{:S(2)}) collective-permute-start(bf16[256,256]{1,0:T(8,128)(2,1)S(1)} %pad_maximum_fusion.refs_0_), channel_id=1, source_target_pairs={{0,2},{2,4},{4,6},{6,8},{8,10},{10,12},{12,14},{14,16},{16,18},{18... | collective-permute-start | bytes 393224 | tf_op jit(solution)/shard_map/ppermute | solution.py:253
  10.3 0.0 copy-done.10
  10.3 0.7 %constant_dynamic-slice_fusion.5 = bf16[128,1024]{1,0:T(8,128)(2,1)} fusion(bf16[128,2048]{1,0:T(8,128)(2,1)S(1)} %copy-done.10, s32[]{:T(128)S(6)} %select_n.12), kind=kLoop, calls=%fused_computation.7 | loop fusion | bytes 524292 | tf_op jit(solution)/shard_map/dynamic_slice | solution.py:271
  11.0 2.0 %collective-permute-start = (bf16[128,1024]{1,0:T(8,128)(2,1)}, bf16[128,1024]{1,0:T(8,128)(2,1)S(1)}, u32[]{:S(2)}, u32[]{:S(2)}) collective-permute-start(bf16[128,1024]{1,0:T(8,128)(2,1)} %constant_dynamic-slice_fusion.5), channel_id=1, source_target_pairs={{0,1},{1,0},{2,3},{3,2},{4,5},{5,4},{6,7},{7,6},{8,9},{9,8},{10,11... | collective-permute-start | bytes 786440 | tf_op jit(solution)/shard_map/ppermute | solution.py:277
  13.1 0.0 copy-start.11
  13.1 0.7 %copy-done.11 = s32[32]{0:T(128)S(1)} copy-done((s32[32]{0:T(128)S(1)}, s32[32]{0:T(128)}, u32[]{:S(2)}) %copy-start.11) | copy-done | bytes 152
  13.7 0.6 %pad_add_fusion.info = s32[34]{0:T(128)} fusion(s32[32]{0:T(128)S(1)} %copy-done.11, s32[1]{0:T(128)} %bitcast.1, s32[1]{0:T(128)} %bitcast), kind=kLoop, calls=%fused_computation.8 | loop fusion | flops 68 | bytes 272 | tf_op jit(solution)/shard_map/concatenate | solution.py:263
  14.3 0.8 %masks.1 = (f32[896,128]{1,0:T(8,128)S(1)}, f32[896,128]{1,0:T(8,128)S(1)}) custom-call(s32[34]{0:T(128)} %pad_add_fusion.info), custom_call_target="tpu_custom_call" | custom-call | tf_op jit(solution)/shard_map/masks/pallas_call | solution.py:179
  15.2 0.0 copy-start.8
  15.2 0.0 collective-permute-done.5.refs_3_
  15.2 3.9 %collective-permute-done.4.refs_2_ = bf16[256,256]{1,0:T(8,128)(2,1)S(1)} collective-permute-done((bf16[256,256]{1,0:T(8,128)(2,1)S(1)}, bf16[256,256]{1,0:T(8,128)(2,1)S(1)}, u32[]{:S(2)}, u32[]{:S(2)}) %collective-permute-start.4) | collective-permute-done | bytes 131104 | tf_op jit(solution)/shard_map/ppermute | solution.py:253
  19.1 0.0 copy-start.4
  19.1 1.0 %collective-permute-done.3.refs_1_ = bf16[256,256]{1,0:T(8,128)(2,1)S(1)} collective-permute-done((bf16[256,256]{1,0:T(8,128)(2,1)S(1)}, bf16[256,256]{1,0:T(8,128)(2,1)S(1)}, u32[]{:S(2)}, u32[]{:S(2)}) %collective-permute-start.3) | collective-permute-done | bytes 131104 | tf_op jit(solution)/shard_map/ppermute | solution.py:253
  20.1 0.0 copy-start.6
  20.1 6.6 %attend_first.1 = (bf16[256,1024]{1,0:T(8,128)(2,1)}, bf16[256,1024]{1,0:T(8,128)(2,1)}, f32[1024,256]{1,0:T(8,128)S(1)}) custom-call(s32[34]{0:T(128)} %pad_add_fusion.info, bf16[128,2048]{1,0:T(8,128)(2,1)} %q_hbm.1, bf16[128,2048]{1,0:T(8,128)(2,1)} %do_hbm.1, f32[896,128]{1,0:T(8,128)S(1)} %get-tuple-element.18.bias_ref, ...), custom_call_target="tpu_custom_call" | custom-call | flops 1409286144 | bytes 2097152 | tf_op jit(solution)/shard_map/attend_first/pallas_call | solution.py:213
  26.8 0.0 copy-done.8
  26.8 0.0 copy-done.4
  26.8 0.0 copy-done.6
  26.8 0.0 collective-permute-done.1.do_hbm
  26.8 0.0 copy-start
  26.8 0.7 %copy-done = bf16[128,1024]{1,0:T(8,128)(2,1)} copy-done((bf16[128,1024]{1,0:T(8,128)(2,1)}, bf16[128,1024]{1,0:T(8,128)(2,1)S(1)}, u32[]{:S(2)}) %copy-start) | copy-done | bytes 262168
  27.5 0.0 collective-permute-done.q_hbm
  27.5 0.0 copy-start.2
  27.5 0.7 %copy-done.2 = bf16[128,1024]{1,0:T(8,128)(2,1)} copy-done((bf16[128,1024]{1,0:T(8,128)(2,1)}, bf16[128,1024]{1,0:T(8,128)(2,1)S(1)}, u32[]{:S(2)}) %copy-start.2) | copy-done | bytes 262168
  28.2 0.0 copy-start.1
  28.2 0.9 %copy-done.1 = bf16[128,1024]{1,0:T(8,128)(2,1)S(1)} copy-done((bf16[128,1024]{1,0:T(8,128)(2,1)S(1)}, bf16[128,1024]{1,0:T(8,128)(2,1)}, u32[]{:S(2)}) %copy-start.1) | copy-done | bytes 262168
  29.2 0.0 copy-start.3
  29.2 0.9 %copy-done.3 = bf16[128,1024]{1,0:T(8,128)(2,1)S(1)} copy-done((bf16[128,1024]{1,0:T(8,128)(2,1)S(1)}, bf16[128,1024]{1,0:T(8,128)(2,1)}, u32[]{:S(2)}) %copy-start.3) | copy-done | bytes 262168
  30.1 0.0 copy-start.5
  30.1 0.9 %copy-done.5 = bf16[256,256]{1,0:T(8,128)(2,1)S(1)} copy-done((bf16[256,256]{1,0:T(8,128)(2,1)S(1)}, bf16[256,256]{1,0:T(8,128)(2,1)}, u32[]{:S(2)}) %copy-start.5) | copy-done | bytes 131096
  31.0 0.9 %copy-done.7 = bf16[256,256]{1,0:T(8,128)(2,1)S(1)} copy-done((bf16[256,256]{1,0:T(8,128)(2,1)S(1)}, bf16[256,256]{1,0:T(8,128)(2,1)}, u32[]{:S(2)}) %copy-start.7) | copy-done | bytes 131096
  31.9 1.0 %copy-done.9 = f32[896,128]{1,0:T(8,128)S(1)} copy-done((f32[896,128]{1,0:T(8,128)S(1)}, f32[896,128]{1,0:T(8,128)}, u32[]{:S(2)}) %copy-start.9) | copy-done | bytes 458776
  32.9 5.7 %attend_last.1 = (bf16[256,1024]{1,0:T(8,128)(2,1)}, bf16[256,1024]{1,0:T(8,128)(2,1)}, f32[256,256]{1,0:T(8,128)S(1)}, bf16[256,256]{1,0:T(8,128)(2,1)S(1)}, bf...) custom-call(s32[34]{0:T(128)} %pad_add_fusion.info, ...), custom_call_target="tpu_custom_call", output_to_operand_aliasing={{0}: (9, {}), {1}: (10, {})} | custom-call | flops 1409286144 | bytes 2097152 | tf_op jit(solution)/shard_map/attend_last/pallas_call | solution.py:213
  38.7 0.1 collective-permute-start.6
  38.7 0.3 collective-permute-start.7
  39.0 0.6 %collective-permute-start.8 = (bf16[256,256]{1,0:T(8,128)(2,1)S(1)}, bf16[256,256]{1,0:T(8,128)(2,1)S(1)}, u32[]{:S(2)}, u32[]{:S(2)}) collective-permute-start(bf16[256,256]{1,0:T(8,128)(2,1)S(1)} %get-tuple-element.27), channel_id=1, source_target_pairs={{0,26},{2,28},{4,30},{6,0},{8,2},{10,4},{12,6},{14,8},{16,10},{18,... | collective-permute-start | bytes 393224 | tf_op jit(solution)/shard_map/ppermute | solution.py:253
  39.7 3.0 %collective-permute-done.6.refs_0_ = bf16[256,256]{1,0:T(8,128)(2,1)S(1)} collective-permute-done((bf16[256,256]{1,0:T(8,128)(2,1)S(1)}, bf16[256,256]{1,0:T(8,128)(2,1)S(1)}, u32[]{:S(2)}, u32[]{:S(2)}) %collective-permute-start.6) | collective-permute-done | bytes 131104 | tf_op jit(solution)/shard_map/ppermute | solution.py:253
  42.6 2.6 %collective-permute-done.7.refs_1_ = bf16[256,256]{1,0:T(8,128)(2,1)S(1)} collective-permute-done((bf16[256,256]{1,0:T(8,128)(2,1)S(1)}, bf16[256,256]{1,0:T(8,128)(2,1)S(1)}, u32[]{:S(2)}, u32[]{:S(2)}) %collective-permute-start.7) | collective-permute-done | bytes 131104 | tf_op jit(solution)/shard_map/ppermute | solution.py:253
  45.3 1.4 %collective-permute-done.8.refs_2_ = bf16[256,256]{1,0:T(8,128)(2,1)S(1)} collective-permute-done((bf16[256,256]{1,0:T(8,128)(2,1)S(1)}, bf16[256,256]{1,0:T(8,128)(2,1)S(1)}, u32[]{:S(2)}, u32[]{:S(2)}) %collective-permute-start.8) | collective-permute-done | bytes 131104 | tf_op jit(solution)/shard_map/ppermute | solution.py:253
  46.7 0.7 %gather.1 = (bf16[256,128]{1,0:T(8,128)(2,1)}, bf16[256,128]{1,0:T(8,128)(2,1)}) custom-call(f32[256,256]{1,0:T(8,128)S(1)} %get-tuple-element.24.own_ref, bf16[256,256]{1,0:T(8,128)(2,1)S(1)} %collective-permute-done.6.refs_0_, bf16[256,256]{1,0:T(8,128)(2,1)S(1)} %collective-permute-done.7.refs_1_, bf16[256,256]{1,0:T(8,128)(2,1)S(1)} %collective-permute-done.8.refs_2_), custom_call_target="tpu_custom_call" | custom-call | tf_op jit(solution)/shard_map/gather/pallas_call | solution.py:291
  (4 shorter events, 0.0 us)
Async XLA Ops:
  1.5 8.8 %copy-start.10 = (bf16[128,2048]{1,0:T(8,128)(2,1)S(1)}, bf16[128,2048]{1,0:T(8,128)(2,1)}, u32[]{:S(2)}) copy-start(bf16[128,2048]{1,0:T(8,128)(2,1)} %q_hbm.1) | copy-start | bytes 1572868
  1.5 5.5 %collective-permute-start.2 = (bf16[128,256]{1,0:T(8,128)(2,1)S(1)}, bf16[128,256]{1,0:T(8,128)(2,1)S(1)}, u32[]{:S(2)}, u32[]{:S(2)}) collective-permute-start(bf16[128,256]{1,0:T(8,128)(2,1)S(1)} %pad_maximum_fusion.1), channel_id=1, source_target_pairs={{0,1},{1,0},{2,3},{3,2},{4,5},{5,4},{6,7},{7,6},{8,9},{9,8},{10,11... | collective-permute-start | bytes 196616 | tf_op jit(solution)/shard_map/ppermute | solution.py:277
  5.5 21.3 %collective-permute-start.1 = (bf16[128,1024]{1,0:T(8,128)(2,1)S(1)}, bf16[128,1024]{1,0:T(8,128)(2,1)S(1)}, u32[]{:S(2)}, u32[]{:S(2)}) collective-permute-start(bf16[128,1024]{1,0:T(8,128)(2,1)S(1)} %constant_dynamic-slice_fusion.4), channel_id=1, source_target_pairs={{0,1},{1,0},{2,3},{3,2},{4,5},{5,4},{6,7},{7,6},{8,9},{9,8},{10,11... | collective-permute-start | bytes 786440 | tf_op jit(solution)/shard_map/ppermute | solution.py:277
  7.0 8.2 %collective-permute-start.5 = (bf16[256,256]{1,0:T(8,128)(2,1)S(1)}, bf16[256,256]{1,0:T(8,128)(2,1)S(1)}, u32[]{:S(2)}, u32[]{:S(2)}) collective-permute-start(bf16[256,256]{1,0:T(8,128)(2,1)S(1)} %pad_maximum_fusion.refs_0_), channel_id=1, source_target_pairs={{0,6},{2,8},{4,10},{6,12},{8,14},{10,16},{12,18},{14,20},{16,22},{... | collective-permute-start | bytes 393224 | tf_op jit(solution)/shard_map/ppermute | solution.py:253
  7.2 11.9 %collective-permute-start.4 = (bf16[256,256]{1,0:T(8,128)(2,1)S(1)}, bf16[256,256]{1,0:T(8,128)(2,1)S(1)}, u32[]{:S(2)}, u32[]{:S(2)}) collective-permute-start(bf16[256,256]{1,0:T(8,128)(2,1)S(1)} %pad_maximum_fusion.refs_0_), channel_id=1, source_target_pairs={{0,4},{2,6},{4,8},{6,10},{8,12},{10,14},{12,16},{14,18},{16,20},{1... | collective-permute-start | bytes 393224 | tf_op jit(solution)/shard_map/ppermute | solution.py:253
  9.0 11.2 %collective-permute-start.3 = (bf16[256,256]{1,0:T(8,128)(2,1)S(1)}, bf16[256,256]{1,0:T(8,128)(2,1)S(1)}, u32[]{:S(2)}, u32[]{:S(2)}) collective-permute-start(bf16[256,256]{1,0:T(8,128)(2,1)S(1)} %pad_maximum_fusion.refs_0_), channel_id=1, source_target_pairs={{0,2},{2,4},{4,6},{6,8},{8,10},{10,12},{12,14},{14,16},{16,18},{18... | collective-permute-start | bytes 393224 | tf_op jit(solution)/shard_map/ppermute | solution.py:253
  11.0 16.5 %collective-permute-start = (bf16[128,1024]{1,0:T(8,128)(2,1)}, bf16[128,1024]{1,0:T(8,128)(2,1)S(1)}, u32[]{:S(2)}, u32[]{:S(2)}) collective-permute-start(bf16[128,1024]{1,0:T(8,128)(2,1)} %constant_dynamic-slice_fusion.5), channel_id=1, source_target_pairs={{0,1},{1,0},{2,3},{3,2},{4,5},{5,4},{6,7},{7,6},{8,9},{9,8},{10,11... | collective-permute-start | bytes 786440 | tf_op jit(solution)/shard_map/ppermute | solution.py:277
  13.1 0.7 %copy-start.11 = (s32[32]{0:T(128)S(1)}, s32[32]{0:T(128)}, u32[]{:S(2)}) copy-start(s32[32]{0:T(128)} %param.9) | copy-start | bytes 388
  15.2 11.6 %copy-start.8 = (f32[896,128]{1,0:T(8,128)}, f32[896,128]{1,0:T(8,128)S(1)}, u32[]{:S(2)}) copy-start(f32[896,128]{1,0:T(8,128)S(1)} %get-tuple-element.17.bias_ref) | copy-start | bytes 1376260
  19.1 7.7 %copy-start.4 = (bf16[256,256]{1,0:T(8,128)(2,1)}, bf16[256,256]{1,0:T(8,128)(2,1)S(1)}, u32[]{:S(2)}) copy-start(bf16[256,256]{1,0:T(8,128)(2,1)S(1)} %collective-permute-done.4.refs_2_) | copy-start | bytes 393220
  20.1 6.7 %copy-start.6 = (bf16[256,256]{1,0:T(8,128)(2,1)}, bf16[256,256]{1,0:T(8,128)(2,1)S(1)}, u32[]{:S(2)}) copy-start(bf16[256,256]{1,0:T(8,128)(2,1)S(1)} %collective-permute-done.3.refs_1_) | copy-start | bytes 393220
  26.8 0.7 %copy-start = (bf16[128,1024]{1,0:T(8,128)(2,1)}, bf16[128,1024]{1,0:T(8,128)(2,1)S(1)}, u32[]{:S(2)}) copy-start(bf16[128,1024]{1,0:T(8,128)(2,1)S(1)} %collective-permute-done.1.do_hbm) | copy-start | bytes 786436
  27.5 0.7 %copy-start.2 = (bf16[128,1024]{1,0:T(8,128)(2,1)}, bf16[128,1024]{1,0:T(8,128)(2,1)S(1)}, u32[]{:S(2)}) copy-start(bf16[128,1024]{1,0:T(8,128)(2,1)S(1)} %collective-permute-done.q_hbm) | copy-start | bytes 786436
  28.2 0.9 %copy-start.1 = (bf16[128,1024]{1,0:T(8,128)(2,1)S(1)}, bf16[128,1024]{1,0:T(8,128)(2,1)}, u32[]{:S(2)}) copy-start(bf16[128,1024]{1,0:T(8,128)(2,1)} %copy-done) | copy-start | bytes 786436
  29.2 0.9 %copy-start.3 = (bf16[128,1024]{1,0:T(8,128)(2,1)S(1)}, bf16[128,1024]{1,0:T(8,128)(2,1)}, u32[]{:S(2)}) copy-start(bf16[128,1024]{1,0:T(8,128)(2,1)} %copy-done.2) | copy-start | bytes 786436
  30.1 0.9 %copy-start.5 = (bf16[256,256]{1,0:T(8,128)(2,1)S(1)}, bf16[256,256]{1,0:T(8,128)(2,1)}, u32[]{:S(2)}) copy-start(bf16[256,256]{1,0:T(8,128)(2,1)} %copy-done.4) | copy-start | bytes 393220
  31.0 0.9 %copy-start.7 = (bf16[256,256]{1,0:T(8,128)(2,1)S(1)}, bf16[256,256]{1,0:T(8,128)(2,1)}, u32[]{:S(2)}) copy-start(bf16[256,256]{1,0:T(8,128)(2,1)} %copy-done.6) | copy-start | bytes 393220
  31.9 1.0 %copy-start.9 = (f32[896,128]{1,0:T(8,128)S(1)}, f32[896,128]{1,0:T(8,128)}, u32[]{:S(2)}) copy-start(f32[896,128]{1,0:T(8,128)} %copy-done.8) | copy-start | bytes 1376260
  38.7 3.9 %collective-permute-start.6 = (bf16[256,256]{1,0:T(8,128)(2,1)S(1)}, bf16[256,256]{1,0:T(8,128)(2,1)S(1)}, u32[]{:S(2)}, u32[]{:S(2)}) collective-permute-start(bf16[256,256]{1,0:T(8,128)(2,1)S(1)} %get-tuple-element.25), channel_id=1, source_target_pairs={{0,30},{2,0},{4,2},{6,4},{8,6},{10,8},{12,10},{14,12},{16,14},{18,... | collective-permute-start | bytes 393224 | tf_op jit(solution)/shard_map/ppermute | solution.py:253
  38.7 6.5 %collective-permute-start.7 = (bf16[256,256]{1,0:T(8,128)(2,1)S(1)}, bf16[256,256]{1,0:T(8,128)(2,1)S(1)}, u32[]{:S(2)}, u32[]{:S(2)}) collective-permute-start(bf16[256,256]{1,0:T(8,128)(2,1)S(1)} %get-tuple-element.26), channel_id=1, source_target_pairs={{0,28},{2,30},{4,0},{6,2},{8,4},{10,6},{12,8},{14,10},{16,12},{18,... | collective-permute-start | bytes 393224 | tf_op jit(solution)/shard_map/ppermute | solution.py:253
  39.0 7.6 %collective-permute-start.8 = (bf16[256,256]{1,0:T(8,128)(2,1)S(1)}, bf16[256,256]{1,0:T(8,128)(2,1)S(1)}, u32[]{:S(2)}, u32[]{:S(2)}) collective-permute-start(bf16[256,256]{1,0:T(8,128)(2,1)S(1)} %get-tuple-element.27), channel_id=1, source_target_pairs={{0,26},{2,28},{4,30},{6,0},{8,2},{10,4},{12,6},{14,8},{16,10},{18,... | collective-permute-start | bytes 393224 | tf_op jit(solution)/shard_map/ppermute | solution.py:253

commit v3 on v2

--- a/solution.py
+++ b/solution.py
@@ -181,6 +181,7 @@
         out_shape=[pltpu.VMEM((lead + rows, rows), jnp.float32)] * tiles,
         in_specs=[SCALARS],
         out_specs=[WHOLE] * tiles,
+        compiler_params=pltpu.CompilerParams(vmem_limit_bytes=4 << 20),
         name="masks",
     )(info)
 
@@ -232,6 +233,7 @@
             pltpu.SemaphoreType.DMA((2 + 2 * (heads // HEADS),)),
         ],
         input_output_aliases=aliases,
+        compiler_params=pltpu.CompilerParams(vmem_limit_bytes=24 << 20),
         cost_estimate=pl.CostEstimate(
             flops=12 * keys * rows * columns, transcendentals=keys * rows * heads, bytes_accessed=1 << 21
         ),
@@ -293,6 +295,7 @@
         out_shape=[jax.ShapeDtypeStruct((shard, hd), jnp.bfloat16)] * 2,
         in_specs=[WHOLE] * WIN,
         out_specs=[WHOLE] * 2,
+        compiler_params=pltpu.CompilerParams(vmem_limit_bytes=4 << 20),
         name="gather",
     )(*in_vmem(total, *near))
     return out, dq, grad_keys, grad_values

time: 47.8 us -> 40.3 us (0.84)
  local copies, waits for them, and re-layouts: 9.3 us -> 2.48 us
  waiting for transfers between devices: 13.3 us -> 14.6 us
  Pallas kernels: 13.9 us -> 12.7 us
  other arithmetic: 0.63 us -> 0.1 us
    unnamed x24 -> x6, local copies, waits for them, and re-layouts: 6.78 us -> 0.67 us
    ppermute x6, waiting for transfers between devices: 11.9 us -> 13.2 us  [ring(): lax.ppermute(value, axis, [(i, (i + steps) % count) for i in range(count)])]
    pallas_call x2, Pallas kernels: 12.3 us -> 11.3 us  [attend(): pl.pallas_call(functools.partial(attend_kernel, tiles, index), out_shape=...]
    dynamic_slice x3, local copies, waits for them, and re-layouts: 2.52 us -> 1.81 us  [half(): return lax.dynamic_slice_in_dim(x, index * width, width, 1)]
    concatenate x1, other arithmetic: 0.6 us -> 0.08 us  [body(): jnp.concatenate([jnp.stack([lax.axis_index('ctx'), head]).astype(jnp.int3...]
  transfers between devices with their start and end apart: 9 -> 9, of which waited for: 6 -> 6; matrix products, arithmetic and copies ran while one was open for 5% -> 3% of each run, Pallas kernels for 16% -> 16%
where the time goes in v3:
time: 40.3 us; the launch traced here: 40.1 us
  waiting for transfers between devices  14.6 us (36%)
  Pallas kernels  12.7 us (32%)
  starting transfers between devices  9.5 us (24%)
  local copies, waits for them, and re-layouts  2.48 us (6%)
  between operations  0.74 us (2%)
    ppermute x6, waiting for transfers between devices, ring(): lax.ppermute(value, axis, [(i, (i + steps) % count) for i in range(count)])  13.2 us
    pallas_call x2, Pallas kernels, attend(): pl.pallas_call(functools.partial(attend_kernel, tiles, index), out_shape=...  11.3 us
    ppermute x3, starting transfers between devices, swap(): return lax.ppermute(x, 'head', [(0, 1), (1, 0)])  5.25 us
    ppermute x6, starting transfers between devices, ring(): lax.ppermute(value, axis, [(i, (i + steps) % count) for i in range(count)])  4.25 us
    dynamic_slice x3, local copies, waits for them, and re-layouts, half(): return lax.dynamic_slice_in_dim(x, index * width, width, 1)  1.81 us
    ppermute x3, waiting for transfers between devices, swap(): return lax.ppermute(x, 'head', [(0, 1), (1, 0)])  1.38 us
  transfers between devices with their start and end apart: 9, of which 6 were waited for; matrix products, arithmetic and copies ran while one was open for 3% of the time, Pallas kernels for 16%

profile of v3, /device:TPU:0, one launch (start us, length us, event | category | flops | bytes accessed | tf_op | source)
XLA Modules:
  0.0 40.1 jit_solution(7735234243190201892)
XLA Ops:
  0.6 0.8 %constant_dynamic-slice_fusion.2 = (bf16[128,128]{1,0:T(8,128)(2,1)S(1)}, bf16[128,128]{1,0:T(8,128)(2,1)S(1)}, bf16[128,128]{1,0:T(8,128)(2,1)S(1)}, bf16[128,128]{1,0:T(8,128)(2,1)S(1)}) fusion(bf16[128,256]{1,0:T(8,128)(2,1)} %param.7, s32[]{:T(128)S(6)} %select_n.13, s32[]{:T(128)S(6)} %select_n.14, bf16[128,256]{1,0:T(8,128)(2,1)} %param.6), kind=kLoop, calls=%fused_computation.4 | loop fusion | bytes 262152 | tf_op jit(solution)/shard_map/dynamic_slice | solution.py:273
  1.5 0.0 copy-start
  1.5 3.0 %collective-permute-start.2 = (bf16[128,256]{1,0:T(8,128)(2,1)S(1)}, bf16[128,256]{1,0:T(8,128)(2,1)S(1)}, u32[]{:S(2)}, u32[]{:S(2)}) collective-permute-start(bf16[128,256]{1,0:T(8,128)(2,1)S(1)} %pad_maximum_fusion.1), channel_id=1, source_target_pairs={{0,1},{1,0},{2,3},{3,2},{4,5},{5,4},{6,7},{7,6},{8,9},{9,8},{10,11... | collective-permute-start | bytes 196616 | tf_op jit(solution)/shard_map/ppermute | solution.py:279
  4.5 1.0 %constant_dynamic-slice_fusion.4 = bf16[128,1024]{1,0:T(8,128)(2,1)S(1)} fusion(bf16[128,2048]{1,0:T(8,128)(2,1)} %do_hbm.1, s32[]{:T(128)S(6)} %select_n.12), kind=kLoop, calls=%fused_computation.6 | loop fusion | bytes 524292 | tf_op jit(solution)/shard_map/dynamic_slice | solution.py:273
  5.5 0.0 copy-start.1
  5.5 0.1 collective-permute-start.1
  5.6 1.4 %collective-permute-done.2 = bf16[128,256]{1,0:T(8,128)(2,1)S(1)} collective-permute-done((bf16[128,256]{1,0:T(8,128)(2,1)S(1)}, bf16[128,256]{1,0:T(8,128)(2,1)S(1)}, u32[]{:S(2)}, u32[]{:S(2)}) %collective-permute-start.2) | collective-permute-done | bytes 65568 | tf_op jit(solution)/shard_map/ppermute | solution.py:279
  7.0 0.2 collective-permute-start.5
  7.2 1.8 %collective-permute-start.4 = (bf16[256,256]{1,0:T(8,128)(2,1)S(1)}, bf16[256,256]{1,0:T(8,128)(2,1)S(1)}, u32[]{:S(2)}, u32[]{:S(2)}) collective-permute-start(bf16[256,256]{1,0:T(8,128)(2,1)S(1)} %pad_maximum_fusion.refs_0_), channel_id=1, source_target_pairs={{0,4},{2,6},{4,8},{6,10},{8,12},{10,14},{12,16},{14,18},{16,20},{1... | collective-permute-start | bytes 393224 | tf_op jit(solution)/shard_map/ppermute | solution.py:255
  9.0 1.3 %collective-permute-start.3 = (bf16[256,256]{1,0:T(8,128)(2,1)S(1)}, bf16[256,256]{1,0:T(8,128)(2,1)S(1)}, u32[]{:S(2)}, u32[]{:S(2)}) collective-permute-start(bf16[256,256]{1,0:T(8,128)(2,1)S(1)} %pad_maximum_fusion.refs_0_), channel_id=1, source_target_pairs={{0,2},{2,4},{4,6},{6,8},{8,10},{10,12},{12,14},{14,16},{16,18},{18... | collective-permute-start | bytes 393224 | tf_op jit(solution)/shard_map/ppermute | solution.py:255
  10.3 0.0 copy-done
  10.3 2.1 %collective-permute-start = (bf16[128,1024]{1,0:T(8,128)(2,1)S(1)}, bf16[128,1024]{1,0:T(8,128)(2,1)S(1)}, u32[]{:S(2)}, u32[]{:S(2)}) collective-permute-start(bf16[128,1024]{1,0:T(8,128)(2,1)S(1)} %constant_dynamic-slice_fusion.5), channel_id=1, source_target_pairs={{0,1},{1,0},{2,3},{3,2},{4,5},{5,4},{6,7},{7,6},{8,9},{9,8},{10,11... | collective-permute-start | bytes 786440 | tf_op jit(solution)/shard_map/ppermute | solution.py:279
  12.4 0.0 copy-start.2
  12.4 0.7 %copy-done.2 = s32[32]{0:T(128)S(1)} copy-done((s32[32]{0:T(128)S(1)}, s32[32]{0:T(128)}, u32[]{:S(2)}) %copy-start.2) | copy-done | bytes 152
  13.1 0.1 pad_add_fusion.info
  13.2 0.7 %masks.1 = (f32[896,128]{1,0:T(8,128)S(1)}, f32[896,128]{1,0:T(8,128)S(1)}) custom-call(s32[34]{0:T(128)S(1)} %pad_add_fusion.info), custom_call_target="tpu_custom_call" | custom-call | tf_op jit(solution)/shard_map/masks/pallas_call | solution.py:179
  13.9 0.0 collective-permute-done.5.refs_3_
  13.9 5.2 %collective-permute-done.4.refs_2_ = bf16[256,256]{1,0:T(8,128)(2,1)S(1)} collective-permute-done((bf16[256,256]{1,0:T(8,128)(2,1)S(1)}, bf16[256,256]{1,0:T(8,128)(2,1)S(1)}, u32[]{:S(2)}, u32[]{:S(2)}) %collective-permute-start.4) | collective-permute-done | bytes 131104 | tf_op jit(solution)/shard_map/ppermute | solution.py:255
  19.1 1.0 %collective-permute-done.3.refs_1_ = bf16[256,256]{1,0:T(8,128)(2,1)S(1)} collective-permute-done((bf16[256,256]{1,0:T(8,128)(2,1)S(1)}, bf16[256,256]{1,0:T(8,128)(2,1)S(1)}, u32[]{:S(2)}, u32[]{:S(2)}) %collective-permute-start.3) | collective-permute-done | bytes 131104 | tf_op jit(solution)/shard_map/ppermute | solution.py:255
  20.1 0.0 copy-done.1
  20.1 5.5 %attend_first.1 = (bf16[256,1024]{1,0:T(8,128)(2,1)}, bf16[256,1024]{1,0:T(8,128)(2,1)}, f32[1024,256]{1,0:T(8,128)S(1)}) custom-call(s32[34]{0:T(128)S(1)} %pad_add_fusion.info, bf16[128,2048]{1,0:T(8,128)(2,1)S(1)} %copy-done, bf16[128,2048]{1,0:T(8,128)(2,1)S(1)} %copy-done.1, f32[896,128]{1,0:T(8,128)S(1)} %get-tuple-element.18.bias_ref, ...), custom_call_target="tpu_custom_call" | custom-call | flops 1409286144 | bytes 2097152 | tf_op jit(solution)/shard_map/attend_first/pallas_call | solution.py:214
  25.7 0.0 collective-permute-done.1.do_hbm
  25.7 0.0 collective-permute-done.q_hbm
  25.7 5.7 %attend_last.1 = (bf16[256,1024]{1,0:T(8,128)(2,1)}, bf16[256,1024]{1,0:T(8,128)(2,1)}, f32[256,256]{1,0:T(8,128)S(1)}, bf16[256,256]{1,0:T(8,128)(2,1)S(1)}, bf...) custom-call(s32[34]{0:T(128)S(1)} %pad_add_fusion.info, ...), custom_call_target="tpu_custom_call", output_to_operand_aliasing={{0}: (9, {}), {1}: (10, {})} | custom-call | flops 1409286144 | bytes 2097152 | tf_op jit(solution)/shard_map/attend_last/pallas_call | solution.py:214
  31.4 0.1 collective-permute-start.6
  31.5 0.3 collective-permute-start.7
  31.8 0.6 %collective-permute-start.8 = (bf16[256,256]{1,0:T(8,128)(2,1)S(1)}, bf16[256,256]{1,0:T(8,128)(2,1)S(1)}, u32[]{:S(2)}, u32[]{:S(2)}) collective-permute-start(bf16[256,256]{1,0:T(8,128)(2,1)S(1)} %get-tuple-element.27), channel_id=1, source_target_pairs={{0,26},{2,28},{4,30},{6,0},{8,2},{10,4},{12,6},{14,8},{16,10},{18,... | collective-permute-start | bytes 393224 | tf_op jit(solution)/shard_map/ppermute | solution.py:255
  32.4 3.0 %collective-permute-done.6.refs_0_ = bf16[256,256]{1,0:T(8,128)(2,1)S(1)} collective-permute-done((bf16[256,256]{1,0:T(8,128)(2,1)S(1)}, bf16[256,256]{1,0:T(8,128)(2,1)S(1)}, u32[]{:S(2)}, u32[]{:S(2)}) %collective-permute-start.6) | collective-permute-done | bytes 131104 | tf_op jit(solution)/shard_map/ppermute | solution.py:255
  35.4 2.6 %collective-permute-done.7.refs_1_ = bf16[256,256]{1,0:T(8,128)(2,1)S(1)} collective-permute-done((bf16[256,256]{1,0:T(8,128)(2,1)S(1)}, bf16[256,256]{1,0:T(8,128)(2,1)S(1)}, u32[]{:S(2)}, u32[]{:S(2)}) %collective-permute-start.7) | collective-permute-done | bytes 131104 | tf_op jit(solution)/shard_map/ppermute | solution.py:255
  38.0 1.4 %collective-permute-done.8.refs_2_ = bf16[256,256]{1,0:T(8,128)(2,1)S(1)} collective-permute-done((bf16[256,256]{1,0:T(8,128)(2,1)S(1)}, bf16[256,256]{1,0:T(8,128)(2,1)S(1)}, u32[]{:S(2)}, u32[]{:S(2)}) %collective-permute-start.8) | collective-permute-done | bytes 131104 | tf_op jit(solution)/shard_map/ppermute | solution.py:255
  39.4 0.7 %gather.1 = (bf16[256,128]{1,0:T(8,128)(2,1)}, bf16[256,128]{1,0:T(8,128)(2,1)}) custom-call(f32[256,256]{1,0:T(8,128)S(1)} %get-tuple-element.24.own_ref, bf16[256,256]{1,0:T(8,128)(2,1)S(1)} %collective-permute-done.6.refs_0_, bf16[256,256]{1,0:T(8,128)(2,1)S(1)} %collective-permute-done.7.refs_1_, bf16[256,256]{1,0:T(8,128)(2,1)S(1)} %collective-permute-done.8.refs_2_), custom_call_target="tpu_custom_call" | custom-call | tf_op jit(solution)/shard_map/gather/pallas_call | solution.py:293
  (3 shorter events, 0.0 us)
Async XLA Ops:
  1.5 8.8 %copy-start = (bf16[128,2048]{1,0:T(8,128)(2,1)S(1)}, bf16[128,2048]{1,0:T(8,128)(2,1)}, u32[]{:S(2)}) copy-start(bf16[128,2048]{1,0:T(8,128)(2,1)} %q_hbm.1) | copy-start | bytes 1572868
  1.5 5.5 %collective-permute-start.2 = (bf16[128,256]{1,0:T(8,128)(2,1)S(1)}, bf16[128,256]{1,0:T(8,128)(2,1)S(1)}, u32[]{:S(2)}, u32[]{:S(2)}) collective-permute-start(bf16[128,256]{1,0:T(8,128)(2,1)S(1)} %pad_maximum_fusion.1), channel_id=1, source_target_pairs={{0,1},{1,0},{2,3},{3,2},{4,5},{5,4},{6,7},{7,6},{8,9},{9,8},{10,11... | collective-permute-start | bytes 196616 | tf_op jit(solution)/shard_map/ppermute | solution.py:279
  5.5 14.6 %copy-start.1 = (bf16[128,2048]{1,0:T(8,128)(2,1)S(1)}, bf16[128,2048]{1,0:T(8,128)(2,1)}, u32[]{:S(2)}) copy-start(bf16[128,2048]{1,0:T(8,128)(2,1)} %do_hbm.1) | copy-start | bytes 1572868
  5.5 20.2 %collective-permute-start.1 = (bf16[128,1024]{1,0:T(8,128)(2,1)S(1)}, bf16[128,1024]{1,0:T(8,128)(2,1)S(1)}, u32[]{:S(2)}, u32[]{:S(2)}) collective-permute-start(bf16[128,1024]{1,0:T(8,128)(2,1)S(1)} %constant_dynamic-slice_fusion.4), channel_id=1, source_target_pairs={{0,1},{1,0},{2,3},{3,2},{4,5},{5,4},{6,7},{7,6},{8,9},{9,8},{10,11... | collective-permute-start | bytes 786440 | tf_op jit(solution)/shard_map/ppermute | solution.py:279
  7.0 6.9 %collective-permute-start.5 = (bf16[256,256]{1,0:T(8,128)(2,1)S(1)}, bf16[256,256]{1,0:T(8,128)(2,1)S(1)}, u32[]{:S(2)}, u32[]{:S(2)}) collective-permute-start(bf16[256,256]{1,0:T(8,128)(2,1)S(1)} %pad_maximum_fusion.refs_0_), channel_id=1, source_target_pairs={{0,6},{2,8},{4,10},{6,12},{8,14},{10,16},{12,18},{14,20},{16,22},{... | collective-permute-start | bytes 393224 | tf_op jit(solution)/shard_map/ppermute | solution.py:255
  7.2 11.9 %collective-permute-start.4 = (bf16[256,256]{1,0:T(8,128)(2,1)S(1)}, bf16[256,256]{1,0:T(8,128)(2,1)S(1)}, u32[]{:S(2)}, u32[]{:S(2)}) collective-permute-start(bf16[256,256]{1,0:T(8,128)(2,1)S(1)} %pad_maximum_fusion.refs_0_), channel_id=1, source_target_pairs={{0,4},{2,6},{4,8},{6,10},{8,12},{10,14},{12,16},{14,18},{16,20},{1... | collective-permute-start | bytes 393224 | tf_op jit(solution)/shard_map/ppermute | solution.py:255
  9.0 11.2 %collective-permute-start.3 = (bf16[256,256]{1,0:T(8,128)(2,1)S(1)}, bf16[256,256]{1,0:T(8,128)(2,1)S(1)}, u32[]{:S(2)}, u32[]{:S(2)}) collective-permute-start(bf16[256,256]{1,0:T(8,128)(2,1)S(1)} %pad_maximum_fusion.refs_0_), channel_id=1, source_target_pairs={{0,2},{2,4},{4,6},{6,8},{8,10},{10,12},{12,14},{14,16},{16,18},{18... | collective-permute-start | bytes 393224 | tf_op jit(solution)/shard_map/ppermute | solution.py:255
  10.3 15.4 %collective-permute-start = (bf16[128,1024]{1,0:T(8,128)(2,1)S(1)}, bf16[128,1024]{1,0:T(8,128)(2,1)S(1)}, u32[]{:S(2)}, u32[]{:S(2)}) collective-permute-start(bf16[128,1024]{1,0:T(8,128)(2,1)S(1)} %constant_dynamic-slice_fusion.5), channel_id=1, source_target_pairs={{0,1},{1,0},{2,3},{3,2},{4,5},{5,4},{6,7},{7,6},{8,9},{9,8},{10,11... | collective-permute-start | bytes 786440 | tf_op jit(solution)/shard_map/ppermute | solution.py:279
  12.4 0.7 %copy-start.2 = (s32[32]{0:T(128)S(1)}, s32[32]{0:T(128)}, u32[]{:S(2)}) copy-start(s32[32]{0:T(128)} %param.9) | copy-start | bytes 388
  31.4 3.9 %collective-permute-start.6 = (bf16[256,256]{1,0:T(8,128)(2,1)S(1)}, bf16[256,256]{1,0:T(8,128)(2,1)S(1)}, u32[]{:S(2)}, u32[]{:S(2)}) collective-permute-start(bf16[256,256]{1,0:T(8,128)(2,1)S(1)} %get-tuple-element.25), channel_id=1, source_target_pairs={{0,30},{2,0},{4,2},{6,4},{8,6},{10,8},{12,10},{14,12},{16,14},{18,... | collective-permute-start | bytes 393224 | tf_op jit(solution)/shard_map/ppermute | solution.py:255
  31.5 6.5 %collective-permute-start.7 = (bf16[256,256]{1,0:T(8,128)(2,1)S(1)}, bf16[256,256]{1,0:T(8,128)(2,1)S(1)}, u32[]{:S(2)}, u32[]{:S(2)}) collective-permute-start(bf16[256,256]{1,0:T(8,128)(2,1)S(1)} %get-tuple-element.26), channel_id=1, source_target_pairs={{0,28},{2,30},{4,0},{6,2},{8,4},{10,6},{12,8},{14,10},{16,12},{18,... | collective-permute-start | bytes 393224 | tf_op jit(solution)/shard_map/ppermute | solution.py:255
  31.8 7.6 %collective-permute-start.8 = (bf16[256,256]{1,0:T(8,128)(2,1)S(1)}, bf16[256,256]{1,0:T(8,128)(2,1)S(1)}, u32[]{:S(2)}, u32[]{:S(2)}) collective-permute-start(bf16[256,256]{1,0:T(8,128)(2,1)S(1)} %get-tuple-element.27), channel_id=1, source_target_pairs={{0,26},{2,28},{4,30},{6,0},{8,2},{10,4},{12,6},{14,8},{16,10},{18,... | collective-permute-start | bytes 393224 | tf_op jit(solution)/shard_map/ppermute | solution.py:255

commit v4 on v3

--- a/solution.py
+++ b/solution.py
@@ -49,7 +49,10 @@
             bias_ref[b * KEYS : (b + 1) * KEYS, :] = jnp.where(ok, 0.0, MASKED)
 
 
-def attend_kernel(tiles, index, info, q_hbm, do_hbm, bias_ref, *refs):
+def attend_kernel(tiles, index, loaded, info, *refs):
+    sources = refs[: 1 if loaded else 2]
+    bias_ref = refs[len(sources)]
+    refs = refs[len(sources) + 1 :]
     shard_refs = refs[:WIN]
     refs = refs[WIN:]
     last = index == tiles - 1
@@ -65,7 +68,7 @@
     else:
         acc_out = refs[2]
         refs = refs[3:]
-    k_ref, v_ref, kt_ref, vt_ref, q_ref, do_ref, q_rows, do_rows, p_ref, ds_ref, out_ref, dq_ref, acc_ref, sem = refs
+    k_ref, v_ref, kt_ref, vt_ref, q_do, q_rows, do_rows, p_ref, ds_ref, out_ref, dq_ref, acc_ref, sem = refs
 
     shard, width = shard_refs[0].shape
     hd = width // 2
@@ -82,28 +85,29 @@
     scaling = 1 / math.sqrt(hd)
 
     loads = []
-    if q_hbm.shape[1] == columns:
-        q_ref, do_ref = q_hbm, do_hbm
+    if loaded:
+        q_do = sources[0]
     else:
         mine = pl.ds(pl.multiple_of(info[1] * columns, 128), columns)
-        loads = [
-            pltpu.make_async_copy(q_hbm.at[:, mine], q_ref, sem.at[0]),
-            pltpu.make_async_copy(do_hbm.at[:, mine], do_ref, sem.at[1]),
-        ]
+        for i, source in enumerate(sources):
+            target = q_do.at[:, i * columns : (i + 1) * columns]
+            loads.append(pltpu.make_async_copy(source.at[:, mine], target, sem.at[i]))
     for copy in loads:
         copy.start()
     part = shard // tiles
-    for s in range(WIN):
+    odd = info[0] & 1
+    starts = [(WIN - 1) * shard, odd * 2 * shard, shard, (1 - odd) * 2 * shard]
+    for ref, start in zip(shard_refs, starts):
         for j in range(tiles):
-            at = pl.ds(pl.multiple_of((WIN - 1 - s) * shard + (j ^ flip) * part, KEYS), part)
-            k_ref[at, :] = shard_refs[s][j * part : (j + 1) * part, :hd]
-            v_ref[at, :] = shard_refs[s][j * part : (j + 1) * part, hd:]
+            at = pl.ds(pl.multiple_of(start + (j ^ flip) * part, KEYS), part)
+            k_ref[at, :] = ref[j * part : (j + 1) * part, :hd]
+            v_ref[at, :] = ref[j * part : (j + 1) * part, hd:]
     window = pl.ds(base, keys)
     for copy in loads:
         copy.wait()
     for h in range(heads):
-        q_rows[h * rows : (h + 1) * rows, :] = q_ref[:, h * hd : (h + 1) * hd]
-        do_rows[h * rows : (h + 1) * rows, :] = do_ref[:, h * hd : (h + 1) * hd]
+        q_rows[h * rows : (h + 1) * rows, :] = q_do[:, h * hd : (h + 1) * hd]
+        do_rows[h * rows : (h + 1) * rows, :] = q_do[:, columns + h * hd : columns + (h + 1) * hd]
     kt_ref[...] = k_ref[window, :].T
     vt_ref[...] = v_ref[window, :].T
     n = HEADS * rows
@@ -163,12 +167,10 @@
             acc_ref[...] = acc_in[...]
             acc_ref[window, :hd] += dk
             acc_ref[window, hd:] += dv
-        own_ref[:, :hd] = acc_ref[lead:, :hd] * scaling
-        own_ref[:, hd:] = acc_ref[lead:, hd:]
-        for s in range(1, WIN):
-            rows_of = slice((WIN - 1 - s) * shard, (WIN - s) * shard)
-            far_refs[s - 1][:, :hd] = (acc_ref[rows_of, :hd] * scaling).astype(jnp.bfloat16)
-            far_refs[s - 1][:, hd:] = acc_ref[rows_of, hd:].astype(jnp.bfloat16)
+        for ref, start in zip((own_ref, *far_refs), starts):
+            rows_of = pl.ds(pl.multiple_of(start, KEYS), shard)
+            ref[:, :hd] = (acc_ref[rows_of, :hd] * scaling).astype(ref.dtype)
+            ref[:, hd:] = acc_ref[rows_of, hd:].astype(ref.dtype)
     for copy in stores:
         copy.wait()
 
@@ -186,7 +188,7 @@
     )(info)
 
 
-def attend(info, q, do, bias, shards, before, tiles, columns):
+def attend(info, q_do, bias, shards, before, tiles, columns):
     shard, width = shards[0].shape
     hd = width // 2
     rows = shard // tiles
@@ -195,9 +197,9 @@
     keys = (WIN - 1) * shard + rows
     heads = columns // hd
     bf16, f32 = jnp.bfloat16, jnp.float32
-    inner = q.shape[1] == columns
-    args = [info, *(in_vmem(q, do) if inner else (q, do)), *in_vmem(bias, *shards)]
-    in_specs = [SCALARS] + [WHOLE if inner else ANY] * 2 + [WHOLE] * (1 + WIN)
+    inner = len(q_do) == 1
+    args = [info, *(in_vmem(*q_do) if inner else q_do), *in_vmem(bias, *shards)]
+    in_specs = [SCALARS] + [WHOLE if inner else ANY] * len(q_do) + [WHOLE] * (1 + WIN)
     aliases = {}
     if before is not None:
         aliases = {len(args) + 1: 0, len(args) + 2: 1}
@@ -206,13 +208,13 @@
     out_shape = [jax.ShapeDtypeStruct((shard, columns), bf16)] * 2
     out_specs = [ANY, ANY]
     if last:
-        out_shape += [pltpu.VMEM((shard, width), f32)] + [pltpu.VMEM((shard, width), bf16)] * (WIN - 1)
+        out_shape += [pltpu.VMEM((shard, width), d) for d in (f32, bf16, f32, bf16)]
         out_specs += [WHOLE] * WIN
     else:
         out_shape += [pltpu.VMEM((WIN * shard, width), f32)]
         out_specs += [WHOLE]
     return pl.pallas_call(
-        functools.partial(attend_kernel, tiles, index),
+        functools.partial(attend_kernel, tiles, index, inner),
         out_shape=out_shape,
         in_specs=in_specs,
         out_specs=out_specs,
@@ -221,8 +223,7 @@
             pltpu.VMEM((WIN * shard, hd), bf16),
             pltpu.VMEM((hd, keys), bf16),
             pltpu.VMEM((hd, keys), bf16),
-            pltpu.VMEM((rows, columns) if not inner else (16, 128), bf16),
-            pltpu.VMEM((rows, columns) if not inner else (16, 128), bf16),
+            pltpu.VMEM((16, 128) if inner else (rows, 2 * columns), bf16),
             pltpu.VMEM((heads * rows, hd), bf16),
             pltpu.VMEM((heads * rows, hd), bf16),
             pltpu.VMEM((keys, heads * rows), bf16),
@@ -250,9 +251,17 @@
     refs[-1][...] = total[:, hd:].astype(jnp.bfloat16)
 
 
-def ring(value, axis, steps):
-    count = lax.axis_size(axis)
-    return lax.ppermute(value, axis, [(i, (i + steps) % count) for i in range(count)])
+def move(value, kind, back=False):
+    count = lax.axis_size("ctx")
+    steps = {"A": lambda i: 3 if i % 2 else 1, "B": lambda i: 2, "C": lambda i: -1 if i % 2 else 1}[kind]
+    pairs = [(i, (i + steps(i)) % count) for i in range(count)]
+    return lax.ppermute(value, "ctx", [p[::-1] for p in pairs] if back else pairs)
+
+
+def window(own):
+    b = move(own, "B")
+    a = move(own, "A")
+    return [own, a, b, move(b, "C")]
 
 
 def body(queries, keys, values, d_out, doc_lengths):
@@ -279,25 +288,28 @@
             return lax.ppermute(x, "head", [(0, 1), (1, 0)])
 
         own = jnp.concatenate([key_value(head), swap(key_value(other))], axis=0)
-        q_other = swap(half(queries, other))
-        do_other = swap(half(d_out, other))
-        shards = [own] + [ring(own, "ctx", s) for s in range(1, WIN)]
-        out, dq, acc = attend(info, queries, d_out, bias[0], shards, None, 2, columns)
-        out, dq, total, *far = attend(info, q_other, do_other, bias[1], shards, (acc, out, dq), 2, columns)
+        both = swap(jnp.concatenate([half(queries, other), half(d_out, other)], axis=1))
+        shards = window(own)
+        out, dq, acc = attend(info, (queries, d_out), bias[0], shards, None, 2, columns)
+        out, dq, total, *far = attend(info, (both,), bias[1], shards, (acc, out, dq), 2, columns)
     else:
         swap = lambda x: lax.all_to_all(x, "head", split_axis=1, concat_axis=0, tiled=True)
         own = jnp.concatenate([swap(keys), swap(values)], axis=1)
-        shards = [own] + [ring(own, "ctx", s) for s in range(1, WIN)]
-        out, dq, total, *far = attend(info, swap(queries), swap(d_out), bias[0], shards, None, 1, columns)
-    near = [ring(x, "ctx", -s) for s, x in zip(range(1, WIN), far)]
+        shards = window(own)
+        out, dq, total, *far = attend(
+            info, (jnp.concatenate([swap(queries), swap(d_out)], axis=1),), bias[0], shards, None, 1, columns
+        )
+    far_c = move(far[2], "C", True)
+    near_a = move(far[0], "A", True)
+    near_b = move((far[1] + far_c.astype(jnp.float32)).astype(jnp.bfloat16), "B", True)
     grad_keys, grad_values = pl.pallas_call(
         gather_kernel,
         out_shape=[jax.ShapeDtypeStruct((shard, hd), jnp.bfloat16)] * 2,
-        in_specs=[WHOLE] * WIN,
+        in_specs=[WHOLE] * 3,
         out_specs=[WHOLE] * 2,
         compiler_params=pltpu.CompilerParams(vmem_limit_bytes=4 << 20),
         name="gather",
-    )(*in_vmem(total, *near))
+    )(*in_vmem(total, near_a, near_b))
     return out, dq, grad_keys, grad_values
 
 

time: 40.3 us -> 36.9 us (0.916)
  waiting for transfers between devices: 14.6 us -> 12.1 us
  starting transfers between devices: 9.5 us -> 8.46 us
    ppermute x6, waiting for transfers between devices: 13.2 us -> 10.9 us  [move(): lax.ppermute(value, 'ctx', [p[::-1] for p in pairs] if back else pairs)]
    ppermute x3 -> x2, starting transfers between devices: 5.25 us -> 3.12 us  [swap(): return lax.ppermute(x, 'head', [(0, 1), (1, 0)])]
    ppermute x6, starting transfers between devices: 4.25 us -> 5.34 us  [move(): lax.ppermute(value, 'ctx', [p[::-1] for p in pairs] if back else pairs)]
    ppermute x3 -> x2, waiting for transfers between devices: 1.38 us -> 1.17 us  [swap(): return lax.ppermute(x, 'head', [(0, 1), (1, 0)])]
    dynamic_slice x3 -> x2, local copies, waits for them, and re-layouts: 1.81 us -> 1.89 us  [half(): return lax.dynamic_slice_in_dim(x, index * width, width, 1)]
  transfers between devices with their start and end apart: 9 -> 8, of which waited for: 6 -> 4; matrix products, arithmetic and copies ran while one was open for 3% -> 3% of each run, Pallas kernels for 16% -> 17%
where the time goes in v4:
time: 36.9 us; the launch traced here: 36.7 us
  Pallas kernels  12.7 us (34%)
  waiting for transfers between devices  12.1 us (33%)
  starting transfers between devices  8.46 us (23%)
  local copies, waits for them, and re-layouts  2.56 us (7%)
  between operations  0.76 us (2%)
    pallas_call x2, Pallas kernels, attend(): pl.pallas_call(functools.partial(attend_kernel, tiles, index, inner), out...  11.2 us
    ppermute x6, waiting for transfers between devices, move(): lax.ppermute(value, 'ctx', [p[::-1] for p in pairs] if back else pairs)  10.9 us
    ppermute x6, starting transfers between devices, move(): lax.ppermute(value, 'ctx', [p[::-1] for p in pairs] if back else pairs)  5.34 us
    ppermute x2, starting transfers between devices, swap(): return lax.ppermute(x, 'head', [(0, 1), (1, 0)])  3.12 us
    dynamic_slice x2, local copies, waits for them, and re-layouts, half(): return lax.dynamic_slice_in_dim(x, index * width, width, 1)  1.89 us
    ppermute x2, waiting for transfers between devices, swap(): return lax.ppermute(x, 'head', [(0, 1), (1, 0)])  1.17 us
  transfers between devices with their start and end apart: 8, of which 4 were waited for; matrix products, arithmetic and copies ran while one was open for 3% of the time, Pallas kernels for 17%

profile of v4, /device:TPU:0, one launch (start us, length us, event | category | flops | bytes accessed | tf_op | source)
XLA Modules:
  0.0 36.7 jit_solution(8295246504518214100)
XLA Ops:
  0.6 0.8 %constant_dynamic-slice_fusion.2 = (bf16[128,128]{1,0:T(8,128)(2,1)S(1)}, bf16[128,128]{1,0:T(8,128)(2,1)S(1)}, bf16[128,128]{1,0:T(8,128)(2,1)S(1)}, bf16[128,128]{1,0:T(8,128)(2,1)S(1)}) fusion(bf16[128,256]{1,0:T(8,128)(2,1)} %param.7, s32[]{:T(128)S(6)} %select_n.13, s32[]{:T(128)S(6)} %select_n.14, bf16[128,256]{1,0:T(8,128)(2,1)} %param.6), kind=kLoop, calls=%fused_computation.6 | loop fusion | bytes 262152 | tf_op jit(solution)/shard_map/dynamic_slice | solution.py:282
  1.5 3.0 %collective-permute-start.1 = (bf16[128,256]{1,0:T(8,128)(2,1)S(1)}, bf16[128,256]{1,0:T(8,128)(2,1)S(1)}, u32[]{:S(2)}, u32[]{:S(2)}) collective-permute-start(bf16[128,256]{1,0:T(8,128)(2,1)S(1)} %pad_maximum_fusion.2), channel_id=1, source_target_pairs={{0,1},{1,0},{2,3},{3,2},{4,5},{5,4},{6,7},{7,6},{8,9},{9,8},{10,11... | collective-permute-start | bytes 196616 | tf_op jit(solution)/shard_map/ppermute | solution.py:288
  4.5 1.1 %constant_dynamic-slice_fusion.4 = (bf16[128,1024]{1,0:T(8,128)(2,1)S(1)}, bf16[128,1024]{1,0:T(8,128)(2,1)S(1)}) fusion(bf16[128,2048]{1,0:T(8,128)(2,1)} %refs_1_.1, s32[]{:T(128)S(6)} %select_n.12, bf16[128,2048]{1,0:T(8,128)(2,1)} %refs_0_.1), kind=kLoop, calls=%fused_computation.8 | loop fusion | bytes 1048580 | tf_op jit(solution)/shard_map/dynamic_slice | solution.py:282
  5.6 0.0 copy-start
  5.6 0.0 copy-start.1
  5.7 0.1 collective-permute-start
  5.7 1.2 %collective-permute-done.1 = bf16[128,256]{1,0:T(8,128)(2,1)S(1)} collective-permute-done((bf16[128,256]{1,0:T(8,128)(2,1)S(1)}, bf16[128,256]{1,0:T(8,128)(2,1)S(1)}, u32[]{:S(2)}, u32[]{:S(2)}) %collective-permute-start.1) | collective-permute-done | bytes 65568 | tf_op jit(solution)/shard_map/ppermute | solution.py:288
  6.9 2.0 %collective-permute-start.3 = (bf16[256,256]{1,0:T(8,128)(2,1)S(1)}, bf16[256,256]{1,0:T(8,128)(2,1)S(1)}, u32[]{:S(2)}, u32[]{:S(2)}) collective-permute-start(bf16[256,256]{1,0:T(8,128)(2,1)S(1)} %pad_maximum_fusion.1.refs_3_.refs_2_), channel_id=1, source_target_pairs={{0,4},{2,6},{4,8},{6,10},{8,12},{10,14},{12,16},{14,18},{16,20},{1... | collective-permute-start | bytes 393224 | tf_op jit(solution)/shard_map/ppermute | solution.py:258
  8.9 0.0 collective-permute-start.2
  8.9 6.2 %collective-permute-done.3.refs_5_.refs_4_ = bf16[256,256]{1,0:T(8,128)(2,1)S(1)} collective-permute-done((bf16[256,256]{1,0:T(8,128)(2,1)S(1)}, bf16[256,256]{1,0:T(8,128)(2,1)S(1)}, u32[]{:S(2)}, u32[]{:S(2)}) %collective-permute-start.3) | collective-permute-done | bytes 131104 | tf_op jit(solution)/shard_map/ppermute | solution.py:258
  15.1 0.0 collective-permute-start.4
  15.1 0.0 copy-start.2
  15.1 0.7 %copy-done.2 = s32[32]{0:T(128)S(1)} copy-done((s32[32]{0:T(128)S(1)}, s32[32]{0:T(128)}, u32[]{:S(2)}) %copy-start.2) | copy-done | bytes 152
  15.8 0.1 pad_add_fusion.info
  15.8 0.7 %masks.1 = (f32[896,128]{1,0:T(8,128)S(1)}, f32[896,128]{1,0:T(8,128)S(1)}) custom-call(s32[34]{0:T(128)S(1)} %pad_add_fusion.info), custom_call_target="tpu_custom_call" | custom-call | tf_op jit(solution)/shard_map/masks/pallas_call | solution.py:181
  16.6 0.0 collective-permute-done.2.refs_4_.refs_3_
  16.6 0.0 collective-permute-done.4.refs_6_.refs_5_
  16.6 0.0 copy-done
  16.6 0.0 copy-done.1
  16.6 5.5 %attend_first.1 = (bf16[256,1024]{1,0:T(8,128)(2,1)}, bf16[256,1024]{1,0:T(8,128)(2,1)}, f32[1024,256]{1,0:T(8,128)S(1)}) custom-call(s32[34]{0:T(128)S(1)} %pad_add_fusion.info, bf16[128,2048]{1,0:T(8,128)(2,1)S(1)} %copy-done.1, bf16[128,2048]{1,0:T(8,128)(2,1)S(1)} %copy-done, f32[896,128]{1,0:T(8,128)S(1)} %get-tuple-element.18.refs_2_, ...), custom_call_target="tpu_custom_call" | custom-call | flops 1409286144 | bytes 2097152 | tf_op jit(solution)/shard_map/attend_first/pallas_call | solution.py:216
  22.2 0.0 collective-permute-done.refs_0_
  22.2 5.7 %attend_last.1 = (bf16[256,1024]{1,0:T(8,128)(2,1)}, bf16[256,1024]{1,0:T(8,128)(2,1)}, f32[256,256]{1,0:T(8,128)S(1)}, bf16[256,256]{1,0:T(8,128)(2,1)S(1)}, f3...) custom-call(s32[34]{0:T(128)S(1)} %pad_add_fusion.info, ...), custom_call_target="tpu_custom_call", output_to_operand_aliasing={{0}: (8, {}), {1}: (9, {})} | custom-call | flops 1409286144 | bytes 2097152 | tf_op jit(solution)/shard_map/attend_last/pallas_call | solution.py:216
  27.9 0.6 %collective-permute-start.6 = (bf16[256,256]{1,0:T(8,128)(2,1)S(1)}, bf16[256,256]{1,0:T(8,128)(2,1)S(1)}, u32[]{:S(2)}, u32[]{:S(2)}) collective-permute-start(bf16[256,256]{1,0:T(8,128)(2,1)S(1)} %get-tuple-element.27), channel_id=1, source_target_pairs={{2,0},{0,2},{6,4},{4,6},{10,8},{8,10},{14,12},{12,14},{18,16},{16,... | collective-permute-start | bytes 393224 | tf_op jit(solution)/shard_map/ppermute | solution.py:258
  28.5 2.3 %collective-permute-start.5 = (bf16[256,256]{1,0:T(8,128)(2,1)S(1)}, bf16[256,256]{1,0:T(8,128)(2,1)S(1)}, u32[]{:S(2)}, u32[]{:S(2)}) collective-permute-start(bf16[256,256]{1,0:T(8,128)(2,1)S(1)} %get-tuple-element.25), channel_id=1, source_target_pairs={{2,0},{8,2},{6,4},{12,6},{10,8},{16,10},{14,12},{20,14},{18,16},{2... | collective-permute-start | bytes 393224 | tf_op jit(solution)/shard_map/ppermute | solution.py:258
  30.8 0.0 collective-permute-done.6
  30.8 0.5 %collective-permute-start.7 = (bf16[256,256]{1,0:T(8,128)(2,1)S(1)}, bf16[256,256]{1,0:T(8,128)(2,1)S(1)}, u32[]{:S(2)}, u32[]{:S(2)}) collective-permute-start(bf16[256,256]{1,0:T(8,128)(2,1)S(1)} %add_convert_fusion), channel_id=1, source_target_pairs={{4,0},{6,2},{8,4},{10,6},{12,8},{14,10},{16,12},{18,14},{20,16},{2... | collective-permute-start | bytes 393224 | tf_op jit(solution)/shard_map/ppermute | solution.py:258
  31.3 3.3 %collective-permute-done.5.refs_0_ = bf16[256,256]{1,0:T(8,128)(2,1)S(1)} collective-permute-done((bf16[256,256]{1,0:T(8,128)(2,1)S(1)}, bf16[256,256]{1,0:T(8,128)(2,1)S(1)}, u32[]{:S(2)}, u32[]{:S(2)}) %collective-permute-start.5) | collective-permute-done | bytes 131104 | tf_op jit(solution)/shard_map/ppermute | solution.py:258
  34.6 1.4 %collective-permute-done.7.refs_1_ = bf16[256,256]{1,0:T(8,128)(2,1)S(1)} collective-permute-done((bf16[256,256]{1,0:T(8,128)(2,1)S(1)}, bf16[256,256]{1,0:T(8,128)(2,1)S(1)}, u32[]{:S(2)}, u32[]{:S(2)}) %collective-permute-start.7) | collective-permute-done | bytes 131104 | tf_op jit(solution)/shard_map/ppermute | solution.py:258
  36.0 0.7 %gather.1 = (bf16[256,128]{1,0:T(8,128)(2,1)}, bf16[256,128]{1,0:T(8,128)(2,1)}) custom-call(f32[256,256]{1,0:T(8,128)S(1)} %get-tuple-element.24.own_ref, bf16[256,256]{1,0:T(8,128)(2,1)S(1)} %collective-permute-done.5.refs_0_, bf16[256,256]{1,0:T(8,128)(2,1)S(1)} %collective-permute-done.7.refs_1_), custom_call_target="tpu_custom_call" | custom-call | tf_op jit(solution)/shard_map/gather/pallas_call | solution.py:305
  (4 shorter events, 0.1 us)
Async XLA Ops:
  1.5 5.4 %collective-permute-start.1 = (bf16[128,256]{1,0:T(8,128)(2,1)S(1)}, bf16[128,256]{1,0:T(8,128)(2,1)S(1)}, u32[]{:S(2)}, u32[]{:S(2)}) collective-permute-start(bf16[128,256]{1,0:T(8,128)(2,1)S(1)} %pad_maximum_fusion.2), channel_id=1, source_target_pairs={{0,1},{1,0},{2,3},{3,2},{4,5},{5,4},{6,7},{7,6},{8,9},{9,8},{10,11... | collective-permute-start | bytes 196616 | tf_op jit(solution)/shard_map/ppermute | solution.py:288
  5.6 11.0 %copy-start = (bf16[128,2048]{1,0:T(8,128)(2,1)S(1)}, bf16[128,2048]{1,0:T(8,128)(2,1)}, u32[]{:S(2)}) copy-start(bf16[128,2048]{1,0:T(8,128)(2,1)} %refs_1_.1) | copy-start | bytes 1572868
  5.6 11.0 %copy-start.1 = (bf16[128,2048]{1,0:T(8,128)(2,1)S(1)}, bf16[128,2048]{1,0:T(8,128)(2,1)}, u32[]{:S(2)}) copy-start(bf16[128,2048]{1,0:T(8,128)(2,1)} %refs_0_.1) | copy-start | bytes 1572868
  5.7 16.5 %collective-permute-start = (bf16[128,2048]{1,0:T(8,128)(2,1)S(1)}, bf16[128,2048]{1,0:T(8,128)(2,1)S(1)}, u32[]{:S(2)}, u32[]{:S(2)}) collective-permute-start(bf16[128,2048]{1,0:T(8,128)(2,1)S(1)} %pad_maximum_fusion), channel_id=1, source_target_pairs={{0,1},{1,0},{2,3},{3,2},{4,5},{5,4},{6,7},{7,6},{8,9},{9,8},{10,11... | collective-permute-start | bytes 1572872 | tf_op jit(solution)/shard_map/ppermute | solution.py:288
  6.9 8.2 %collective-permute-start.3 = (bf16[256,256]{1,0:T(8,128)(2,1)S(1)}, bf16[256,256]{1,0:T(8,128)(2,1)S(1)}, u32[]{:S(2)}, u32[]{:S(2)}) collective-permute-start(bf16[256,256]{1,0:T(8,128)(2,1)S(1)} %pad_maximum_fusion.1.refs_3_.refs_2_), channel_id=1, source_target_pairs={{0,4},{2,6},{4,8},{6,10},{8,12},{10,14},{12,16},{14,18},{16,20},{1... | collective-permute-start | bytes 393224 | tf_op jit(solution)/shard_map/ppermute | solution.py:258
  8.9 7.7 %collective-permute-start.2 = (bf16[256,256]{1,0:T(8,128)(2,1)S(1)}, bf16[256,256]{1,0:T(8,128)(2,1)S(1)}, u32[]{:S(2)}, u32[]{:S(2)}) collective-permute-start(bf16[256,256]{1,0:T(8,128)(2,1)S(1)} %pad_maximum_fusion.1.refs_3_.refs_2_), channel_id=1, source_target_pairs={{0,2},{2,8},{4,6},{6,12},{8,10},{10,16},{12,14},{14,20},{16,18},{1... | collective-permute-start | bytes 393224 | tf_op jit(solution)/shard_map/ppermute | solution.py:258
  15.1 1.5 %collective-permute-start.4 = (bf16[256,256]{1,0:T(8,128)(2,1)S(1)}, bf16[256,256]{1,0:T(8,128)(2,1)S(1)}, u32[]{:S(2)}, u32[]{:S(2)}) collective-permute-start(bf16[256,256]{1,0:T(8,128)(2,1)S(1)} %collective-permute-done.3.refs_5_.refs_4_), channel_id=1, source_target_pairs={{0,2},{2,0},{4,6},{6,4},{8,10},{10,8},{12,14},{14,12},{16,18},{18,... | collective-permute-start | bytes 393224 | tf_op jit(solution)/shard_map/ppermute | solution.py:258
  15.1 0.7 %copy-start.2 = (s32[32]{0:T(128)S(1)}, s32[32]{0:T(128)}, u32[]{:S(2)}) copy-start(s32[32]{0:T(128)} %param.9) | copy-start | bytes 388
  27.9 2.9 %collective-permute-start.6 = (bf16[256,256]{1,0:T(8,128)(2,1)S(1)}, bf16[256,256]{1,0:T(8,128)(2,1)S(1)}, u32[]{:S(2)}, u32[]{:S(2)}) collective-permute-start(bf16[256,256]{1,0:T(8,128)(2,1)S(1)} %get-tuple-element.27), channel_id=1, source_target_pairs={{2,0},{0,2},{6,4},{4,6},{10,8},{8,10},{14,12},{12,14},{18,16},{16,... | collective-permute-start | bytes 393224 | tf_op jit(solution)/shard_map/ppermute | solution.py:258
  28.5 6.1 %collective-permute-start.5 = (bf16[256,256]{1,0:T(8,128)(2,1)S(1)}, bf16[256,256]{1,0:T(8,128)(2,1)S(1)}, u32[]{:S(2)}, u32[]{:S(2)}) collective-permute-start(bf16[256,256]{1,0:T(8,128)(2,1)S(1)} %get-tuple-element.25), channel_id=1, source_target_pairs={{2,0},{8,2},{6,4},{12,6},{10,8},{16,10},{14,12},{20,14},{18,16},{2... | collective-permute-start | bytes 393224 | tf_op jit(solution)/shard_map/ppermute | solution.py:258
  30.8 5.2 %collective-permute-start.7 = (bf16[256,256]{1,0:T(8,128)(2,1)S(1)}, bf16[256,256]{1,0:T(8,128)(2,1)S(1)}, u32[]{:S(2)}, u32[]{:S(2)}) collective-permute-start(bf16[256,256]{1,0:T(8,128)(2,1)S(1)} %add_convert_fusion), channel_id=1, source_target_pairs={{4,0},{6,2},{8,4},{10,6},{12,8},{14,10},{16,12},{18,14},{20,16},{2... | collective-permute-start | bytes 393224 | tf_op jit(solution)/shard_map/ppermute | solution.py:258

commit v5 on v4

--- a/solution.py
+++ b/solution.py
@@ -56,9 +56,9 @@
     shard_refs = refs[:WIN]
     refs = refs[WIN:]
     last = index == tiles - 1
-    acc_in = None
+    acc_refs = []
     if index:
-        acc_in = refs[0]
+        acc_refs = [refs[0]]
         refs = refs[3:]
     out_hbm, dq_hbm = refs[:2]
     if last:
@@ -66,9 +66,9 @@
         far_refs = refs[3 : 2 + WIN]
         refs = refs[2 + WIN :]
     else:
-        acc_out = refs[2]
-        refs = refs[3:]
-    k_ref, v_ref, kt_ref, vt_ref, q_do, q_rows, do_rows, p_ref, ds_ref, out_ref, dq_ref, acc_ref, sem = refs
+        refs = [*refs[3:-1], refs[2], refs[-1]]
+    k_ref, v_ref, kt_ref, vt_ref, q_rows, do_rows, p_ref, ds_ref, out_ref, dq_ref, acc, sem = refs
+    acc_refs.append(acc)
 
     shard, width = shard_refs[0].shape
     hd = width // 2
@@ -84,16 +84,11 @@
     log2e = math.log2(math.e) / math.sqrt(hd)
     scaling = 1 / math.sqrt(hd)
 
-    loads = []
     if loaded:
-        q_do = sources[0]
+        q_do = [(sources[0], 0), (sources[0], columns)]
     else:
-        mine = pl.ds(pl.multiple_of(info[1] * columns, 128), columns)
-        for i, source in enumerate(sources):
-            target = q_do.at[:, i * columns : (i + 1) * columns]
-            loads.append(pltpu.make_async_copy(source.at[:, mine], target, sem.at[i]))
-    for copy in loads:
-        copy.start()
+        mine = pl.multiple_of(info[1] * columns, 128)
+        q_do = [(source, mine) for source in sources]
     part = shard // tiles
     odd = info[0] & 1
     starts = [(WIN - 1) * shard, odd * 2 * shard, shard, (1 - odd) * 2 * shard]
@@ -103,11 +98,9 @@
             k_ref[at, :] = ref[j * part : (j + 1) * part, :hd]
             v_ref[at, :] = ref[j * part : (j + 1) * part, hd:]
     window = pl.ds(base, keys)
-    for copy in loads:
-        copy.wait()
-    for h in range(heads):
-        q_rows[h * rows : (h + 1) * rows, :] = q_do[:, h * hd : (h + 1) * hd]
-        do_rows[h * rows : (h + 1) * rows, :] = q_do[:, columns + h * hd : columns + (h + 1) * hd]
+    for (source, start), target in zip(q_do, (q_rows, do_rows)):
+        for h in range(heads):
+            target[h * rows : (h + 1) * rows, :] = source[:, pl.ds(start + h * hd, hd)]
     kt_ref[...] = k_ref[window, :].T
     vt_ref[...] = v_ref[window, :].T
     n = HEADS * rows
@@ -115,62 +108,80 @@
     def at(p):
         return slice(p * n, (p + 1) * n)
 
-    def weights(p):
+    def scores(p):
         s = dot(k_ref[window, :], q_rows[at(p), :], NT)
         s = s + jnp.concatenate([bias_ref[...]] * HEADS, axis=1)
-        top = jnp.max(fold(s, jnp.max), axis=0, keepdims=True)
+        return s, jnp.max(fold(s, jnp.max), axis=0, keepdims=True)
+
+    def weights(p, s, top):
         e = jnp.exp2((s - top) * log2e)
         total = jnp.sum(fold(e, jnp.sum), axis=0, keepdims=True)
         p_f32 = e * (1.0 / total)
         p_ref[:, at(p)] = p_f32.astype(jnp.bfloat16)
         return p_f32
 
-    def backward(p, p_f32):
+    def columns_out(p, x, vmem, hbm, slot):
+        for i in range(HEADS):
+            h = p * HEADS + i
+            vmem[:, h * hd : (h + 1) * hd] = x[:, i * rows : (i + 1) * rows].T
+        here = slice(p * HEADS * hd, (p + 1) * HEADS * hd)
+        place = pl.ds(pl.multiple_of(tile * rows, rows), rows)
+        copy = pltpu.make_async_copy(vmem.at[:, here], hbm.at[place, here], sem.at[slot])
+        copy.start()
+        stores.append(copy)
+
+    def outputs(p):
         out = dot(vt_ref[...], p_ref[:, at(p)], NN).astype(jnp.bfloat16)
         do_t = do_rows[at(p), :].T.astype(jnp.float32)
         delta = jnp.sum(do_t * out.astype(jnp.float32), axis=0, keepdims=True)
-        dp = dot(v_ref[window, :], do_rows[at(p), :], NT)
+        columns_out(p, out, out_ref, out_hbm, 2 * p)
+        return delta
+
+    def dprobs(p):
+        return dot(v_ref[window, :], do_rows[at(p), :], NT)
+
+    def dscores(p, p_f32, dp, delta):
         ds_ref[:, at(p)] = (p_f32 * (dp - delta)).astype(jnp.bfloat16)
+
+    def dqueries(p):
         dq = (dot(kt_ref[...], ds_ref[:, at(p)], NN) * scaling).astype(jnp.bfloat16)
-        for i in range(HEADS):
-            h = p * HEADS + i
-            out_ref[:, h * hd : (h + 1) * hd] = out[:, i * rows : (i + 1) * rows].T
-            dq_ref[:, h * hd : (h + 1) * hd] = dq[:, i * rows : (i + 1) * rows].T
-        place = pl.ds(pl.multiple_of(tile * rows, rows), rows), pl.ds(p * HEADS * hd, HEADS * hd)
-        here = slice(None), slice(p * HEADS * hd, (p + 1) * HEADS * hd)
-        stores = [
-            pltpu.make_async_copy(out_ref.at[here], out_hbm.at[place], sem.at[2 + 2 * p]),
-            pltpu.make_async_copy(dq_ref.at[here], dq_hbm.at[place], sem.at[3 + 2 * p]),
-        ]
-        for copy in stores:
-            copy.start()
-        return stores
-
+        columns_out(p, dq, dq_ref, dq_hbm, 2 * p + 1)
+
+    def sums(p):
+        dk, dv = dot(ds_ref[:, at(p)], q_rows[at(p), :], NN), dot(p_ref[:, at(p)], do_rows[at(p), :], NN)
+        if p:
+            acc_ref[inside, :hd] += dk
+            acc_ref[inside, hd:] += dv
+        else:
+            acc_ref[inside, :hd], acc_ref[inside, hd:] = dk, dv
+
+    inside = slice(KEYS, KEYS + keys)
+    acc_ref = acc_refs[-1]
+    acc_ref[:KEYS, :] = jnp.zeros((KEYS, width), jnp.float32)
+    acc_ref[KEYS + keys :, :] = jnp.zeros((KEYS, width), jnp.float32)
     stores = []
-    ahead = weights(0)
+    w = weights(0, *scores(0))
     for p in range(pairs):
-        now = ahead
-        if p + 1 < pairs:
-            ahead = weights(p + 1)
-        stores += backward(p, now)
-    dv = dot(p_ref[...], do_rows[...], NN)
-    dk = dot(ds_ref[...], q_rows[...], NN)
-    if not last:
-        acc_out[...] = jnp.zeros_like(acc_out)
-        acc_out[window, :hd] = dk
-        acc_out[window, hd:] = dv
-    else:
-        if acc_in is None:
-            acc_ref[:, :hd] = dk
-            acc_ref[:, hd:] = dv
-        else:
-            acc_ref[...] = acc_in[...]
-            acc_ref[window, :hd] += dk
-            acc_ref[window, hd:] += dv
+        nsc = scores(p + 1) if p + 1 < pairs else None
+        dp = dprobs(p)
+        delta = outputs(p)
+        if p:
+            dqueries(p - 1)
+            sums(p - 1)
+        nw = weights(p + 1, *nsc) if p + 1 < pairs else None
+        dscores(p, w, dp, delta)
+        w = nw
+    dqueries(pairs - 1)
+    sums(pairs - 1)
+    if last:
         for ref, start in zip((own_ref, *far_refs), starts):
-            rows_of = pl.ds(pl.multiple_of(start, KEYS), shard)
-            ref[:, :hd] = (acc_ref[rows_of, :hd] * scaling).astype(ref.dtype)
-            ref[:, hd:] = acc_ref[rows_of, hd:].astype(ref.dtype)
+            total = None
+            for i, acc in enumerate(acc_refs):
+                at_tile = (i ^ flip) * rows if tiles > 1 else 0
+                x = acc[pl.ds(pl.multiple_of(start - at_tile + KEYS, KEYS), shard), :]
+                total = x if total is None else total + x
+            ref[:, :hd] = (total[:, :hd] * scaling).astype(ref.dtype)
+            ref[:, hd:] = total[:, hd:].astype(ref.dtype)
     for copy in stores:
         copy.wait()
 
@@ -197,9 +208,10 @@
     keys = (WIN - 1) * shard + rows
     heads = columns // hd
     bf16, f32 = jnp.bfloat16, jnp.float32
+    acc = pltpu.VMEM((keys + 2 * KEYS, width), f32)
     inner = len(q_do) == 1
-    args = [info, *(in_vmem(*q_do) if inner else q_do), *in_vmem(bias, *shards)]
-    in_specs = [SCALARS] + [WHOLE if inner else ANY] * len(q_do) + [WHOLE] * (1 + WIN)
+    args = [info, *in_vmem(*q_do, bias, *shards)]
+    in_specs = [SCALARS] + [WHOLE] * (len(q_do) + 1 + WIN)
     aliases = {}
     if before is not None:
         aliases = {len(args) + 1: 0, len(args) + 2: 1}
@@ -211,7 +223,7 @@
         out_shape += [pltpu.VMEM((shard, width), d) for d in (f32, bf16, f32, bf16)]
         out_specs += [WHOLE] * WIN
     else:
-        out_shape += [pltpu.VMEM((WIN * shard, width), f32)]
+        out_shape += [acc]
         out_specs += [WHOLE]
     return pl.pallas_call(
         functools.partial(attend_kernel, tiles, index, inner),
@@ -223,15 +235,14 @@
             pltpu.VMEM((WIN * shard, hd), bf16),
             pltpu.VMEM((hd, keys), bf16),
             pltpu.VMEM((hd, keys), bf16),
-            pltpu.VMEM((16, 128) if inner else (rows, 2 * columns), bf16),
             pltpu.VMEM((heads * rows, hd), bf16),
             pltpu.VMEM((heads * rows, hd), bf16),
             pltpu.VMEM((keys, heads * rows), bf16),
             pltpu.VMEM((keys, heads * rows), bf16),
             pltpu.VMEM((rows, columns), bf16),
             pltpu.VMEM((rows, columns), bf16),
-            pltpu.VMEM((WIN * shard, width) if last else (8, 128), f32),
-            pltpu.SemaphoreType.DMA((2 + 2 * (heads // HEADS),)),
+            *([acc] if last else []),
+            pltpu.SemaphoreType.DMA((2 * (heads // HEADS),)),
         ],
         input_output_aliases=aliases,
         compiler_params=pltpu.CompilerParams(vmem_limit_bytes=24 << 20),
@@ -258,10 +269,11 @@
     return lax.ppermute(value, "ctx", [p[::-1] for p in pairs] if back else pairs)
 
 
-def window(own):
+def window(own, bias):
     b = move(own, "B")
     a = move(own, "A")
-    return [own, a, b, move(b, "C")]
+    b, *bias = lax.optimization_barrier((b, *bias))
+    return [own, a, b, move(b, "C")], bias
 
 
 def body(queries, keys, values, d_out, doc_lengths):
@@ -289,13 +301,13 @@
 
         own = jnp.concatenate([key_value(head), swap(key_value(other))], axis=0)
         both = swap(jnp.concatenate([half(queries, other), half(d_out, other)], axis=1))
-        shards = window(own)
+        shards, bias = window(own, bias)
         out, dq, acc = attend(info, (queries, d_out), bias[0], shards, None, 2, columns)
         out, dq, total, *far = attend(info, (both,), bias[1], shards, (acc, out, dq), 2, columns)
     else:
         swap = lambda x: lax.all_to_all(x, "head", split_axis=1, concat_axis=0, tiled=True)
         own = jnp.concatenate([swap(keys), swap(values)], axis=1)
-        shards = window(own)
+        shards, bias = window(own, bias)
         out, dq, total, *far = attend(
             info, (jnp.concatenate([swap(queries), swap(d_out)], axis=1),), bias[0], shards, None, 1, columns
         )

time: 36.9 us -> 35.8 us (0.970)
  Pallas kernels: 12.7 us -> 11.6 us
  starting transfers between devices: 8.46 us -> 9.21 us
  local copies, waits for them, and re-layouts: 2.56 us -> 1.99 us
    pallas_call x2, Pallas kernels: 11.2 us -> 10.2 us  [attend(): pl.pallas_call(functools.partial(attend_kernel, tiles, index, inner), out...]
    ppermute x6, starting transfers between devices: 5.34 us -> 6.06 us  [move(): lax.ppermute(value, 'ctx', [p[::-1] for p in pairs] if back else pairs)]
    unnamed x6, local copies, waits for them, and re-layouts: 0.67 us -> 0.01 us
  transfers between devices with their start and end apart: 8 -> 8, of which waited for: 4 -> 6; matrix products, arithmetic and copies ran while one was open for 3% -> 4% of each run, Pallas kernels for 17% -> 16%
where the time goes in v5:
time: 35.8 us; the launch traced here: 35.6 us
  waiting for transfers between devices  11.9 us (33%)
  Pallas kernels  11.6 us (32%)
  starting transfers between devices  9.21 us (26%)
  local copies, waits for them, and re-layouts  1.99 us (6%)
  between operations  0.72 us (2%)
    ppermute x6, waiting for transfers between devices, move(): lax.ppermute(value, 'ctx', [p[::-1] for p in pairs] if back else pairs)  10.9 us
    pallas_call x2, Pallas kernels, attend(): pl.pallas_call(functools.partial(attend_kernel, tiles, index, inner), out...  10.2 us
    ppermute x6, starting transfers between devices, move(): lax.ppermute(value, 'ctx', [p[::-1] for p in pairs] if back else pairs)  6.06 us
    ppermute x2, starting transfers between devices, swap(): return lax.ppermute(x, 'head', [(0, 1), (1, 0)])  3.15 us
    dynamic_slice x2, local copies, waits for them, and re-layouts, half(): return lax.dynamic_slice_in_dim(x, index * width, width, 1)  1.98 us
    ppermute x2, waiting for transfers between devices, swap(): return lax.ppermute(x, 'head', [(0, 1), (1, 0)])  0.98 us
    pallas_call x1, Pallas kernels, masks(): pl.pallas_call(functools.partial(mask_kernel, lead), out_shape=[pltpu.VME...  0.73 us
  transfers between devices with their start and end apart: 8, of which 6 were waited for; matrix products, arithmetic and copies ran while one was open for 4% of the time, Pallas kernels for 16%

profile of v5, /device:TPU:0, one launch (start us, length us, event | category | flops | bytes accessed | tf_op | source)
XLA Modules:
  0.0 35.6 jit_solution(15908918566201426429)
XLA Ops:
  0.6 0.8 %constant_dynamic-slice_fusion.2 = (bf16[128,128]{1,0:T(8,128)(2,1)S(1)}, bf16[128,128]{1,0:T(8,128)(2,1)S(1)}, bf16[128,128]{1,0:T(8,128)(2,1)S(1)}, bf16[128,128]{1,0:T(8,128)(2,1)S(1)}) fusion(bf16[128,256]{1,0:T(8,128)(2,1)} %param.7, s32[]{:T(128)S(6)} %select_n.13, s32[]{:T(128)S(6)} %select_n.14, bf16[128,256]{1,0:T(8,128)(2,1)} %param.6), kind=kLoop, calls=%fused_computation.6 | loop fusion | bytes 262152 | tf_op jit(solution)/shard_map/dynamic_slice | solution.py:294
  1.5 3.0 %collective-permute-start.1 = (bf16[128,256]{1,0:T(8,128)(2,1)S(1)}, bf16[128,256]{1,0:T(8,128)(2,1)S(1)}, u32[]{:S(2)}, u32[]{:S(2)}) collective-permute-start(bf16[128,256]{1,0:T(8,128)(2,1)S(1)} %pad_maximum_fusion.2), channel_id=1, source_target_pairs={{0,1},{1,0},{2,3},{3,2},{4,5},{5,4},{6,7},{7,6},{8,9},{9,8},{10,11... | collective-permute-start | bytes 196616 | tf_op jit(solution)/shard_map/ppermute | solution.py:300
  4.5 0.0 copy-start.2
  4.5 0.0 copy-start
  4.5 0.0 copy-start.1
  4.5 1.2 %constant_dynamic-slice_fusion.4 = (bf16[128,1024]{1,0:T(8,128)(2,1)S(1)}, bf16[128,1024]{1,0:T(8,128)(2,1)S(1)}) fusion(bf16[128,2048]{1,0:T(8,128)(2,1)} %refs_1_.1, s32[]{:T(128)S(6)} %select_n.12, bf16[128,2048]{1,0:T(8,128)(2,1)} %refs_0_.1), kind=kLoop, calls=%fused_computation.8 | loop fusion | bytes 1048580 | tf_op jit(solution)/shard_map/dynamic_slice | solution.py:294
  5.7 0.1 collective-permute-start
  5.8 1.0 %collective-permute-done.1 = bf16[128,256]{1,0:T(8,128)(2,1)S(1)} collective-permute-done((bf16[128,256]{1,0:T(8,128)(2,1)S(1)}, bf16[128,256]{1,0:T(8,128)(2,1)S(1)}, u32[]{:S(2)}, u32[]{:S(2)}) %collective-permute-start.1) | collective-permute-done | bytes 65568 | tf_op jit(solution)/shard_map/ppermute | solution.py:300
  6.8 2.0 %collective-permute-start.2 = (bf16[256,256]{1,0:T(8,128)(2,1)S(1)}, bf16[256,256]{1,0:T(8,128)(2,1)S(1)}, u32[]{:S(2)}, u32[]{:S(2)}) collective-permute-start(bf16[256,256]{1,0:T(8,128)(2,1)S(1)} %pad_maximum_fusion.1.refs_3_.refs_2_), channel_id=1, source_target_pairs={{0,4},{2,6},{4,8},{6,10},{8,12},{10,14},{12,16},{14,18},{16,20},{1... | collective-permute-start | bytes 393224 | tf_op jit(solution)/shard_map/ppermute | solution.py:269
  8.9 0.0 copy-done.2
  8.9 0.1 pad_add_fusion.info
  9.0 0.7 %masks.1 = (f32[896,128]{1,0:T(8,128)S(1)}, f32[896,128]{1,0:T(8,128)S(1)}) custom-call(s32[34]{0:T(128)S(1)} %pad_add_fusion.info), custom_call_target="tpu_custom_call" | custom-call | tf_op jit(solution)/shard_map/masks/pallas_call | solution.py:192
  9.7 0.1 collective-permute-start.3
  9.8 5.1 %collective-permute-done.2.refs_5_.refs_4_ = bf16[256,256]{1,0:T(8,128)(2,1)S(1)} collective-permute-done((bf16[256,256]{1,0:T(8,128)(2,1)S(1)}, bf16[256,256]{1,0:T(8,128)(2,1)S(1)}, u32[]{:S(2)}, u32[]{:S(2)}) %collective-permute-start.2) | collective-permute-done | bytes 131104 | tf_op jit(solution)/shard_map/ppermute | solution.py:269
  14.9 0.0 collective-permute-start.4
  14.9 1.1 %collective-permute-done.3.refs_4_.refs_3_ = bf16[256,256]{1,0:T(8,128)(2,1)S(1)} collective-permute-done((bf16[256,256]{1,0:T(8,128)(2,1)S(1)}, bf16[256,256]{1,0:T(8,128)(2,1)S(1)}, u32[]{:S(2)}, u32[]{:S(2)}) %collective-permute-start.3) | collective-permute-done | bytes 131104 | tf_op jit(solution)/shard_map/ppermute | solution.py:269
  15.9 0.3 collective-permute-done.4.refs_6_.refs_5_
  16.2 0.0 copy-done
  16.2 0.0 copy-done.1
  16.2 5.0 %attend_first.1 = (bf16[256,1024]{1,0:T(8,128)(2,1)}, bf16[256,1024]{1,0:T(8,128)(2,1)}, f32[1152,256]{1,0:T(8,128)S(1)}) custom-call(s32[34]{0:T(128)S(1)} %pad_add_fusion.info, bf16[128,2048]{1,0:T(8,128)(2,1)S(1)} %copy-done.1, bf16[128,2048]{1,0:T(8,128)(2,1)S(1)} %copy-done, f32[896,128]{1,0:T(8,128)S(1)} %get-tuple-element.24.refs_2_, ...), custom_call_target="tpu_custom_call" | custom-call | flops 1409286144 | bytes 2097152 | tf_op jit(solution)/shard_map/attend_first/pallas_call | solution.py:228
  21.2 0.0 collective-permute-done.refs_0_
  21.2 5.2 %attend_last.1 = (bf16[256,1024]{1,0:T(8,128)(2,1)}, bf16[256,1024]{1,0:T(8,128)(2,1)}, f32[256,256]{1,0:T(8,128)S(1)}, bf16[256,256]{1,0:T(8,128)(2,1)S(1)}, f3...) custom-call(s32[34]{0:T(128)S(1)} %pad_add_fusion.info, ...), custom_call_target="tpu_custom_call", output_to_operand_aliasing={{0}: (8, {}), {1}: (9, {})} | custom-call | flops 1409286144 | bytes 2097152 | tf_op jit(solution)/shard_map/attend_last/pallas_call | solution.py:228
  26.4 0.2 collective-permute-start.6
  26.7 3.0 %collective-permute-start.5 = (bf16[256,256]{1,0:T(8,128)(2,1)S(1)}, bf16[256,256]{1,0:T(8,128)(2,1)S(1)}, u32[]{:S(2)}, u32[]{:S(2)}) collective-permute-start(bf16[256,256]{1,0:T(8,128)(2,1)S(1)} %get-tuple-element.31), channel_id=1, source_target_pairs={{2,0},{8,2},{6,4},{12,6},{10,8},{16,10},{14,12},{20,14},{18,16},{2... | collective-permute-start | bytes 393224 | tf_op jit(solution)/shard_map/ppermute | solution.py:269
  29.6 0.0 collective-permute-done.6
  29.7 0.8 %collective-permute-start.7 = (bf16[256,256]{1,0:T(8,128)(2,1)S(1)}, bf16[256,256]{1,0:T(8,128)(2,1)S(1)}, u32[]{:S(2)}, u32[]{:S(2)}) collective-permute-start(bf16[256,256]{1,0:T(8,128)(2,1)S(1)} %add_convert_fusion), channel_id=1, source_target_pairs={{4,0},{6,2},{8,4},{10,6},{12,8},{14,10},{16,12},{18,14},{20,16},{2... | collective-permute-start | bytes 393224 | tf_op jit(solution)/shard_map/ppermute | solution.py:269
  30.4 3.1 %collective-permute-done.5.refs_0_ = bf16[256,256]{1,0:T(8,128)(2,1)S(1)} collective-permute-done((bf16[256,256]{1,0:T(8,128)(2,1)S(1)}, bf16[256,256]{1,0:T(8,128)(2,1)S(1)}, u32[]{:S(2)}, u32[]{:S(2)}) %collective-permute-start.5) | collective-permute-done | bytes 131104 | tf_op jit(solution)/shard_map/ppermute | solution.py:269
  33.5 1.4 %collective-permute-done.7.refs_1_ = bf16[256,256]{1,0:T(8,128)(2,1)S(1)} collective-permute-done((bf16[256,256]{1,0:T(8,128)(2,1)S(1)}, bf16[256,256]{1,0:T(8,128)(2,1)S(1)}, u32[]{:S(2)}, u32[]{:S(2)}) %collective-permute-start.7) | collective-permute-done | bytes 131104 | tf_op jit(solution)/shard_map/ppermute | solution.py:269
  34.9 0.7 %gather.1 = (bf16[256,128]{1,0:T(8,128)(2,1)}, bf16[256,128]{1,0:T(8,128)(2,1)}) custom-call(f32[256,256]{1,0:T(8,128)S(1)} %get-tuple-element.30.own_ref, bf16[256,256]{1,0:T(8,128)(2,1)S(1)} %collective-permute-done.5.refs_0_, bf16[256,256]{1,0:T(8,128)(2,1)S(1)} %collective-permute-done.7.refs_1_), custom_call_target="tpu_custom_call" | custom-call | tf_op jit(solution)/shard_map/gather/pallas_call | solution.py:317
  (4 shorter events, 0.1 us)
Async XLA Ops:
  1.5 5.3 %collective-permute-start.1 = (bf16[128,256]{1,0:T(8,128)(2,1)S(1)}, bf16[128,256]{1,0:T(8,128)(2,1)S(1)}, u32[]{:S(2)}, u32[]{:S(2)}) collective-permute-start(bf16[128,256]{1,0:T(8,128)(2,1)S(1)} %pad_maximum_fusion.2), channel_id=1, source_target_pairs={{0,1},{1,0},{2,3},{3,2},{4,5},{5,4},{6,7},{7,6},{8,9},{9,8},{10,11... | collective-permute-start | bytes 196616 | tf_op jit(solution)/shard_map/ppermute | solution.py:300
  4.5 4.4 %copy-start.2 = (s32[32]{0:T(128)S(1)}, s32[32]{0:T(128)}, u32[]{:S(2)}) copy-start(s32[32]{0:T(128)} %param.9) | copy-start | bytes 388
  4.5 11.7 %copy-start = (bf16[128,2048]{1,0:T(8,128)(2,1)S(1)}, bf16[128,2048]{1,0:T(8,128)(2,1)}, u32[]{:S(2)}) copy-start(bf16[128,2048]{1,0:T(8,128)(2,1)} %refs_1_.1) | copy-start | bytes 1572868
  4.5 11.7 %copy-start.1 = (bf16[128,2048]{1,0:T(8,128)(2,1)S(1)}, bf16[128,2048]{1,0:T(8,128)(2,1)}, u32[]{:S(2)}) copy-start(bf16[128,2048]{1,0:T(8,128)(2,1)} %refs_0_.1) | copy-start | bytes 1572868
  5.7 15.5 %collective-permute-start = (bf16[128,2048]{1,0:T(8,128)(2,1)S(1)}, bf16[128,2048]{1,0:T(8,128)(2,1)S(1)}, u32[]{:S(2)}, u32[]{:S(2)}) collective-permute-start(bf16[128,2048]{1,0:T(8,128)(2,1)S(1)} %pad_maximum_fusion), channel_id=1, source_target_pairs={{0,1},{1,0},{2,3},{3,2},{4,5},{5,4},{6,7},{7,6},{8,9},{9,8},{10,11... | collective-permute-start | bytes 1572872 | tf_op jit(solution)/shard_map/ppermute | solution.py:300
  6.8 8.0 %collective-permute-start.2 = (bf16[256,256]{1,0:T(8,128)(2,1)S(1)}, bf16[256,256]{1,0:T(8,128)(2,1)S(1)}, u32[]{:S(2)}, u32[]{:S(2)}) collective-permute-start(bf16[256,256]{1,0:T(8,128)(2,1)S(1)} %pad_maximum_fusion.1.refs_3_.refs_2_), channel_id=1, source_target_pairs={{0,4},{2,6},{4,8},{6,10},{8,12},{10,14},{12,16},{14,18},{16,20},{1... | collective-permute-start | bytes 393224 | tf_op jit(solution)/shard_map/ppermute | solution.py:269
  9.7 6.2 %collective-permute-start.3 = (bf16[256,256]{1,0:T(8,128)(2,1)S(1)}, bf16[256,256]{1,0:T(8,128)(2,1)S(1)}, u32[]{:S(2)}, u32[]{:S(2)}) collective-permute-start(bf16[256,256]{1,0:T(8,128)(2,1)S(1)} %pad_maximum_fusion.1.refs_3_.refs_2_), channel_id=1, source_target_pairs={{0,2},{2,8},{4,6},{6,12},{8,10},{10,16},{12,14},{14,20},{16,18},{1... | collective-permute-start | bytes 393224 | tf_op jit(solution)/shard_map/ppermute | solution.py:269
  14.9 1.3 %collective-permute-start.4 = (bf16[256,256]{1,0:T(8,128)(2,1)S(1)}, bf16[256,256]{1,0:T(8,128)(2,1)S(1)}, u32[]{:S(2)}, u32[]{:S(2)}) collective-permute-start(bf16[256,256]{1,0:T(8,128)(2,1)S(1)} %collective-permute-done.2.refs_5_.refs_4_), channel_id=1, source_target_pairs={{0,2},{2,0},{4,6},{6,4},{8,10},{10,8},{12,14},{14,12},{16,18},{18,... | collective-permute-start | bytes 393224 | tf_op jit(solution)/shard_map/ppermute | solution.py:269
  26.4 3.2 %collective-permute-start.6 = (bf16[256,256]{1,0:T(8,128)(2,1)S(1)}, bf16[256,256]{1,0:T(8,128)(2,1)S(1)}, u32[]{:S(2)}, u32[]{:S(2)}) collective-permute-start(bf16[256,256]{1,0:T(8,128)(2,1)S(1)} %get-tuple-element.33), channel_id=1, source_target_pairs={{2,0},{0,2},{6,4},{4,6},{10,8},{8,10},{14,12},{12,14},{18,16},{16,... | collective-permute-start | bytes 393224 | tf_op jit(solution)/shard_map/ppermute | solution.py:269
  26.7 6.8 %collective-permute-start.5 = (bf16[256,256]{1,0:T(8,128)(2,1)S(1)}, bf16[256,256]{1,0:T(8,128)(2,1)S(1)}, u32[]{:S(2)}, u32[]{:S(2)}) collective-permute-start(bf16[256,256]{1,0:T(8,128)(2,1)S(1)} %get-tuple-element.31), channel_id=1, source_target_pairs={{2,0},{8,2},{6,4},{12,6},{10,8},{16,10},{14,12},{20,14},{18,16},{2... | collective-permute-start | bytes 393224 | tf_op jit(solution)/shard_map/ppermute | solution.py:269
  29.7 5.2 %collective-permute-start.7 = (bf16[256,256]{1,0:T(8,128)(2,1)S(1)}, bf16[256,256]{1,0:T(8,128)(2,1)S(1)}, u32[]{:S(2)}, u32[]{:S(2)}) collective-permute-start(bf16[256,256]{1,0:T(8,128)(2,1)S(1)} %add_convert_fusion), channel_id=1, source_target_pairs={{4,0},{6,2},{8,4},{10,6},{12,8},{14,10},{16,12},{18,14},{20,16},{2... | collective-permute-start | bytes 393224 | tf_op jit(solution)/shard_map/ppermute | solution.py:269

commit v6 on v5

v6 whole, which is shorter than its diff:
```python
import functools
import math

import jax
import jax.numpy as jnp
from jax import lax
from jax.experimental import pallas as pl
from jax.experimental.pallas import tpu as pltpu
from jax.sharding import PartitionSpec as P

WIN = 4
HEADS = 2
MASKED = -1e30
NT = (((1,), (1,)), ((), ()))
NN = (((1,), (0,)), ((), ()))
WHOLE = pl.BlockSpec(memory_space=pltpu.VMEM)
ANY = pl.BlockSpec(memory_space=pl.ANY)
SCALARS = pl.BlockSpec(memory_space=pltpu.SMEM)
BF16, F32 = jnp.bfloat16, jnp.float32

OWN, A, B, C = range(WIN)
SLOTS = {1: ((OWN, 0), (B, 0), (A, 0), (C, 0)), 2: ((OWN, None), (B, 1), (B, 0), (A, 1), (A, 0), (C, 1), (C, 0))}
EARLY = 5


def in_vmem(*arrays):
    return [pltpu.with_memory_space_constraint(x, pltpu.VMEM) for x in arrays]


def dot(a, b, dims):
    return lax.dot_general(a, b, dims, preferred_element_type=F32)


def fold(x, op):
    return op(x.reshape(x.shape[0] // 8, 8, x.shape[1]), axis=0)


def distances(info):
    odd = info[0] & 1
    return {OWN: 0, A: 3 - 2 * odd, B: 2, C: 1 + 2 * odd}


def moved(info, tile, shard):
    if shard not in (A, C):
        return None
    odd = info[0] & 1
    return (tile == 1) & (odd == (1 if shard == C else 0))


def tile_of(info, tiles, index):
    return index ^ info[1] if tiles == 2 else index


def stored(info, tiles, part):
    return part ^ info[1] if tiles == 2 else part


def mask_kernel(shard, info, *bias_refs):
    tiles = len(bias_refs)
    part = shard // tiles
    back = distances(info)
    for index, bias_ref in enumerate(bias_refs):
        tile = tile_of(info, tiles, index)
        first = info[0] * shard + tile * part
        query = first + lax.broadcasted_iota(jnp.int32, (1, part), 1)
        low = jnp.zeros((1, part), jnp.int32)
        start = jnp.int32(0)
        for d in range(info.shape[0] - 2):
            low = jnp.where(query >= start, start, low)
            start = start + info[2 + d]
        for slot, (s, j) in enumerate(SLOTS[tiles]):
            at = (info[0] - back[s]) * shard + (tile if j is None else j) * part
            if tiles == 2 and j == 0 and moved(info, tile, s) is not None:
                at = jnp.where(moved(info, tile, s), info[0] * shard, at)
            key = at + lax.broadcasted_iota(jnp.int32, (part, part), 0)
            ok = (key >= low) & (key <= query)
            bias_ref[slot * part : (slot + 1) * part, :] = jnp.where(ok, 0.0, MASKED)


def fill(info, tiles, tile, shard_refs, slots, k_ref=None, v_ref=None):
    shard, width = shard_refs[0].shape
    part, hd = shard // tiles, width // 2

    def rows(s, j):
        return shard_refs[s][pl.ds(pl.multiple_of(stored(info, tiles, j) * part, part), part), :]

    for slot in slots:
        s, j = SLOTS[tiles][slot]
        x = rows(s, tile if j is None else j)
        if tiles == 2 and j == 0 and moved(info, tile, s) is not None:
            x = jnp.where(moved(info, tile, s), rows(OWN, 0), x)
        at = slice(slot * part, (slot + 1) * part)
        if k_ref is not None:
            k_ref[at, :] = x[:, :hd]
        if v_ref is not None:
            v_ref[at, :] = x[:, hd:]


def by_heads(info, sources, columns, rows, hd, *targets):
    if len(sources) == 1:
        places = [(sources[0], 0), (sources[0], columns)]
    else:
        mine = pl.multiple_of(info[1] * columns, 128)
        places = [(source, mine) for source in sources]
    for (source, start), target in zip(places, targets):
        for h in range(columns // hd):
            target[h * rows : (h + 1) * rows, :] = source[:, pl.ds(start + h * hd, hd)]


def scores_of(k, q, bias):
    s = dot(k, q, NT) + jnp.concatenate([bias] * HEADS, axis=1)
    return s, jnp.max(fold(s, jnp.max), axis=0, keepdims=True)


def early_kernel(info, q_ref, do_ref, bias_ref, *refs):
    shard_refs, (e_ref, dp_ref, top_ref, sum_ref, k_ref, v_ref, q_rows, do_rows) = refs[:3], refs[3:]
    rows = bias_ref.shape[1]
    hd = k_ref.shape[1]
    early = e_ref.shape[0]
    n = HEADS * rows
    log2e = math.log2(math.e) / math.sqrt(hd)
    fill(info, 2, tile_of(info, 2, 0), shard_refs, range(EARLY), k_ref, v_ref)
    by_heads(info, (q_ref, do_ref), q_ref.shape[1] // 2, rows, hd, q_rows, do_rows)
    pairs = q_rows.shape[0] // n
    sc = scores_of(k_ref[...], q_rows[:n, :], bias_ref[:early, :])
    for p in range(pairs):
        at = slice(p * n, (p + 1) * n)
        s, top = sc
        if p + 1 < pairs:
            sc = scores_of(k_ref[...], q_rows[(p + 1) * n : (p + 2) * n, :], bias_ref[:early, :])
        dp_ref[:, at] = dot(v_ref[...], do_rows[at, :], NT)
        e = jnp.exp2((s - top) * log2e)
        e_ref[:, at] = e
        top_ref[:, at] = top
        sum_ref[:, at] = jnp.sum(fold(e, jnp.sum), axis=0, keepdims=True)


def attend_kernel(tiles, index, info, *refs):
    last = index == tiles - 1
    ahead = not last
    sources, refs = (refs[:2], refs[2:]) if ahead else (refs[:1], refs[1:])
    bias_ref, *refs = refs
    shard_refs, refs = refs[:WIN], refs[WIN:]
    acc_refs = []
    if ahead:
        (e_early, dp_early, top_early, sum_early), refs = refs[:4], refs[4:]
    if index:
        acc_refs, refs = [refs[0]], refs[2:]
    out_hbm, ds_ref, *refs = refs
    if last:
        grad_refs, refs = refs[:WIN], refs[WIN:]
        acc_refs.append(refs[0])
    else:
        acc_refs.append(refs[0])
    acc_ref, k_ref, v_ref, vt_ref, q_rows, do_rows, p_ref, out_ref, sem = refs

    shard, width = shard_refs[0].shape
    hd = width // 2
    keys, rows = bias_ref.shape
    columns = out_hbm.shape[1]
    pairs = columns // hd // HEADS
    part = shard // tiles
    tile = tile_of(info, tiles, index)
    n = HEADS * rows
    early = EARLY * part if ahead else 0
    log2e = math.log2(math.e) / math.sqrt(hd)
    scaling = 1 / math.sqrt(hd)
    fill(info, tiles, tile, shard_refs, range(len(SLOTS[tiles])), k_ref, v_ref)
    by_heads(info, sources, columns, rows, hd, q_rows, do_rows)
    vt_ref[...] = v_ref[...].T

    def at(p):
        return slice(p * n, (p + 1) * n)

    def scores(p):
        return scores_of(k_ref[early:, :], q_rows[at(p), :], bias_ref[early:, :])

    def weights(p, s, top):
        if ahead:
            before = top_early[:, at(p)]
            top = jnp.maximum(top, before)
            rescale = jnp.exp2((before - top) * log2e)
        e = jnp.exp2((s - top) * log2e)
        total = jnp.sum(fold(e, jnp.sum), axis=0, keepdims=True)
        if ahead:
            total = total + sum_early[:, at(p)] * rescale
        inverse = 1.0 / total
        p_f32 = e * inverse
        p_ref[early:, at(p)] = p_f32.astype(BF16)
        if ahead:
            first = e_early[:, at(p)] * (rescale * inverse)
            p_ref[:early, at(p)] = first.astype(BF16)
            return first, p_f32
        return (p_f32,)

    def outputs(p):
        out = dot(vt_ref[...], p_ref[:, at(p)], NN).astype(BF16)
        do_t = do_rows[at(p), :].T.astype(F32)
        delta = jnp.sum(do_t * out.astype(F32), axis=0, keepdims=True)
        for i in range(HEADS):
            h = p * HEADS + i
            out_ref[:, h * hd : (h + 1) * hd] = out[:, i * rows : (i + 1) * rows].T
        here = slice(p * HEADS * hd, (p + 1) * HEADS * hd)
        place = pl.ds(pl.multiple_of(tile * rows, rows), rows)
        copy = pltpu.make_async_copy(out_ref.at[:, here], out_hbm.at[place, here], sem.at[p])
        copy.start()
        stores.append(copy)
        return delta

    def dprobs(p):
        return dot(v_ref[early:, :], do_rows[at(p), :], NT)

    def dscores(p, w, dp, delta):
        if ahead:
            ds_ref[:early, at(p)] = (w[0] * (dp_early[:, at(p)] - delta)).astype(BF16)
        ds_ref[early:, at(p)] = (w[-1] * (dp - delta)).astype(BF16)

    def sums(p):
        dk, dv = dot(ds_ref[:, at(p)], q_rows[at(p), :], NN), dot(p_ref[:, at(p)], do_rows[at(p), :], NN)
        if p:
            acc_ref[:, :hd] += dk
            acc_ref[:, hd:] += dv
        else:
            acc_ref[:, :hd], acc_ref[:, hd:] = dk, dv

    stores = []
    w = weights(0, *scores(0))
    for p in range(pairs):
        following = scores(p + 1) if p + 1 < pairs else None
        dp = dprobs(p)
        delta = outputs(p)
        if p:
            sums(p - 1)
        nw = weights(p + 1, *following) if p + 1 < pairs else None
        dscores(p, w, dp, delta)
        w = nw
    sums(pairs - 1)
    if last:

        def give(ref, row, x):
            where = pl.ds(pl.multiple_of(row * part, part), part)
            ref[where, :hd] = (x[:, :hd] * scaling).astype(ref.dtype)
            ref[where, hd:] = x[:, hd:].astype(ref.dtype)

        parts = [[acc[slot * part : (slot + 1) * part, :] for acc in acc_refs] for slot in range(len(SLOTS[tiles]))]
        own = list(parts[0])
        for (s, j), xs in list(zip(SLOTS[tiles], parts))[1:]:
            if tiles == 2 and j == 0 and s in (A, C):
                for i, x in enumerate(xs):
                    keep = jnp.where(moved(info, tile_of(info, tiles, i), s), 0.0, 1.0)
                    own[1 - i] = own[1 - i] + x * (1.0 - keep)
                    xs[i] = x * keep
            give(grad_refs[s], stored(info, tiles, j), sum(xs[1:], xs[0]))
        for i, x in enumerate(own):
            give(grad_refs[OWN], i, x)
    for copy in stores:
        copy.wait()


def queries_kernel(tiles, info, *refs):
    shard_refs, refs = refs[:WIN], refs[WIN:]
    ds_refs, (dq_hbm, k_ref, kt_ref, dq_ref, sem) = refs[:tiles], refs[tiles:]
    hd, keys = kt_ref.shape
    rows = dq_hbm.shape[0] // tiles
    n = HEADS * rows
    width = HEADS * hd
    stores = []
    for index, ds_ref in enumerate(ds_refs):
        tile = tile_of(info, tiles, index)
        fill(info, tiles, tile, shard_refs, range(len(SLOTS[tiles])), k_ref)
        kt_ref[...] = k_ref[...].T
        for p in range(ds_ref.shape[1] // n):
            dq = (dot(kt_ref[...], ds_ref[:, p * n : (p + 1) * n], NN) * (1 / math.sqrt(hd))).astype(BF16)
            for i in range(HEADS):
                here = slice(p * width + i * hd, p * width + (i + 1) * hd)
                dq_ref[index * rows : (index + 1) * rows, here] = dq[:, i * rows : (i + 1) * rows].T
            here = slice(p * width, (p + 1) * width)
            place = pl.ds(pl.multiple_of(tile * rows, rows), rows)
            source = dq_ref.at[index * rows : (index + 1) * rows, here]
            copy = pltpu.make_async_copy(source, dq_hbm.at[place, here], sem.at[len(stores)])
            copy.start()
            stores.append(copy)
    for copy in stores:
        copy.wait()


def params(mib):
    return pltpu.CompilerParams(vmem_limit_bytes=mib << 20)


def masks(info, shard, tiles):
    part = shard // tiles
    return pl.pallas_call(
        functools.partial(mask_kernel, shard),
        out_shape=[pltpu.VMEM((len(SLOTS[tiles]) * part, part), F32)] * tiles,
        in_specs=[SCALARS],
        out_specs=[WHOLE] * tiles,
        compiler_params=params(4),
        name="masks",
    )(info)


def early(info, queries, d_out, bias, shards, columns):
    shard, width = shards[0].shape
    part, hd = shard // 2, width // 2
    all_rows = columns // hd * part
    keys = EARLY * part
    row = pltpu.VMEM((1, all_rows), F32)
    return pl.pallas_call(
        early_kernel,
        out_shape=[pltpu.VMEM((keys, all_rows), F32)] * 2 + [row, row],
        in_specs=[SCALARS] + [WHOLE] * 6,
        out_specs=[WHOLE] * 4,
        scratch_shapes=[pltpu.VMEM((keys, hd), BF16)] * 2 + [pltpu.VMEM((all_rows, hd), BF16)] * 2,
        compiler_params=params(16),
        cost_estimate=pl.CostEstimate(
            flops=4 * keys * all_rows * hd, transcendentals=keys * all_rows, bytes_accessed=1 << 21
        ),
        name="early",
    )(info, *in_vmem(queries, d_out, bias, *shards))


def attend(info, q_do, bias, shards, prepared, before, tiles, columns):
    shard, width = shards[0].shape
    hd = width // 2
    index = 0 if before is None else 1
    last = index == tiles - 1
    keys, rows = bias.shape
    all_rows = columns // hd * rows
    acc = pltpu.VMEM((keys, width), F32)
    args = [info, *in_vmem(*q_do, bias, *shards, *prepared)]
    in_specs = [SCALARS] + [WHOLE] * (len(args) - 1)
    aliases = {}
    if before is not None:
        aliases = {len(args) + 1: 0}
        args += [*in_vmem(before[0]), before[1]]
        in_specs += [WHOLE, ANY]
    out_shape = [jax.ShapeDtypeStruct((shard, columns), BF16), pltpu.VMEM((keys, all_rows), BF16)]
    if last:
        out_shape += [pltpu.VMEM((shard, width), d) for d in (F32, BF16, F32, BF16)]
    else:
        out_shape += [acc]
    return pl.pallas_call(
        functools.partial(attend_kernel, tiles, index),
        out_shape=out_shape,
        in_specs=in_specs,
        out_specs=[ANY] + [WHOLE] * (len(out_shape) - 1),
        scratch_shapes=[
            *([acc] if last else []),
            pltpu.VMEM((keys, hd), BF16),
            pltpu.VMEM((keys, hd), BF16),
            pltpu.VMEM((hd, keys), BF16),
            pltpu.VMEM((all_rows, hd), BF16),
            pltpu.VMEM((all_rows, hd), BF16),
            pltpu.VMEM((keys, all_rows), BF16),
            pltpu.VMEM((rows, columns), BF16),
            pltpu.SemaphoreType.DMA((columns // hd // HEADS,)),
        ],
        input_output_aliases=aliases,
        compiler_params=params(24),
        cost_estimate=pl.CostEstimate(
            flops=10 * keys * rows * columns, transcendentals=keys * all_rows, bytes_accessed=1 << 21
        ),
        name="attend_last" if last else "attend_first",
    )(*args)


def query_gradients(info, shards, dscores, columns):
    shard, width = shards[0].shape
    tiles = len(dscores)
    hd, keys = width // 2, dscores[0].shape[0]
    return pl.pallas_call(
        functools.partial(queries_kernel, tiles),
        out_shape=jax.ShapeDtypeStruct((shard, columns), BF16),
        in_specs=[SCALARS] + [WHOLE] * (WIN + tiles),
        out_specs=ANY,
        scratch_shapes=[
            pltpu.VMEM((keys, hd), BF16),
            pltpu.VMEM((hd, keys), BF16),
            pltpu.VMEM((shard, columns), BF16),
            pltpu.SemaphoreType.DMA((tiles * (columns // hd // HEADS),)),
        ],
        compiler_params=params(12),
        cost_estimate=pl.CostEstimate(flops=2 * keys * shard * columns, transcendentals=0, bytes_accessed=1 << 21),
        name="query_gradients",
    )(info, *in_vmem(*shards, *dscores))


def gather_kernel(own_ref, *refs):
    total = own_ref[...]
    for r in refs[:-2]:
        total = total + r[...].astype(F32)
    hd = refs[-1].shape[1]
    refs[-2][...] = total[:, :hd].astype(BF16)
    refs[-1][...] = total[:, hd:].astype(BF16)


def in_order_kernel(info, own_ref, *refs):
    near, (k_ref, v_ref) = refs[:-2], refs[-2:]
    shard, hd = k_ref.shape
    part = shard // 2
    total = own_ref[...]
    for r in near:
        total = total + r[...].astype(F32)
    for j in range(2):
        to = pl.ds(pl.multiple_of((j ^ info[1]) * part, part), part)
        k_ref[to, :] = total[j * part : (j + 1) * part, :hd].astype(BF16)
        v_ref[to, :] = total[j * part : (j + 1) * part, hd:].astype(BF16)


def move(value, kind, back=False):
    count = lax.axis_size("ctx")
    steps = {A: lambda i: 3 if i % 2 else 1, B: lambda i: 2, C: lambda i: -1 if i % 2 else 1}[kind]
    pairs = [(i, (i + steps(i)) % count) for i in range(count)]
    return lax.ppermute(value, "ctx", [p[::-1] for p in pairs] if back else pairs)


def window(own, bias):
    b = move(own, B)
    a = move(own, A)
    b, *bias = lax.optimization_barrier((b, *bias))
    return [own, a, b, move(b, C)], bias


def body(queries, keys, values, d_out, doc_lengths):
    count = lax.axis_size("head")
    head = lax.axis_index("head")
    shard = count * queries.shape[0]
    hd = keys.shape[1] // count
    columns = queries.shape[1] // count
    info = jnp.concatenate([jnp.stack([lax.axis_index("ctx"), head]).astype(jnp.int32), doc_lengths])
    tiles = 2 if count == 2 else 1
    bias = masks(info, shard, tiles)
    if tiles == 2:
        other = 1 - head

        def half(x, index):
            width = x.shape[1] // 2
            return lax.dynamic_slice_in_dim(x, index * width, width, 1)

        def key_value(index):
            return jnp.concatenate([half(keys, index), half(values, index)], axis=1)

        def swap(x):
            return lax.ppermute(x, "head", [(0, 1), (1, 0)])

        own = jnp.concatenate([key_value(head), swap(key_value(other))], axis=0)
        both = swap(jnp.concatenate([half(queries, other), half(d_out, other)], axis=1))
        shards, bias = window(own, bias)
        prepared = early(info, queries, d_out, bias[0], shards[:C], columns)
        out, ds_first, acc = attend(info, (queries, d_out), bias[0], shards, prepared, None, 2, columns)
        out, ds_last, *grads = attend(info, (both,), bias[1], shards, (), (acc, out), 2, columns)
        dscores = (ds_first, ds_last)
    else:
        swap = lambda x: lax.all_to_all(x, "head", split_axis=1, concat_axis=0, tiled=True)
        own = jnp.concatenate([swap(keys), swap(values)], axis=1)
        both = jnp.concatenate([swap(queries), swap(d_out)], axis=1)
        shards, bias = window(own, bias)
        out, ds_last, *grads = attend(info, (both,), bias[0], shards, (), None, 1, columns)
        dscores = (ds_last,)
    from_c = move(grads[C], C, True)
    near_a = move(grads[A], A, True)
    near_b = move((grads[B] + from_c.astype(F32)).astype(BF16), B, True)
    dq = query_gradients(info, shards, dscores, columns)
    ordered = [info] if tiles == 2 else []
    grad_keys, grad_values = pl.pallas_call(
        in_order_kernel if tiles == 2 else gather_kernel,
        out_shape=[jax.ShapeDtypeStruct((shard, hd), BF16)] * 2,
        in_specs=[SCALARS] * len(ordered) + [WHOLE] * 3,
        out_specs=[WHOLE] * 2,
        compiler_params=params(4),
        name="gather",
    )(*ordered, *in_vmem(grads[OWN], near_a, near_b))
    return out, dq, grad_keys, grad_values


def solution(mesh):
    rows = P(("ctx", "head"), None)
    return jax.shard_map(
        body,
        mesh=mesh,
        in_specs=(rows, rows, rows, rows, P()),
        out_specs=(P("ctx", "head"),) * 4,
        check_vma=False,
    )
```

time: 35.8 us -> 35.8 us (level)
  Pallas kernels: 11.6 us -> 15 us
  waiting for transfers between devices: 11.9 us -> 8.82 us
    pallas_call x4 -> x6, Pallas kernels: 11.6 us -> 15 us  [the longest x2 9.03 us: attend(): pl.pallas_call(functools.partial(attend_kernel, tiles, index), out_shape=...]
    ppermute x6, waiting for transfers between devices: 10.9 us -> 7.6 us  [move(): lax.ppermute(value, 'ctx', [p[::-1] for p in pairs] if back else pairs)]
  transfers between devices with their start and end apart: 8 -> 8, of which waited for: 6 -> 4; matrix products, arithmetic and copies ran while one was open for 4% -> 3% of each run, Pallas kernels for 16% -> 25%
where the time goes in v6:
time: 35.8 us; the launch traced here: 35.6 us
  Pallas kernels  15 us (42%)
  starting transfers between devices  8.91 us (25%)
  waiting for transfers between devices  8.82 us (25%)
  local copies, waits for them, and re-layouts  1.98 us (6%)
  between operations  0.77 us (2%)
    pallas_call x2, Pallas kernels, attend(): pl.pallas_call(functools.partial(attend_kernel, tiles, index), out_shape=...  9.03 us
    ppermute x6, waiting for transfers between devices, move(): lax.ppermute(value, 'ctx', [p[::-1] for p in pairs] if back else pairs)  7.6 us
    ppermute x6, starting transfers between devices, move(): lax.ppermute(value, 'ctx', [p[::-1] for p in pairs] if back else pairs)  5.79 us
    ppermute x2, starting transfers between devices, swap(): return lax.ppermute(x, 'head', [(0, 1), (1, 0)])  3.12 us
    pallas_call x1, Pallas kernels, query_gradients(): pl.pallas_call(functools.partial(queries_kernel, tiles), out_shape=jax.Sh...  2.13 us
    dynamic_slice x2, local copies, waits for them, and re-layouts, half(): return lax.dynamic_slice_in_dim(x, index * width, width, 1)  1.97 us
    pallas_call x1, Pallas kernels, early(): pl.pallas_call(early_kernel, out_shape=[pltpu.VMEM((keys, all_rows), F32)...  1.87 us
    pallas_call x1, Pallas kernels, body(): pl.pallas_call(in_order_kernel if tiles == 2 else gather_kernel, out_shap...  1.23 us
  transfers between devices with their start and end apart: 8, of which 4 were waited for; matrix products, arithmetic and copies ran while one was open for 3% of the time, Pallas kernels for 25%

profile of v6, /device:TPU:0, one launch (start us, length us, event | category | flops | bytes accessed | tf_op | source)
XLA Modules:
  0.0 35.6 jit_solution(15028615542183548579)
XLA Ops:
  0.6 0.0 copy-start.1
  0.6 0.0 copy-start
  0.7 0.0 copy-start.2
  0.7 0.9 %constant_dynamic-slice_fusion.2 = (bf16[128,128]{1,0:T(8,128)(2,1)S(1)}, bf16[128,128]{1,0:T(8,128)(2,1)S(1)}, bf16[128,128]{1,0:T(8,128)(2,1)S(1)}, bf16[128,128]{1,0:T(8,128)(2,1)S(1)}) fusion(bf16[128,256]{1,0:T(8,128)(2,1)} %param.7, s32[]{:T(128)S(6)} %select_n.13, s32[]{:T(128)S(6)} %select_n.14, bf16[128,256]{1,0:T(8,128)(2,1)} %param.6), kind=kLoop, calls=%fused_computation.6 | loop fusion | bytes 262152 | tf_op jit(solution)/shard_map/dynamic_slice | solution.py:439
  1.6 3.0 %collective-permute-start.1 = (bf16[128,256]{1,0:T(8,128)(2,1)S(1)}, bf16[128,256]{1,0:T(8,128)(2,1)S(1)}, u32[]{:S(2)}, u32[]{:S(2)}) collective-permute-start(bf16[128,256]{1,0:T(8,128)(2,1)S(1)} %pad_maximum_fusion.2), channel_id=1, source_target_pairs={{0,1},{1,0},{2,3},{3,2},{4,5},{5,4},{6,7},{7,6},{8,9},{9,8},{10,11... | collective-permute-start | bytes 196616 | tf_op jit(solution)/shard_map/ppermute | solution.py:445
  4.6 1.1 %constant_dynamic-slice_fusion.4 = (bf16[128,1024]{1,0:T(8,128)(2,1)S(1)}, bf16[128,1024]{1,0:T(8,128)(2,1)S(1)}) fusion(bf16[128,2048]{1,0:T(8,128)(2,1)} %refs_1_.1, s32[]{:T(128)S(6)} %select_n.12, bf16[128,2048]{1,0:T(8,128)(2,1)} %refs_0_.1), kind=kLoop, calls=%fused_computation.8 | loop fusion | bytes 1048580 | tf_op jit(solution)/shard_map/dynamic_slice | solution.py:439
  5.7 0.1 collective-permute-start
  5.8 1.2 %collective-permute-done.1 = bf16[128,256]{1,0:T(8,128)(2,1)S(1)} collective-permute-done((bf16[128,256]{1,0:T(8,128)(2,1)S(1)}, bf16[128,256]{1,0:T(8,128)(2,1)S(1)}, u32[]{:S(2)}, u32[]{:S(2)}) %collective-permute-start.1) | collective-permute-done | bytes 65568 | tf_op jit(solution)/shard_map/ppermute | solution.py:445
  7.1 1.9 %collective-permute-start.2 = (bf16[256,256]{1,0:T(8,128)(2,1)S(1)}, bf16[256,256]{1,0:T(8,128)(2,1)S(1)}, u32[]{:S(2)}, u32[]{:S(2)}) collective-permute-start(bf16[256,256]{1,0:T(8,128)(2,1)S(1)} %pad_maximum_fusion.1.refs_0_.refs_3_.refs_2_), channel_id=1, source_target_pairs={{0,4},{2,6},{4,8},{6,10},{8,12},{10,14},{12,16},{14,18},{16,20},{1... | collective-permute-start | bytes 393224 | tf_op jit(solution)/shard_map/ppermute | solution.py:415
  9.0 0.0 collective-permute-start.3
  9.0 0.0 copy-done.2
  9.0 0.1 pad_add_fusion.info
  9.1 0.7 %masks.1 = (f32[896,128]{1,0:T(8,128)S(1)}, f32[896,128]{1,0:T(8,128)S(1)}) custom-call(s32[34]{0:T(128)S(1)} %pad_add_fusion.info), custom_call_target="tpu_custom_call" | custom-call | tf_op jit(solution)/shard_map/masks/pallas_call | solution.py:293
  9.8 5.4 %collective-permute-done.2.refs_2_.refs_5_.refs_4_ = bf16[256,256]{1,0:T(8,128)(2,1)S(1)} collective-permute-done((bf16[256,256]{1,0:T(8,128)(2,1)S(1)}, bf16[256,256]{1,0:T(8,128)(2,1)S(1)}, u32[]{:S(2)}, u32[]{:S(2)}) %collective-permute-start.2) | collective-permute-done | bytes 131104 | tf_op jit(solution)/shard_map/ppermute | solution.py:415
  15.2 0.0 collective-permute-start.4
  15.2 0.0 collective-permute-done.3.refs_1_.refs_4_.refs_3_
  15.2 0.0 copy-done.1
  15.2 0.0 copy-done
  15.2 1.9 %early.1 = (f32[640,1024]{1,0:T(8,128)S(1)}, f32[640,1024]{1,0:T(8,128)S(1)}, f32[1,1024]{1,0:T(1,128)S(1)}, f32[1,1024]{1,0:T(1,128)S(1)}) custom-call(s32[34]{0:T(128)S(1)} %pad_add_fusion.info, bf16[128,2048]{1,0:T(8,128)(2,1)S(1)} %copy-done.1, bf16[128,2048]{1,0:T(8,128)(2,1)S(1)} %copy-done, f32[896,128]{1,0:T(8,128)S(1)} %get-tuple-element.28.bias_ref.refs_2_, ...), custom_call_target="tpu_custom_call" | custom-call | flops 335544320 | bytes 2097152 | tf_op jit(solution)/shard_map/early/pallas_call | solution.py:309
  17.1 0.0 collective-permute-done.4.refs_6_.refs_5_.refs_3_
  17.1 4.2 %attend_first.1 = (bf16[256,1024]{1,0:T(8,128)(2,1)}, bf16[896,1024]{1,0:T(8,128)(2,1)S(1)}, f32[896,256]{1,0:T(8,128)S(1)}) custom-call(s32[34]{0:T(128)S(1)} %pad_add_fusion.info, bf16[128,2048]{1,0:T(8,128)(2,1)S(1)} %copy-done.1, bf16[128,2048]{1,0:T(8,128)(2,1)S(1)} %copy-done, f32[896,128]{1,0:T(8,128)S(1)} %get-tuple-element.28.bias_ref.refs_2_, ...), custom_call_target="tpu_custom_call" | custom-call | flops 1174405120 | bytes 2097152 | tf_op jit(solution)/shard_map/attend_first/pallas_call | solution.py:343
  21.3 0.0 collective-permute-done.refs_0_
  21.3 4.8 %attend_last.1 = (bf16[256,1024]{1,0:T(8,128)(2,1)}, bf16[896,1024]{1,0:T(8,128)(2,1)S(1)}, f32[256,256]{1,0:T(8,128)S(1)}, bf16[256,256]{1,0:T(8,128)(2,1)S(1)}...) custom-call(s32[34]{0:T(128)S(1)} %pad_add_fusion.info, ...), custom_call_target="tpu_custom_call", output_to_operand_aliasing={{0}: (8, {})} | custom-call | flops 1174405120 | bytes 2097152 | tf_op jit(solution)/shard_map/attend_last/pallas_call | solution.py:343
  26.2 0.6 %collective-permute-start.6 = (bf16[256,256]{1,0:T(8,128)(2,1)S(1)}, bf16[256,256]{1,0:T(8,128)(2,1)S(1)}, u32[]{:S(2)}, u32[]{:S(2)}) collective-permute-start(bf16[256,256]{1,0:T(8,128)(2,1)S(1)} %get-tuple-element.41), channel_id=1, source_target_pairs={{2,0},{0,2},{6,4},{4,6},{10,8},{8,10},{14,12},{12,14},{18,16},{16,... | collective-permute-start | bytes 393224 | tf_op jit(solution)/shard_map/ppermute | solution.py:415
  26.8 2.3 %collective-permute-start.5 = (bf16[256,256]{1,0:T(8,128)(2,1)S(1)}, bf16[256,256]{1,0:T(8,128)(2,1)S(1)}, u32[]{:S(2)}, u32[]{:S(2)}) collective-permute-start(bf16[256,256]{1,0:T(8,128)(2,1)S(1)} %get-tuple-element.39), channel_id=1, source_target_pairs={{2,0},{8,2},{6,4},{12,6},{10,8},{16,10},{14,12},{20,14},{18,16},{2... | collective-permute-start | bytes 393224 | tf_op jit(solution)/shard_map/ppermute | solution.py:415
  29.1 0.0 collective-permute-done.6
  29.1 0.9 %collective-permute-start.7 = (bf16[256,256]{1,0:T(8,128)(2,1)S(1)}, bf16[256,256]{1,0:T(8,128)(2,1)S(1)}, u32[]{:S(2)}, u32[]{:S(2)}) collective-permute-start(bf16[256,256]{1,0:T(8,128)(2,1)S(1)} %add_convert_fusion), channel_id=1, source_target_pairs={{4,0},{6,2},{8,4},{10,6},{12,8},{14,10},{16,12},{18,14},{20,16},{2... | collective-permute-start | bytes 393224 | tf_op jit(solution)/shard_map/ppermute | solution.py:415
  30.1 2.1 %query_gradients.1 = bf16[256,1024]{1,0:T(8,128)(2,1)} custom-call(s32[34]{0:T(128)S(1)} %pad_add_fusion.info, bf16[256,256]{1,0:T(8,128)(2,1)S(1)} %pad_maximum_fusion.1.refs_0_.refs_3_.refs_2_, bf16[256,256]{1,0:T(8,128)(2,1)S(1)} %collective-permute-done.3.refs_1_.refs_4_.refs_3_, bf16[256,256]{1,0:T(8,128)(2,1)S(1)} %collective-permute-done.2.refs_2_.refs_5_.refs_4_, ...), custom_call_target="tpu_custom_call" | custom-call | flops 469762048 | bytes 2097152 | tf_op jit(solution)/shard_map/query_gradients/pallas_call | solution.py:372
  32.2 0.6 %collective-permute-done.5.refs_0_ = bf16[256,256]{1,0:T(8,128)(2,1)S(1)} collective-permute-done((bf16[256,256]{1,0:T(8,128)(2,1)S(1)}, bf16[256,256]{1,0:T(8,128)(2,1)S(1)}, u32[]{:S(2)}, u32[]{:S(2)}) %collective-permute-start.5) | collective-permute-done | bytes 131104 | tf_op jit(solution)/shard_map/ppermute | solution.py:415
  32.8 1.6 %collective-permute-done.7.refs_1_ = bf16[256,256]{1,0:T(8,128)(2,1)S(1)} collective-permute-done((bf16[256,256]{1,0:T(8,128)(2,1)S(1)}, bf16[256,256]{1,0:T(8,128)(2,1)S(1)}, u32[]{:S(2)}, u32[]{:S(2)}) %collective-permute-start.7) | collective-permute-done | bytes 131104 | tf_op jit(solution)/shard_map/ppermute | solution.py:415
  34.4 1.2 %gather.1 = (bf16[256,128]{1,0:T(8,128)(2,1)}, bf16[256,128]{1,0:T(8,128)(2,1)}) custom-call(s32[34]{0:T(128)S(1)} %pad_add_fusion.info, f32[256,256]{1,0:T(8,128)S(1)} %get-tuple-element.38.own_ref, bf16[256,256]{1,0:T(8,128)(2,1)S(1)} %collective-permute-done.5.refs_0_, bf16[256,256]{1,0:T(8,128)(2,1)S(1)} %collective-permute-done.7.refs_1_), custom_call_target="tpu_custom_call" | custom-call | tf_op jit(solution)/shard_map/gather/pallas_call | solution.py:466
  (4 shorter events, 0.1 us)
Async XLA Ops:
  0.6 14.6 %copy-start.1 = (bf16[128,2048]{1,0:T(8,128)(2,1)S(1)}, bf16[128,2048]{1,0:T(8,128)(2,1)}, u32[]{:S(2)}) copy-start(bf16[128,2048]{1,0:T(8,128)(2,1)} %refs_0_.1) | copy-start | bytes 1572868
  0.6 14.6 %copy-start = (bf16[128,2048]{1,0:T(8,128)(2,1)S(1)}, bf16[128,2048]{1,0:T(8,128)(2,1)}, u32[]{:S(2)}) copy-start(bf16[128,2048]{1,0:T(8,128)(2,1)} %refs_1_.1) | copy-start | bytes 1572868
  0.7 8.3 %copy-start.2 = (s32[32]{0:T(128)S(1)}, s32[32]{0:T(128)}, u32[]{:S(2)}) copy-start(s32[32]{0:T(128)} %param.9) | copy-start | bytes 388
  1.6 5.5 %collective-permute-start.1 = (bf16[128,256]{1,0:T(8,128)(2,1)S(1)}, bf16[128,256]{1,0:T(8,128)(2,1)S(1)}, u32[]{:S(2)}, u32[]{:S(2)}) collective-permute-start(bf16[128,256]{1,0:T(8,128)(2,1)S(1)} %pad_maximum_fusion.2), channel_id=1, source_target_pairs={{0,1},{1,0},{2,3},{3,2},{4,5},{5,4},{6,7},{7,6},{8,9},{9,8},{10,11... | collective-permute-start | bytes 196616 | tf_op jit(solution)/shard_map/ppermute | solution.py:445
  5.7 15.6 %collective-permute-start = (bf16[128,2048]{1,0:T(8,128)(2,1)S(1)}, bf16[128,2048]{1,0:T(8,128)(2,1)S(1)}, u32[]{:S(2)}, u32[]{:S(2)}) collective-permute-start(bf16[128,2048]{1,0:T(8,128)(2,1)S(1)} %pad_maximum_fusion), channel_id=1, source_target_pairs={{0,1},{1,0},{2,3},{3,2},{4,5},{5,4},{6,7},{7,6},{8,9},{9,8},{10,11... | collective-permute-start | bytes 1572872 | tf_op jit(solution)/shard_map/ppermute | solution.py:445
  7.1 8.2 %collective-permute-start.2 = (bf16[256,256]{1,0:T(8,128)(2,1)S(1)}, bf16[256,256]{1,0:T(8,128)(2,1)S(1)}, u32[]{:S(2)}, u32[]{:S(2)}) collective-permute-start(bf16[256,256]{1,0:T(8,128)(2,1)S(1)} %pad_maximum_fusion.1.refs_0_.refs_3_.refs_2_), channel_id=1, source_target_pairs={{0,4},{2,6},{4,8},{6,10},{8,12},{10,14},{12,16},{14,18},{16,20},{1... | collective-permute-start | bytes 393224 | tf_op jit(solution)/shard_map/ppermute | solution.py:415
  9.0 6.2 %collective-permute-start.3 = (bf16[256,256]{1,0:T(8,128)(2,1)S(1)}, bf16[256,256]{1,0:T(8,128)(2,1)S(1)}, u32[]{:S(2)}, u32[]{:S(2)}) collective-permute-start(bf16[256,256]{1,0:T(8,128)(2,1)S(1)} %pad_maximum_fusion.1.refs_0_.refs_3_.refs_2_), channel_id=1, source_target_pairs={{0,2},{2,8},{4,6},{6,12},{8,10},{10,16},{12,14},{14,20},{16,18},{1... | collective-permute-start | bytes 393224 | tf_op jit(solution)/shard_map/ppermute | solution.py:415
  15.2 1.9 %collective-permute-start.4 = (bf16[256,256]{1,0:T(8,128)(2,1)S(1)}, bf16[256,256]{1,0:T(8,128)(2,1)S(1)}, u32[]{:S(2)}, u32[]{:S(2)}) collective-permute-start(bf16[256,256]{1,0:T(8,128)(2,1)S(1)} %collective-permute-done.2.refs_2_.refs_5_.refs_4_), channel_id=1, source_target_pairs={{0,2},{2,0},{4,6},{6,4},{8,10},{10,8},{12,14},{14,12},{16,18},{18,... | collective-permute-start | bytes 393224 | tf_op jit(solution)/shard_map/ppermute | solution.py:415
  26.2 2.9 %collective-permute-start.6 = (bf16[256,256]{1,0:T(8,128)(2,1)S(1)}, bf16[256,256]{1,0:T(8,128)(2,1)S(1)}, u32[]{:S(2)}, u32[]{:S(2)}) collective-permute-start(bf16[256,256]{1,0:T(8,128)(2,1)S(1)} %get-tuple-element.41), channel_id=1, source_target_pairs={{2,0},{0,2},{6,4},{4,6},{10,8},{8,10},{14,12},{12,14},{18,16},{16,... | collective-permute-start | bytes 393224 | tf_op jit(solution)/shard_map/ppermute | solution.py:415
  26.8 6.1 %collective-permute-start.5 = (bf16[256,256]{1,0:T(8,128)(2,1)S(1)}, bf16[256,256]{1,0:T(8,128)(2,1)S(1)}, u32[]{:S(2)}, u32[]{:S(2)}) collective-permute-start(bf16[256,256]{1,0:T(8,128)(2,1)S(1)} %get-tuple-element.39), channel_id=1, source_target_pairs={{2,0},{8,2},{6,4},{12,6},{10,8},{16,10},{14,12},{20,14},{18,16},{2... | collective-permute-start | bytes 393224 | tf_op jit(solution)/shard_map/ppermute | solution.py:415
  29.1 5.3 %collective-permute-start.7 = (bf16[256,256]{1,0:T(8,128)(2,1)S(1)}, bf16[256,256]{1,0:T(8,128)(2,1)S(1)}, u32[]{:S(2)}, u32[]{:S(2)}) collective-permute-start(bf16[256,256]{1,0:T(8,128)(2,1)S(1)} %add_convert_fusion), channel_id=1, source_target_pairs={{4,0},{6,2},{8,4},{10,6},{12,8},{14,10},{16,12},{18,14},{20,16},{2... | collective-permute-start | bytes 393224 | tf_op jit(solution)/shard_map/ppermute | solution.py:415

commit v7 on v6

--- a/solution.py
+++ b/solution.py
@@ -20,7 +20,6 @@
 
 OWN, A, B, C = range(WIN)
 SLOTS = {1: ((OWN, 0), (B, 0), (A, 0), (C, 0)), 2: ((OWN, None), (B, 1), (B, 0), (A, 1), (A, 0), (C, 1), (C, 0))}
-EARLY = 5
 
 
 def in_vmem(*arrays):
@@ -33,6 +32,10 @@
 
 def fold(x, op):
     return op(x.reshape(x.shape[0] // 8, 8, x.shape[1]), axis=0)
+
+
+def place():
+    return lax.axis_index("ctx"), lax.axis_index("head")
 
 
 def distances(info):
@@ -55,7 +58,8 @@
     return part ^ info[1] if tiles == 2 else part
 
 
-def mask_kernel(shard, info, *bias_refs):
+def mask_kernel(shard, lengths, *bias_refs):
+    info = place()
     tiles = len(bias_refs)
     part = shard // tiles
     back = distances(info)
@@ -65,9 +69,9 @@
         query = first + lax.broadcasted_iota(jnp.int32, (1, part), 1)
         low = jnp.zeros((1, part), jnp.int32)
         start = jnp.int32(0)
-        for d in range(info.shape[0] - 2):
+        for d in range(lengths.shape[0]):
             low = jnp.where(query >= start, start, low)
-            start = start + info[2 + d]
+            start = start + lengths[d]
         for slot, (s, j) in enumerate(SLOTS[tiles]):
             at = (info[0] - back[s]) * shard + (tile if j is None else j) * part
             if tiles == 2 and j == 0 and moved(info, tile, s) is not None:
@@ -96,54 +100,13 @@
             v_ref[at, :] = x[:, hd:]
 
 
-def by_heads(info, sources, columns, rows, hd, *targets):
-    if len(sources) == 1:
-        places = [(sources[0], 0), (sources[0], columns)]
-    else:
-        mine = pl.multiple_of(info[1] * columns, 128)
-        places = [(source, mine) for source in sources]
-    for (source, start), target in zip(places, targets):
-        for h in range(columns // hd):
-            target[h * rows : (h + 1) * rows, :] = source[:, pl.ds(start + h * hd, hd)]
-
-
-def scores_of(k, q, bias):
-    s = dot(k, q, NT) + jnp.concatenate([bias] * HEADS, axis=1)
-    return s, jnp.max(fold(s, jnp.max), axis=0, keepdims=True)
-
-
-def early_kernel(info, q_ref, do_ref, bias_ref, *refs):
-    shard_refs, (e_ref, dp_ref, top_ref, sum_ref, k_ref, v_ref, q_rows, do_rows) = refs[:3], refs[3:]
-    rows = bias_ref.shape[1]
-    hd = k_ref.shape[1]
-    early = e_ref.shape[0]
-    n = HEADS * rows
-    log2e = math.log2(math.e) / math.sqrt(hd)
-    fill(info, 2, tile_of(info, 2, 0), shard_refs, range(EARLY), k_ref, v_ref)
-    by_heads(info, (q_ref, do_ref), q_ref.shape[1] // 2, rows, hd, q_rows, do_rows)
-    pairs = q_rows.shape[0] // n
-    sc = scores_of(k_ref[...], q_rows[:n, :], bias_ref[:early, :])
-    for p in range(pairs):
-        at = slice(p * n, (p + 1) * n)
-        s, top = sc
-        if p + 1 < pairs:
-            sc = scores_of(k_ref[...], q_rows[(p + 1) * n : (p + 2) * n, :], bias_ref[:early, :])
-        dp_ref[:, at] = dot(v_ref[...], do_rows[at, :], NT)
-        e = jnp.exp2((s - top) * log2e)
-        e_ref[:, at] = e
-        top_ref[:, at] = top
-        sum_ref[:, at] = jnp.sum(fold(e, jnp.sum), axis=0, keepdims=True)
-
-
-def attend_kernel(tiles, index, info, *refs):
+def attend_kernel(tiles, index, *refs):
+    info = place()
     last = index == tiles - 1
-    ahead = not last
-    sources, refs = (refs[:2], refs[2:]) if ahead else (refs[:1], refs[1:])
+    sources, refs = (refs[:1], refs[1:]) if last else (refs[:2], refs[2:])
     bias_ref, *refs = refs
     shard_refs, refs = refs[:WIN], refs[WIN:]
     acc_refs = []
-    if ahead:
-        (e_early, dp_early, top_early, sum_early), refs = refs[:4], refs[4:]
     if index:
         acc_refs, refs = [refs[0]], refs[2:]
     out_hbm, ds_ref, *refs = refs
@@ -152,7 +115,7 @@
         acc_refs.append(refs[0])
     else:
         acc_refs.append(refs[0])
-    acc_ref, k_ref, v_ref, vt_ref, q_rows, do_rows, p_ref, out_ref, sem = refs
+    acc_ref, k_ref, v_ref, vt_ref, p_ref, out_ref, sem = refs
 
     shard, width = shard_refs[0].shape
     hd = width // 2
@@ -162,61 +125,57 @@
     part = shard // tiles
     tile = tile_of(info, tiles, index)
     n = HEADS * rows
-    early = EARLY * part if ahead else 0
     log2e = math.log2(math.e) / math.sqrt(hd)
     scaling = 1 / math.sqrt(hd)
     fill(info, tiles, tile, shard_refs, range(len(SLOTS[tiles])), k_ref, v_ref)
-    by_heads(info, sources, columns, rows, hd, q_rows, do_rows)
     vt_ref[...] = v_ref[...].T
 
     def at(p):
         return slice(p * n, (p + 1) * n)
 
+    if last:
+        q_do = [(sources[0], 0), (sources[0], columns)]
+    else:
+        q_do = [(source, pl.multiple_of(info[1] * columns, 128)) for source in sources]
+
+    def rows_of(p):
+        heads = range(p * HEADS, (p + 1) * HEADS)
+        return [jnp.concatenate([x[:, pl.ds(start + h * hd, hd)] for h in heads], axis=0) for x, start in q_do]
+
     def scores(p):
-        return scores_of(k_ref[early:, :], q_rows[at(p), :], bias_ref[early:, :])
+        s = dot(k_ref[...], rows_of(p)[0], NT) + jnp.concatenate([bias_ref[...]] * HEADS, axis=1)
+        return s, jnp.max(fold(s, jnp.max), axis=0, keepdims=True)
 
     def weights(p, s, top):
-        if ahead:
-            before = top_early[:, at(p)]
-            top = jnp.maximum(top, before)
-            rescale = jnp.exp2((before - top) * log2e)
         e = jnp.exp2((s - top) * log2e)
         total = jnp.sum(fold(e, jnp.sum), axis=0, keepdims=True)
-        if ahead:
-            total = total + sum_early[:, at(p)] * rescale
-        inverse = 1.0 / total
-        p_f32 = e * inverse
-        p_ref[early:, at(p)] = p_f32.astype(BF16)
-        if ahead:
-            first = e_early[:, at(p)] * (rescale * inverse)
-            p_ref[:early, at(p)] = first.astype(BF16)
-            return first, p_f32
-        return (p_f32,)
+        p_f32 = e * (1.0 / total)
+        p_ref[:, at(p)] = p_f32.astype(BF16)
+        return p_f32
 
     def outputs(p):
         out = dot(vt_ref[...], p_ref[:, at(p)], NN).astype(BF16)
-        do_t = do_rows[at(p), :].T.astype(F32)
+        do_t = rows_of(p)[1].T.astype(F32)
         delta = jnp.sum(do_t * out.astype(F32), axis=0, keepdims=True)
         for i in range(HEADS):
             h = p * HEADS + i
             out_ref[:, h * hd : (h + 1) * hd] = out[:, i * rows : (i + 1) * rows].T
         here = slice(p * HEADS * hd, (p + 1) * HEADS * hd)
-        place = pl.ds(pl.multiple_of(tile * rows, rows), rows)
-        copy = pltpu.make_async_copy(out_ref.at[:, here], out_hbm.at[place, here], sem.at[p])
+        there = pl.ds(pl.multiple_of(tile * rows, rows), rows)
+        copy = pltpu.make_async_copy(out_ref.at[:, here], out_hbm.at[there, here], sem.at[p])
         copy.start()
         stores.append(copy)
         return delta
 
     def dprobs(p):
-        return dot(v_ref[early:, :], do_rows[at(p), :], NT)
+        return dot(v_ref[...], rows_of(p)[1], NT)
 
     def dscores(p, w, dp, delta):
-        if ahead:
-            ds_ref[:early, at(p)] = (w[0] * (dp_early[:, at(p)] - delta)).astype(BF16)
-        ds_ref[early:, at(p)] = (w[-1] * (dp - delta)).astype(BF16)
+        ds_ref[:, at(p)] = (w * (dp - delta)).astype(BF16)
 
     def sums(p):
-        dk, dv = dot(ds_ref[:, at(p)], q_rows[at(p), :], NN), dot(p_ref[:, at(p)], do_rows[at(p), :], NN)
+        q, do = rows_of(p)
+        dk, dv = dot(ds_ref[:, at(p)], q, NN), dot(p_ref[:, at(p)], do, NN)
         if p:
             acc_ref[:, :hd] += dk
             acc_ref[:, hd:] += dv
@@ -257,7 +216,8 @@
         copy.wait()
 
 
-def queries_kernel(tiles, info, *refs):
+def queries_kernel(tiles, *refs):
+    info = place()
     shard_refs, refs = refs[:WIN], refs[WIN:]
     ds_refs, (dq_hbm, k_ref, kt_ref, dq_ref, sem) = refs[:tiles], refs[tiles:]
     hd, keys = kt_ref.shape
@@ -275,9 +235,9 @@
                 here = slice(p * width + i * hd, p * width + (i + 1) * hd)
                 dq_ref[index * rows : (index + 1) * rows, here] = dq[:, i * rows : (i + 1) * rows].T
             here = slice(p * width, (p + 1) * width)
-            place = pl.ds(pl.multiple_of(tile * rows, rows), rows)
+            there = pl.ds(pl.multiple_of(tile * rows, rows), rows)
             source = dq_ref.at[index * rows : (index + 1) * rows, here]
-            copy = pltpu.make_async_copy(source, dq_hbm.at[place, here], sem.at[len(stores)])
+            copy = pltpu.make_async_copy(source, dq_hbm.at[there, here], sem.at[len(stores)])
             copy.start()
             stores.append(copy)
     for copy in stores:
@@ -288,7 +248,7 @@
     return pltpu.CompilerParams(vmem_limit_bytes=mib << 20)
 
 
-def masks(info, shard, tiles):
+def masks(doc_lengths, shard, tiles):
     part = shard // tiles
     return pl.pallas_call(
         functools.partial(mask_kernel, shard),
@@ -297,30 +257,10 @@
         out_specs=[WHOLE] * tiles,
         compiler_params=params(4),
         name="masks",
-    )(info)
-
-
-def early(info, queries, d_out, bias, shards, columns):
-    shard, width = shards[0].shape
-    part, hd = shard // 2, width // 2
-    all_rows = columns // hd * part
-    keys = EARLY * part
-    row = pltpu.VMEM((1, all_rows), F32)
-    return pl.pallas_call(
-        early_kernel,
-        out_shape=[pltpu.VMEM((keys, all_rows), F32)] * 2 + [row, row],
-        in_specs=[SCALARS] + [WHOLE] * 6,
-        out_specs=[WHOLE] * 4,
-        scratch_shapes=[pltpu.VMEM((keys, hd), BF16)] * 2 + [pltpu.VMEM((all_rows, hd), BF16)] * 2,
-        compiler_params=params(16),
-        cost_estimate=pl.CostEstimate(
-            flops=4 * keys * all_rows * hd, transcendentals=keys * all_rows, bytes_accessed=1 << 21
-        ),
-        name="early",
-    )(info, *in_vmem(queries, d_out, bias, *shards))
-
-
-def attend(info, q_do, bias, shards, prepared, before, tiles, columns):
+    )(doc_lengths)
+
+
+def attend(q_do, bias, shards, before, tiles, columns):
     shard, width = shards[0].shape
     hd = width // 2
     index = 0 if before is None else 1
@@ -328,8 +268,8 @@
     keys, rows = bias.shape
     all_rows = columns // hd * rows
     acc = pltpu.VMEM((keys, width), F32)
-    args = [info, *in_vmem(*q_do, bias, *shards, *prepared)]
-    in_specs = [SCALARS] + [WHOLE] * (len(args) - 1)
+    args = in_vmem(*q_do, bias, *shards)
+    in_specs = [WHOLE] * len(args)
     aliases = {}
     if before is not None:
         aliases = {len(args) + 1: 0}
@@ -350,8 +290,6 @@
             pltpu.VMEM((keys, hd), BF16),
             pltpu.VMEM((keys, hd), BF16),
             pltpu.VMEM((hd, keys), BF16),
-            pltpu.VMEM((all_rows, hd), BF16),
-            pltpu.VMEM((all_rows, hd), BF16),
             pltpu.VMEM((keys, all_rows), BF16),
             pltpu.VMEM((rows, columns), BF16),
             pltpu.SemaphoreType.DMA((columns // hd // HEADS,)),
@@ -365,14 +303,14 @@
     )(*args)
 
 
-def query_gradients(info, shards, dscores, columns):
+def query_gradients(shards, dscores, columns):
     shard, width = shards[0].shape
     tiles = len(dscores)
     hd, keys = width // 2, dscores[0].shape[0]
     return pl.pallas_call(
         functools.partial(queries_kernel, tiles),
         out_shape=jax.ShapeDtypeStruct((shard, columns), BF16),
-        in_specs=[SCALARS] + [WHOLE] * (WIN + tiles),
+        in_specs=[WHOLE] * (WIN + tiles),
         out_specs=ANY,
         scratch_shapes=[
             pltpu.VMEM((keys, hd), BF16),
@@ -383,7 +321,7 @@
         compiler_params=params(12),
         cost_estimate=pl.CostEstimate(flops=2 * keys * shard * columns, transcendentals=0, bytes_accessed=1 << 21),
         name="query_gradients",
-    )(info, *in_vmem(*shards, *dscores))
+    )(*in_vmem(*shards, *dscores))
 
 
 def gather_kernel(own_ref, *refs):
@@ -395,7 +333,8 @@
     refs[-1][...] = total[:, hd:].astype(BF16)
 
 
-def in_order_kernel(info, own_ref, *refs):
+def in_order_kernel(own_ref, *refs):
+    info = place()
     near, (k_ref, v_ref) = refs[:-2], refs[-2:]
     shard, hd = k_ref.shape
     part = shard // 2
@@ -428,9 +367,8 @@
     shard = count * queries.shape[0]
     hd = keys.shape[1] // count
     columns = queries.shape[1] // count
-    info = jnp.concatenate([jnp.stack([lax.axis_index("ctx"), head]).astype(jnp.int32), doc_lengths])
     tiles = 2 if count == 2 else 1
-    bias = masks(info, shard, tiles)
+    bias = masks(doc_lengths, shard, tiles)
     if tiles == 2:
         other = 1 - head
 
@@ -447,30 +385,28 @@
         own = jnp.concatenate([key_value(head), swap(key_value(other))], axis=0)
         both = swap(jnp.concatenate([half(queries, other), half(d_out, other)], axis=1))
         shards, bias = window(own, bias)
-        prepared = early(info, queries, d_out, bias[0], shards[:C], columns)
-        out, ds_first, acc = attend(info, (queries, d_out), bias[0], shards, prepared, None, 2, columns)
-        out, ds_last, *grads = attend(info, (both,), bias[1], shards, (), (acc, out), 2, columns)
+        out, ds_first, acc = attend((queries, d_out), bias[0], shards, None, 2, columns)
+        out, ds_last, *grads = attend((both,), bias[1], shards, (acc, out), 2, columns)
         dscores = (ds_first, ds_last)
     else:
         swap = lambda x: lax.all_to_all(x, "head", split_axis=1, concat_axis=0, tiled=True)
         own = jnp.concatenate([swap(keys), swap(values)], axis=1)
         both = jnp.concatenate([swap(queries), swap(d_out)], axis=1)
         shards, bias = window(own, bias)
-        out, ds_last, *grads = attend(info, (both,), bias[0], shards, (), None, 1, columns)
+        out, ds_last, *grads = attend((both,), bias[0], shards, None, 1, columns)
         dscores = (ds_last,)
     from_c = move(grads[C], C, True)
     near_a = move(grads[A], A, True)
     near_b = move((grads[B] + from_c.astype(F32)).astype(BF16), B, True)
-    dq = query_gradients(info, shards, dscores, columns)
-    ordered = [info] if tiles == 2 else []
+    dq = query_gradients(shards, dscores, columns)
     grad_keys, grad_values = pl.pallas_call(
         in_order_kernel if tiles == 2 else gather_kernel,
         out_shape=[jax.ShapeDtypeStruct((shard, hd), BF16)] * 2,
-        in_specs=[SCALARS] * len(ordered) + [WHOLE] * 3,
+        in_specs=[WHOLE] * 3,
         out_specs=[WHOLE] * 2,
         compiler_params=params(4),
         name="gather",
-    )(*ordered, *in_vmem(grads[OWN], near_a, near_b))
+    )(*in_vmem(grads[OWN], near_a, near_b))
     return out, dq, grad_keys, grad_values
 
 

time: 35.8 us -> 34.1 us (0.953)
  Pallas kernels: 15 us -> 11.3 us
  waiting for transfers between devices: 8.82 us -> 10 us
  starting transfers between devices: 8.91 us -> 9.78 us
    pallas_call x1 -> x0, Pallas kernels: 1.87 us -> none  [early(): pl.pallas_call(early_kernel, out_shape=[pltpu.VMEM((keys, all_rows), F32)...]
    ppermute x6, waiting for transfers between devices: 7.6 us -> 8.78 us  [move(): lax.ppermute(value, 'ctx', [p[::-1] for p in pairs] if back else pairs)]
    ppermute x6, starting transfers between devices: 5.79 us -> 6.66 us  [move(): lax.ppermute(value, 'ctx', [p[::-1] for p in pairs] if back else pairs)]
    pallas_call x2, Pallas kernels: 9.03 us -> 8.35 us  [attend(): pl.pallas_call(functools.partial(attend_kernel, tiles, index), out_shape=...]
    pallas_call x1, Pallas kernels: 2.13 us -> 1.57 us  [query_gradients(): pl.pallas_call(functools.partial(queries_kernel, tiles), out_shape=jax.Sh...]
    pallas_call x1, Pallas kernels: 1.23 us -> 0.68 us  [body(): pl.pallas_call(in_order_kernel if tiles == 2 else gather_kernel, out_shap...]
  transfers between devices with their start and end apart: 8 -> 8, of which waited for: 4 -> 6; matrix products, arithmetic and copies ran while one was open for 3% -> 3% of each run, Pallas kernels for 25% -> 19%
where the time goes in v7:
time: 34.1 us; the launch traced here: 33.9 us
  Pallas kernels  11.3 us (33%)
  waiting for transfers between devices  10 us (29%)
  starting transfers between devices  9.78 us (29%)
  local copies, waits for them, and re-layouts  1.98 us (6%)
  between operations  0.75 us (2%)
    ppermute x6, waiting for transfers between devices, move(): lax.ppermute(value, 'ctx', [p[::-1] for p in pairs] if back else pairs)  8.78 us
    pallas_call x2, Pallas kernels, attend(): pl.pallas_call(functools.partial(attend_kernel, tiles, index), out_shape=...  8.35 us
    ppermute x6, starting transfers between devices, move(): lax.ppermute(value, 'ctx', [p[::-1] for p in pairs] if back else pairs)  6.66 us
    ppermute x2, starting transfers between devices, swap(): return lax.ppermute(x, 'head', [(0, 1), (1, 0)])  3.12 us
    dynamic_slice x2, local copies, waits for them, and re-layouts, half(): return lax.dynamic_slice_in_dim(x, index * width, width, 1)  1.97 us
    pallas_call x1, Pallas kernels, query_gradients(): pl.pallas_call(functools.partial(queries_kernel, tiles), out_shape=jax.Sh...  1.57 us
    ppermute x2, waiting for transfers between devices, swap(): return lax.ppermute(x, 'head', [(0, 1), (1, 0)])  1.22 us
    pallas_call x1, Pallas kernels, masks(): pl.pallas_call(functools.partial(mask_kernel, shard), out_shape=[pltpu.VM...  0.73 us
  transfers between devices with their start and end apart: 8, of which 6 were waited for; matrix products, arithmetic and copies ran while one was open for 3% of the time, Pallas kernels for 19%

profile of v7, /device:TPU:0, one launch (start us, length us, event | category | flops | bytes accessed | tf_op | source)
XLA Modules:
  0.0 33.9 jit_solution(13099971074575782659)
XLA Ops:
  0.6 0.0 copy-start
  0.6 0.0 copy-start.1
  0.7 0.0 copy-start.2
  0.7 0.9 %constant_dynamic-slice_fusion.2 = (bf16[128,128]{1,0:T(8,128)(2,1)S(1)}, bf16[128,128]{1,0:T(8,128)(2,1)S(1)}, bf16[128,128]{1,0:T(8,128)(2,1)S(1)}, bf16[128,128]{1,0:T(8,128)(2,1)S(1)}) fusion(bf16[128,256]{1,0:T(8,128)(2,1)} %param.7, s32[]{:T(128)S(6)} %select_n.13, s32[]{:T(128)S(6)} %select_n.14, bf16[128,256]{1,0:T(8,128)(2,1)} %param.6), kind=kLoop, calls=%fused_computation.6 | loop fusion | bytes 262152 | tf_op jit(solution)/shard_map/dynamic_slice | solution.py:377
  1.6 3.0 %collective-permute-start.1 = (bf16[128,256]{1,0:T(8,128)(2,1)S(1)}, bf16[128,256]{1,0:T(8,128)(2,1)S(1)}, u32[]{:S(2)}, u32[]{:S(2)}) collective-permute-start(bf16[128,256]{1,0:T(8,128)(2,1)S(1)} %pad_maximum_fusion.2), channel_id=1, source_target_pairs={{0,1},{1,0},{2,3},{3,2},{4,5},{5,4},{6,7},{7,6},{8,9},{9,8},{10,11... | collective-permute-start | bytes 196616 | tf_op jit(solution)/shard_map/ppermute | solution.py:383
  4.6 1.1 %constant_dynamic-slice_fusion.4 = (bf16[128,1024]{1,0:T(8,128)(2,1)S(1)}, bf16[128,1024]{1,0:T(8,128)(2,1)S(1)}) fusion(bf16[128,2048]{1,0:T(8,128)(2,1)} %refs_1_.1, s32[]{:T(128)S(6)} %select_n.12, bf16[128,2048]{1,0:T(8,128)(2,1)} %refs_0_.1), kind=kLoop, calls=%fused_computation.8 | loop fusion | bytes 1048580 | tf_op jit(solution)/shard_map/dynamic_slice | solution.py:377
  5.7 0.1 collective-permute-start
  5.8 1.2 %collective-permute-done.1 = bf16[128,256]{1,0:T(8,128)(2,1)S(1)} collective-permute-done((bf16[128,256]{1,0:T(8,128)(2,1)S(1)}, bf16[128,256]{1,0:T(8,128)(2,1)S(1)}, u32[]{:S(2)}, u32[]{:S(2)}) %collective-permute-start.1) | collective-permute-done | bytes 65568 | tf_op jit(solution)/shard_map/ppermute | solution.py:383
  7.1 1.9 %collective-permute-start.2 = (bf16[256,256]{1,0:T(8,128)(2,1)S(1)}, bf16[256,256]{1,0:T(8,128)(2,1)S(1)}, u32[]{:S(2)}, u32[]{:S(2)}) collective-permute-start(bf16[256,256]{1,0:T(8,128)(2,1)S(1)} %pad_maximum_fusion.1.refs_3_.refs_2_.refs_0_), channel_id=1, source_target_pairs={{0,4},{2,6},{4,8},{6,10},{8,12},{10,14},{12,16},{14,18},{16,20},{1... | collective-permute-start | bytes 393224 | tf_op jit(solution)/shard_map/ppermute | solution.py:354
  9.0 0.0 copy-done.2
  9.0 0.7 %masks.1 = (f32[896,128]{1,0:T(8,128)S(1)}, f32[896,128]{1,0:T(8,128)S(1)}) custom-call(s32[32]{0:T(128)S(1)} %copy-done.2), custom_call_target="tpu_custom_call" | custom-call | tf_op jit(solution)/shard_map/masks/pallas_call | solution.py:253
  9.7 0.1 collective-permute-start.3
  9.8 5.2 %collective-permute-done.2.refs_5_.refs_4_.refs_2_ = bf16[256,256]{1,0:T(8,128)(2,1)S(1)} collective-permute-done((bf16[256,256]{1,0:T(8,128)(2,1)S(1)}, bf16[256,256]{1,0:T(8,128)(2,1)S(1)}, u32[]{:S(2)}, u32[]{:S(2)}) %collective-permute-start.2) | collective-permute-done | bytes 131104 | tf_op jit(solution)/shard_map/ppermute | solution.py:354
  15.0 0.0 collective-permute-start.4
  15.0 1.0 %collective-permute-done.3.refs_4_.refs_3_.refs_1_ = bf16[256,256]{1,0:T(8,128)(2,1)S(1)} collective-permute-done((bf16[256,256]{1,0:T(8,128)(2,1)S(1)}, bf16[256,256]{1,0:T(8,128)(2,1)S(1)}, u32[]{:S(2)}, u32[]{:S(2)}) %collective-permute-start.3) | collective-permute-done | bytes 131104 | tf_op jit(solution)/shard_map/ppermute | solution.py:354
  16.0 0.3 %collective-permute-done.4.refs_6_.refs_5_.refs_3_ = bf16[256,256]{1,0:T(8,128)(2,1)S(1)} collective-permute-done((bf16[256,256]{1,0:T(8,128)(2,1)S(1)}, bf16[256,256]{1,0:T(8,128)(2,1)S(1)}, u32[]{:S(2)}, u32[]{:S(2)}) %collective-permute-start.4) | collective-permute-done | bytes 131104 | tf_op jit(solution)/shard_map/ppermute | solution.py:354
  16.3 0.0 copy-done
  16.3 0.0 copy-done.1
  16.3 4.2 %attend_first.1 = (bf16[256,1024]{1,0:T(8,128)(2,1)}, bf16[896,1024]{1,0:T(8,128)(2,1)S(1)}, f32[896,256]{1,0:T(8,128)S(1)}) custom-call(bf16[128,2048]{1,0:T(8,128)(2,1)S(1)} %copy-done.1, bf16[128,2048]{1,0:T(8,128)(2,1)S(1)} %copy-done, f32[896,128]{1,0:T(8,128)S(1)} %get-tuple-element.24.refs_2_, ...), custom_call_target="tpu_custom_call" | custom-call | flops 1174405120 | bytes 2097152 | tf_op jit(solution)/shard_map/attend_first/pallas_call | solution.py:283
  20.5 0.0 collective-permute-done.refs_0_
  20.5 4.2 %attend_last.1 = (bf16[256,1024]{1,0:T(8,128)(2,1)}, bf16[896,1024]{1,0:T(8,128)(2,1)S(1)}, f32[256,256]{1,0:T(8,128)S(1)}, bf16[256,256]{1,0:T(8,128)(2,1)S(1)}...) custom-call(bf16[128,2048]{1,0:T(8,128)(2,1)S(1)} %collective-permute-done.refs_0_, ...), custom_call_target="tpu_custom_call", output_to_operand_aliasing={{0}: (7, {})} | custom-call | flops 1174405120 | bytes 2097152 | tf_op jit(solution)/shard_map/attend_last/pallas_call | solution.py:283
  24.7 0.2 collective-permute-start.6
  24.9 3.0 %collective-permute-start.5 = (bf16[256,256]{1,0:T(8,128)(2,1)S(1)}, bf16[256,256]{1,0:T(8,128)(2,1)S(1)}, u32[]{:S(2)}, u32[]{:S(2)}) collective-permute-start(bf16[256,256]{1,0:T(8,128)(2,1)S(1)} %get-tuple-element.31), channel_id=1, source_target_pairs={{2,0},{8,2},{6,4},{12,6},{10,8},{16,10},{14,12},{20,14},{18,16},{2... | collective-permute-start | bytes 393224 | tf_op jit(solution)/shard_map/ppermute | solution.py:354
  28.0 0.0 collective-permute-done.6
  28.0 1.4 %collective-permute-start.7 = (bf16[256,256]{1,0:T(8,128)(2,1)S(1)}, bf16[256,256]{1,0:T(8,128)(2,1)S(1)}, u32[]{:S(2)}, u32[]{:S(2)}) collective-permute-start(bf16[256,256]{1,0:T(8,128)(2,1)S(1)} %add_convert_fusion), channel_id=1, source_target_pairs={{4,0},{6,2},{8,4},{10,6},{12,8},{14,10},{16,12},{18,14},{20,16},{2... | collective-permute-start | bytes 393224 | tf_op jit(solution)/shard_map/ppermute | solution.py:354
  29.4 1.6 %query_gradients.1 = bf16[256,1024]{1,0:T(8,128)(2,1)} custom-call(bf16[256,256]{1,0:T(8,128)(2,1)S(1)} %pad_maximum_fusion.1.refs_3_.refs_2_.refs_0_, bf16[256,256]{1,0:T(8,128)(2,1)S(1)} %collective-permute-done.3.refs_4_.refs_3_.refs_1_, bf16[256,256]{1,0:T(8,128)(2,1)S(1)} %collective-permute-done.2.refs_5_.refs_4_.refs_2_, ...), custom_call_target="tpu_custom_call" | custom-call | flops 469762048 | bytes 2097152 | tf_op jit(solution)/shard_map/query_gradients/pallas_call | solution.py:310
  31.0 0.2 collective-permute-done.5.refs_0_
  31.2 2.0 %collective-permute-done.7.refs_1_ = bf16[256,256]{1,0:T(8,128)(2,1)S(1)} collective-permute-done((bf16[256,256]{1,0:T(8,128)(2,1)S(1)}, bf16[256,256]{1,0:T(8,128)(2,1)S(1)}, u32[]{:S(2)}, u32[]{:S(2)}) %collective-permute-start.7) | collective-permute-done | bytes 131104 | tf_op jit(solution)/shard_map/ppermute | solution.py:354
  33.3 0.7 %gather.1 = (bf16[256,128]{1,0:T(8,128)(2,1)}, bf16[256,128]{1,0:T(8,128)(2,1)}) custom-call(f32[256,256]{1,0:T(8,128)S(1)} %get-tuple-element.30.own_ref, bf16[256,256]{1,0:T(8,128)(2,1)S(1)} %collective-permute-done.5.refs_0_, bf16[256,256]{1,0:T(8,128)(2,1)S(1)} %collective-permute-done.7.refs_1_), custom_call_target="tpu_custom_call" | custom-call | tf_op jit(solution)/shard_map/gather/pallas_call | solution.py:402
  (4 shorter events, 0.1 us)
Async XLA Ops:
  0.6 15.7 %copy-start = (bf16[128,2048]{1,0:T(8,128)(2,1)S(1)}, bf16[128,2048]{1,0:T(8,128)(2,1)}, u32[]{:S(2)}) copy-start(bf16[128,2048]{1,0:T(8,128)(2,1)} %refs_1_.1) | copy-start | bytes 1572868
  0.6 15.7 %copy-start.1 = (bf16[128,2048]{1,0:T(8,128)(2,1)S(1)}, bf16[128,2048]{1,0:T(8,128)(2,1)}, u32[]{:S(2)}) copy-start(bf16[128,2048]{1,0:T(8,128)(2,1)} %refs_0_.1) | copy-start | bytes 1572868
  0.7 8.3 %copy-start.2 = (s32[32]{0:T(128)S(1)}, s32[32]{0:T(128)}, u32[]{:S(2)}) copy-start(s32[32]{0:T(128)} %lengths.1) | copy-start | bytes 388
  1.6 5.5 %collective-permute-start.1 = (bf16[128,256]{1,0:T(8,128)(2,1)S(1)}, bf16[128,256]{1,0:T(8,128)(2,1)S(1)}, u32[]{:S(2)}, u32[]{:S(2)}) collective-permute-start(bf16[128,256]{1,0:T(8,128)(2,1)S(1)} %pad_maximum_fusion.2), channel_id=1, source_target_pairs={{0,1},{1,0},{2,3},{3,2},{4,5},{5,4},{6,7},{7,6},{8,9},{9,8},{10,11... | collective-permute-start | bytes 196616 | tf_op jit(solution)/shard_map/ppermute | solution.py:383
  5.7 14.8 %collective-permute-start = (bf16[128,2048]{1,0:T(8,128)(2,1)S(1)}, bf16[128,2048]{1,0:T(8,128)(2,1)S(1)}, u32[]{:S(2)}, u32[]{:S(2)}) collective-permute-start(bf16[128,2048]{1,0:T(8,128)(2,1)S(1)} %pad_maximum_fusion), channel_id=1, source_target_pairs={{0,1},{1,0},{2,3},{3,2},{4,5},{5,4},{6,7},{7,6},{8,9},{9,8},{10,11... | collective-permute-start | bytes 1572872 | tf_op jit(solution)/shard_map/ppermute | solution.py:383
  7.1 7.9 %collective-permute-start.2 = (bf16[256,256]{1,0:T(8,128)(2,1)S(1)}, bf16[256,256]{1,0:T(8,128)(2,1)S(1)}, u32[]{:S(2)}, u32[]{:S(2)}) collective-permute-start(bf16[256,256]{1,0:T(8,128)(2,1)S(1)} %pad_maximum_fusion.1.refs_3_.refs_2_.refs_0_), channel_id=1, source_target_pairs={{0,4},{2,6},{4,8},{6,10},{8,12},{10,14},{12,16},{14,18},{16,20},{1... | collective-permute-start | bytes 393224 | tf_op jit(solution)/shard_map/ppermute | solution.py:354
  9.7 6.2 %collective-permute-start.3 = (bf16[256,256]{1,0:T(8,128)(2,1)S(1)}, bf16[256,256]{1,0:T(8,128)(2,1)S(1)}, u32[]{:S(2)}, u32[]{:S(2)}) collective-permute-start(bf16[256,256]{1,0:T(8,128)(2,1)S(1)} %pad_maximum_fusion.1.refs_3_.refs_2_.refs_0_), channel_id=1, source_target_pairs={{0,2},{2,8},{4,6},{6,12},{8,10},{10,16},{12,14},{14,20},{16,18},{1... | collective-permute-start | bytes 393224 | tf_op jit(solution)/shard_map/ppermute | solution.py:354
  15.0 1.3 %collective-permute-start.4 = (bf16[256,256]{1,0:T(8,128)(2,1)S(1)}, bf16[256,256]{1,0:T(8,128)(2,1)S(1)}, u32[]{:S(2)}, u32[]{:S(2)}) collective-permute-start(bf16[256,256]{1,0:T(8,128)(2,1)S(1)} %collective-permute-done.2.refs_5_.refs_4_.refs_2_), channel_id=1, source_target_pairs={{0,2},{2,0},{4,6},{6,4},{8,10},{10,8},{12,14},{14,12},{16,18},{18,... | collective-permute-start | bytes 393224 | tf_op jit(solution)/shard_map/ppermute | solution.py:354
  24.7 3.2 %collective-permute-start.6 = (bf16[256,256]{1,0:T(8,128)(2,1)S(1)}, bf16[256,256]{1,0:T(8,128)(2,1)S(1)}, u32[]{:S(2)}, u32[]{:S(2)}) collective-permute-start(bf16[256,256]{1,0:T(8,128)(2,1)S(1)} %get-tuple-element.33), channel_id=1, source_target_pairs={{2,0},{0,2},{6,4},{4,6},{10,8},{8,10},{14,12},{12,14},{18,16},{16,... | collective-permute-start | bytes 393224 | tf_op jit(solution)/shard_map/ppermute | solution.py:354
  24.9 6.3 %collective-permute-start.5 = (bf16[256,256]{1,0:T(8,128)(2,1)S(1)}, bf16[256,256]{1,0:T(8,128)(2,1)S(1)}, u32[]{:S(2)}, u32[]{:S(2)}) collective-permute-start(bf16[256,256]{1,0:T(8,128)(2,1)S(1)} %get-tuple-element.31), channel_id=1, source_target_pairs={{2,0},{8,2},{6,4},{12,6},{10,8},{16,10},{14,12},{20,14},{18,16},{2... | collective-permute-start | bytes 393224 | tf_op jit(solution)/shard_map/ppermute | solution.py:354
  28.0 5.3 %collective-permute-start.7 = (bf16[256,256]{1,0:T(8,128)(2,1)S(1)}, bf16[256,256]{1,0:T(8,128)(2,1)S(1)}, u32[]{:S(2)}, u32[]{:S(2)}) collective-permute-start(bf16[256,256]{1,0:T(8,128)(2,1)S(1)} %add_convert_fusion), channel_id=1, source_target_pairs={{4,0},{6,2},{8,4},{10,6},{12,8},{14,10},{16,12},{18,14},{20,16},{2... | collective-permute-start | bytes 393224 | tf_op jit(solution)/shard_map/ppermute | solution.py:354
